TPU v7x, 256 devices: a whole 4x4x8 slice. The times are simulated.
256 devices in a mesh: patch: 64 (over y, x, z_hi), head: 4 (over z_lo, core).
Axes of the slice: x: 4, y: 4, z: 8 (z_hi: 4, z_lo: 2; z = z_hi * 2 + z_lo), core: 2. Of those that a mesh axis runs over, the one named last changes fastest.
Arguments:
- fresh_qkv: bfloat16 [32768, 3, 3072], P('patch', None, 'head'), may hold values from -12 to 12
- kv_cache: bfloat16 [32768, 2, 3072], P('patch', None, 'head'), may hold values from -8 to 8
- hidden: bfloat16 [32768, 3072], P('patch'), may hold values from -6 to 6
- refresh: int32 [4], replicated, may hold values from 0 to 63, as said below
- out_weight: bfloat16 [3072, 3072], P('head'), may hold values from -0.109375 to 0.109375
- final_weight: bfloat16 [3072, 64], replicated, may hold values from -0.109375 to 0.109375
- final_bias: float32 [64], replicated, may hold values from -3 to 3
- gate_scale: float32 [3072], replicated, may hold values from 0.1 to 1.9
- noise_level: float32 [1], replicated, may hold values from 0.15 to 0.35
- noisy_latent: bfloat16 [128, 16, 1024], P('patch'), may hold values from -6 to 6
- velocity_cache: bfloat16 [128, 16, 1024], P('patch'), may hold values from -6 to 6
- conv_weight: bfloat16 [512, 3, 3, 16], P('head'), may hold values from -0.5 to 0.5
- conv_bias: float32 [512], P('head'), may hold values from -3 to 3
Outputs:
- decoded: bfloat16 [128, 512, 1024], P('patch', 'head')
Inputs may be any that keep to these rules, and one draw needn't show every extreme that they name: 4 distinct patch indices; refresh[1] is 63.
All inputs are finite; a program needn't handle non-finite values.
Results may differ from a plain program's by a relative error of at most 0.0044.
The roundings to bfloat16 on the way count: a program that leaves them out, or rounds other values in their place, can miss the bound.
Values may be sent and summed in bfloat16 or wider, within the bound.
No kernel may reach another device: no remote copies, remote signals or barrier semaphores. Data moves between devices by JAX's collectives and lax.ppermute only.
A program may use at most 128 MiB of HBM per device.

v0:
```python
import functools
import math

import jax
import jax.numpy as jnp
from jax import lax
from jax.experimental import pallas as pl
from jax.experimental.pallas import tpu as pltpu
from jax.sharding import Mesh
from jax.sharding import PartitionSpec as P

HEAD_DIM = 128
LAT_CH = 16
PATCHES = 64
SLOTS = 4
HEADS_HERE = 6
HALF = 3
VEC = 64
ROWS = HALF * VEC
PACK = ROWS + 16
KEYS = 512
COLS = 1024
CHUNK = 8
F32 = jnp.float32
BF16 = jnp.bfloat16
PATCH = ("y", "x", "z")
HEAD = ("w", "c")
BITS = {"y": 4, "x": 2, "z": 0}


def shift(value, axis, step):
    if step == 0:
        return value
    return lax.ppermute(value, axis, [(i, (i + step) % 4) for i in range(4)])


def spread_out(value):
    return jnp.broadcast_to(value[None], (4,) + value.shape)


def exchange(value, axis):
    return lax.all_to_all(value, axis, 0, 0)


def cost(flops, moved_bytes, exps=0):
    return pl.CostEstimate(flops=flops, bytes_accessed=moved_bytes, transcendentals=exps)


SMEM = pl.BlockSpec(memory_space=pltpu.SMEM)
VMEM = pl.BlockSpec(memory_space=pltpu.VMEM)


def split(value):
    high = value.astype(BF16)
    return high, (value - high.astype(F32)).astype(BF16)


def select_kernel(refresh_ref, got_ref, o_ref):
    for slot in range(SLOTS):
        rows = got_ref[refresh_ref[slot]]
        for k in range(4):
            o_ref[k, slot * CHUNK : (slot + 1) * CHUNK, :] = rows


def select(refresh, got):
    width = got.shape[2]
    return pl.pallas_call(
        select_kernel,
        in_specs=[SMEM, VMEM],
        out_shape=jax.ShapeDtypeStruct((4, SLOTS * CHUNK, width), BF16),
        cost_estimate=cost(0, 5 * SLOTS * CHUNK * width * 2),
        name="select",
    )(refresh, got)


def values_kernel(v_ref, w_ref, o_ref):
    for h in range(HEADS_HERE):
        cols = slice(h * HEAD_DIM, (h + 1) * HEAD_DIM)
        left = jnp.concatenate(split(w_ref[:, cols]), axis=0)
        both = lax.dot_general(
            left, v_ref[:, cols], (((1,), (1,)), ((), ())), preferred_element_type=F32
        )
        high, low = split(both[:VEC] + both[VEC:])
        o_ref[h, :VEC, :] = high
        o_ref[h, VEC:, :] = low


def project_values(value_rows, mixed):
    return pl.pallas_call(
        values_kernel,
        out_shape=jax.ShapeDtypeStruct((HEADS_HERE, 2 * VEC, KEYS), BF16),
        cost_estimate=cost(4 * KEYS * VEC * HEAD_DIM * HEADS_HERE, 4 * KEYS * 768),
        name="values",
    )(value_rows, mixed)


def base_kernel(refresh_ref, me_ref, level_ref, plain_ref, noisy_ref, cache_ref, o_ref, *rest):
    first_ref, last_ref, block_ref = rest
    row = lax.broadcasted_iota(jnp.int32, (256, 256), 0)
    col = lax.broadcasted_iota(jnp.int32, (256, 256), 1)
    choose = ((row % 128) * 2 + row // 128 == col).astype(F32).astype(BF16)
    stacked = []
    for i in range(4):
        block_ref[i] = plain_ref[:, i * 128 : (i + 1) * 128]
        pieces = []
        for b in range(2):
            parts = [block_ref[i, pl.ds(a * 2 + b, LAT_CH, 4), :] for a in range(2)]
            pieces.append(jnp.concatenate(parts, axis=0))
        stacked.append(jnp.concatenate(pieces, axis=1))
    left = jnp.concatenate(stacked, axis=0)
    high, rest = left.astype(BF16), left - left.astype(BF16).astype(F32)
    mid, low = split(rest)
    field = sum(jnp.dot(part, choose, preferred_element_type=F32) for part in (high, mid, low))
    field = jnp.concatenate([field[i * 32 : (i + 1) * 32] for i in range(4)], axis=1)
    fresh = False
    for slot in range(SLOTS):
        fresh = fresh | (refresh_ref[slot] == me_ref[0])
    level = level_ref[0]
    for a in range(2):
        rows = slice(a * LAT_CH, (a + 1) * LAT_CH)
        velocity = jnp.where(fresh, field[rows], cache_ref[a].astype(F32))
        latent = noisy_ref[a].astype(F32) - level * velocity
        o_ref[rows, :] = latent
        (first_ref, last_ref)[a][...] = latent


def latent_base(refresh, me, level, plain, noisy, cache):
    edge = jax.ShapeDtypeStruct((LAT_CH, COLS), F32)
    return pl.pallas_call(
        base_kernel,
        in_specs=[SMEM] * 3 + [VMEM] * 3,
        out_shape=(jax.ShapeDtypeStruct((2 * LAT_CH, COLS), F32), edge, edge),
        scratch_shapes=[pltpu.VMEM((4, VEC, 128), F32)],
        cost_estimate=cost(6 * 128 * 256 * 256, 1 << 19),
        name="latent_base",
    )(refresh, me, level, plain, noisy, cache)


def pack_lse(entries, width):
    row = lax.broadcasted_iota(jnp.int32, (16, width), 0)
    block = jnp.zeros((16, width), F32)
    for h, lse in enumerate(entries):
        high = lse.astype(BF16).astype(F32)
        rest = lse - high
        mid = rest.astype(BF16).astype(F32)
        low = rest - mid
        for part, value in enumerate((high, mid, low)):
            block = jnp.where(row == part * HALF + h, jnp.broadcast_to(value, block.shape), block)
    return block.astype(BF16)


def attend_kernel(qa_ref, qb_ref, k_ref, v_ref, oa_ref, ob_ref):
    scale = math.log2(math.e) / math.sqrt(HEAD_DIM)
    halves = ((qa_ref, oa_ref), (qb_ref, ob_ref))

    def scores(head):
        half, h = divmod(head, HALF)
        return lax.dot_general(
            k_ref[:, head * HEAD_DIM : (head + 1) * HEAD_DIM],
            halves[half][0][:, h * HEAD_DIM : (h + 1) * HEAD_DIM],
            (((1,), (1,)), ((), ())),
            preferred_element_type=F32,
        )

    dots, lses = scores(0), []
    for head in range(HEADS_HERE):
        half, h = divmod(head, HALF)
        o_ref = halves[half][1]
        following = scores(head + 1) if head + 1 < HEADS_HERE else None
        top = jnp.max(dots, axis=0, keepdims=True)
        exps = jnp.exp2((dots - top) * scale)
        total = jnp.sum(exps, axis=0, keepdims=True)
        parts = jnp.dot(v_ref[head], exps.astype(BF16), preferred_element_type=F32)
        o_ref[h * VEC : (h + 1) * VEC, :] = ((parts[:VEC] + parts[VEC:]) * (1.0 / total)).astype(BF16)
        lses.append(top * (1.0 / math.sqrt(HEAD_DIM)) + jnp.log(total))
        if h == HALF - 1:
            o_ref[ROWS:PACK, :] = pack_lse(lses, o_ref.shape[1])
            lses = []
        dots = following


def attend(qa, qb, keys, values):
    n = qa.shape[0]
    out = jax.ShapeDtypeStruct((PACK, n), BF16)
    return pl.pallas_call(
        attend_kernel,
        out_shape=(out, out),
        cost_estimate=cost(
            4 * n * KEYS * HEAD_DIM * HEADS_HERE, 4 * n * 768 + 4 * KEYS * 768, n * KEYS * HEADS_HERE
        ),
        name="attend",
    )(qa, qb, keys, values)


def merge(parts_of):
    blocks = [p(ROWS, PACK).astype(F32) for p in parts_of]
    outs, lses = [], []
    for h in range(HALF):
        parts = [
            b[h : h + 1] + b[HALF + h : HALF + h + 1] + b[2 * HALF + h : 2 * HALF + h + 1] for b in blocks
        ]
        top = functools.reduce(jnp.maximum, parts)
        weights = [jnp.exp(p - top) for p in parts]
        total = sum(weights)
        inverse = 1.0 / total
        acc = 0.0
        for p, w in zip(parts_of, weights):
            acc = acc + p(h * VEC, (h + 1) * VEC).astype(F32) * (w * inverse)
        outs.append(acc)
        lses.append(top + jnp.log(total))
    return outs, lses


def merge_first_kernel(me_ref, *refs):
    for half, axis in enumerate(("y", "x")):
        ins, o_ref = refs[half * 4 : half * 4 + 4], refs[8 + half]
        outs, lses = merge([lambda a, b, r=r: r[a:b, :] for r in ins])
        packed = pack_lse(lses, KEYS)
        for k in range(4):
            target = ((me_ref[0] >> BITS[axis]) - k) & 3
            cols = slice(k * 128, (k + 1) * 128)
            for h in range(HALF):
                o_ref[target, h * VEC : (h + 1) * VEC, :] = outs[h][:, cols].astype(BF16)
            o_ref[target, ROWS:PACK, :] = packed[:, cols]


def merge_first(me, a_parts, b_parts):
    return pl.pallas_call(
        merge_first_kernel,
        in_specs=[SMEM] + [VMEM] * 8,
        out_shape=(jax.ShapeDtypeStruct((4, PACK, 128), BF16),) * 2,
        cost_estimate=cost(8 * PACK * KEYS * 2, 10 * PACK * KEYS * 2),
        name="merge_first",
    )(me, *a_parts, *b_parts)


def merge_second_kernel(a_ref, b_ref, o_ref):
    for half, ref in enumerate((a_ref, b_ref)):
        outs, lses = merge([lambda a, b, k=k: ref[k, a:b, :] for k in range(4)])
        base = half * PACK
        packed = pack_lse(lses, 128)
        for k in range(4):
            for h in range(HALF):
                o_ref[k, base + h * VEC : base + (h + 1) * VEC, :] = outs[h].astype(BF16)
            o_ref[k, base + ROWS : base + PACK, :] = packed


def merge_second(a_parts, b_parts):
    return pl.pallas_call(
        merge_second_kernel,
        out_shape=jax.ShapeDtypeStruct((4, 2 * PACK, 128), BF16),
        cost_estimate=cost(8 * PACK * 128 * 2, 16 * PACK * 128 * 2),
        name="merge_second",
    )(a_parts, b_parts)


def merge_last_kernel(p_ref, o_ref):
    outs = []
    for base in (0, PACK):
        outs += merge([lambda a, b, k=k: p_ref[k, base + a : base + b, :] for k in range(4)])[0]
    o_ref[...] = sum(outs[1:], outs[0])


def merge_last(parts):
    return pl.pallas_call(
        merge_last_kernel,
        out_shape=jax.ShapeDtypeStruct((VEC, 128), F32),
        cost_estimate=cost(8 * PACK * 128 * 2, 10 * PACK * 128),
        name="merge_last",
    )(parts)


def decode_kernel(refresh_ref, me_ref, level_ref, v_ref, base_ref, up_ref, down_ref, w_ref, b_ref, o_ref):
    level, me = level_ref[0], me_ref[0]
    row = lax.broadcasted_iota(jnp.int32, (512, 128), 0)
    col = lax.broadcasted_iota(jnp.int32, (512, 128), 1)
    lane = row % 128
    target = (row // 256) * 64 + ((lane // 32) * 8 + lane % 8) * 2 + (row // 128) % 2

    def attention_rows(near, kinds):
        slot, on = 0, 0
        for s in range(SLOTS):
            hit = refresh_ref[s] == me + near
            slot = jnp.where(hit, s, slot)
            on = jnp.where(hit, 1, on)
        choose = (((lane // 8) % 4 == slot) & (target == col)).astype(F32).astype(BF16)
        count = LAT_CH * len(kinds)
        stacked = []
        for ys in range(4):
            for pair in range(2):
                pieces = []
                for xs in (pair * 2, pair * 2 + 1):
                    for b in range(2):
                        parts = [v_ref[xs, ys, pl.ds(kind * 2 + b, LAT_CH, 4), :] for kind in kinds]
                        pieces.append(jnp.concatenate(parts, axis=0))
                stacked.append(jnp.concatenate(pieces, axis=1))
        high, low = split(jnp.concatenate(stacked, axis=0))
        field = jnp.dot(high, choose, preferred_element_type=F32) + jnp.dot(
            low, choose, preferred_element_type=F32
        )
        field = jnp.concatenate([field[i * count : (i + 1) * count] for i in range(8)], axis=1)
        return jnp.where(on > 0, field, 0.0)

    own = base_ref[...] - level * attention_rows(0, (0, 1))
    up = up_ref[...] - level * attention_rows(-1, (1,))
    down = down_ref[...] - level * attention_rows(1, (0,))
    latent = jnp.concatenate([up, own, down], axis=0) / 0.3611 + 0.1159
    line = lax.broadcasted_iota(jnp.int32, latent.shape, 0)
    column = lax.broadcasted_iota(jnp.int32, latent.shape, 1)
    inside = ((line >= 16) | (me > 0)) & ((line < 48) | (me < PATCHES - 1))
    latent = jnp.where(inside, latent, 0.0)
    before = jnp.where(column == 0, 0.0, pltpu.roll(latent, 1, 1)).astype(BF16)
    after = jnp.where(column == COLS - 1, 0.0, pltpu.roll(latent, COLS - 1, 1)).astype(BF16)
    middle = latent.astype(BF16)

    channels = w_ref.shape[3]
    line = lax.broadcasted_iota(jnp.int32, (16, channels), 0)
    bias = jnp.broadcast_to(b_ref[...], (16, channels))
    high = bias.astype(BF16).astype(F32)
    mid = (bias - high).astype(BF16).astype(F32)
    bias = jnp.where(line == 0, high, jnp.where(line == 1, mid, jnp.where(line == 2, bias - high - mid, 0.0)))
    weight = [w_ref[u, v] for v in range(3) for u in range(3)] + [bias.astype(BF16)]
    weight = jnp.concatenate(weight, axis=0)
    ones = jnp.ones((16, COLS), BF16)
    for r in range(2):
        stencil = [s[r * 16 : r * 16 + 48] for s in (before, middle, after)] + [ones]
        out = lax.dot_general(
            weight, jnp.concatenate(stencil, axis=0), (((0,), (0,)), ((), ())), preferred_element_type=F32
        )
        o_ref[r] = out.astype(BF16)


def decode(refresh, me, level, gathered, base, up, down, weight, bias):
    return pl.pallas_call(
        decode_kernel,
        out_shape=jax.ShapeDtypeStruct((2, weight.shape[3], COLS), BF16),
        in_specs=[SMEM] * 3 + [VMEM] * 6,
        out_specs=VMEM,
        cost_estimate=cost(4 * 128 * 160 * 1024, 2 << 20),
        name="decode",
    )(refresh, me, level, gathered, base, up, down, weight, bias)


def on_device(
    fresh_qkv,
    kv_cache,
    hidden,
    refresh,
    out_weight,
    final_weight,
    final_bias,
    gate_scale,
    noise_level,
    noisy_latent,
    velocity_cache,
    conv_weight,
    conv_bias,
):
    me = lax.axis_index(PATCH).astype(jnp.int32)
    here = me.reshape(1)
    together = lax.optimization_barrier

    with jax.named_scope("queries"):
        own = fresh_qkv[:, 0].reshape(PATCHES, CHUNK, -1)
        own, fresh_qkv = together((own, fresh_qkv))
        got = exchange(own, PATCH)

    with jax.named_scope("latent_base"):
        plain = lax.dot_general(
            final_weight, hidden, (((0,), (1,)), ((), ())), preferred_element_type=F32
        )
        plain = plain + final_bias[:, None]
        base, edge_first, edge_last = latent_base(
            refresh, here, noise_level, plain, noisy_latent, velocity_cache
        )
        up = lax.ppermute(edge_last, PATCH, [(p, p + 1) for p in range(PATCHES - 1)])
        down = lax.ppermute(edge_first, PATCH, [(p + 1, p) for p in range(PATCHES - 1)])

    with jax.named_scope("keys_values"):
        refreshed = jnp.any(refresh == me)
        keys = jnp.where(refreshed, fresh_qkv[:, 1], kv_cache[:, 0])
        value_rows = jnp.where(refreshed, fresh_qkv[:, 2], kv_cache[:, 1])
        gated = final_weight.T.astype(F32) * gate_scale[None, :]
        high = lax.reduce_precision(gated, 8, 7)
        both = jnp.concatenate([high, gated - high], axis=0).astype(BF16)

    with jax.named_scope("queries"):
        got, base, up, down, keys, value_rows, both = together((got, base, up, down, keys, value_rows, both))
        held = exchange(select(refresh, got), "z")

    with jax.named_scope("keys_values"):
        mixed = lax.dot_general(both, out_weight, (((1,), (1,)), ((), ())), preferred_element_type=F32)
        values = project_values(value_rows, mixed[:VEC] + mixed[VEC:])

    with jax.named_scope("queries"):
        held, mixed = together((held, mixed))
        held = held.reshape(SLOTS * 4 * CHUNK, HEADS_HERE * HEAD_DIM)
        first, second = held[:, : HALF * HEAD_DIM], held[:, HALF * HEAD_DIM :]
        qa = [shift(first, "y", k) for k in range(4)]
        qb = [shift(second, "x", k) for k in range(4)]
        qa, qb, values = together((qa, qb, values))
        qa, qb = jnp.concatenate(qa, axis=0), jnp.concatenate(qb, axis=0)

    with jax.named_scope("attention"):
        back_a, back_b = [None] * 4, [None] * 4
        got_a, got_b = [qa] + [None] * 3, [qb] + [None] * 3
        for k in (1, 3):
            got_a[k], got_b[k] = shift(qa, "x", k), shift(qb, "y", k)
        back_a[0], back_b[0] = attend(qa, qb, keys, values)
        qa, qb, back_a[0], back_b[0] = together((qa, qb, back_a[0], back_b[0]))
        got_a[2], got_b[2] = shift(qa, "x", 2), shift(qb, "y", 2)
        for k in (1, 3, 2):
            out_a, out_b = attend(got_a[k], got_b[k], keys, values)
            back_a[k], back_b[k] = shift(out_a, "x", -k), shift(out_b, "y", -k)
            if k == 1:
                got_a[3], got_b[3], _ = together((got_a[3], got_b[3], out_a))
            if k == 3:
                got_a[2], got_b[2], back_a[1], back_b[1], _ = together(
                    (got_a[2], got_b[2], back_a[1], back_b[1], out_a)
                )
        parts_a, parts_b = merge_first(here, back_a, back_b)
        part = merge_second(exchange(parts_a, "y"), exchange(parts_b, "x"))
        term = merge_last(exchange(part, "z"))

    with jax.named_scope("velocity"):
        term = jnp.sum(lax.all_gather(term, HEAD), axis=0)
        term = exchange(spread_out(term), "y")
        gathered = exchange(spread_out(term), "x")

    with jax.named_scope("decode"):
        weight = conv_weight.transpose(1, 2, 3, 0)
        return decode(
            refresh, here, noise_level, gathered, base, up, down, weight, conv_bias.reshape(1, -1)
        )


def solution(mesh):
    wide = Mesh(mesh.devices.reshape(4, 4, 4, 2, 2), PATCH + HEAD)
    return jax.shard_map(
        on_device,
        mesh=wide,
        in_specs=(
            P(PATCH, None, HEAD),
            P(PATCH, None, HEAD),
            P(PATCH, None),
            P(),
            P(HEAD, None),
            P(),
            P(),
            P(),
            P(),
            P(PATCH, None, None),
            P(PATCH, None, None),
            P(HEAD, None, None, None),
            P(HEAD),
        ),
        out_specs=P(PATCH, HEAD, None),
        check_vma=False,
    )
```

profile of v0, /device:TPU:32, one launch (start us, length us, event | category | flops | bytes accessed | tf_op | source)
XLA Modules:
  0.0 199.4 jit_solution(8866448176109042847)
XLA Ops:
  2.2 13.9 %all-to-all-start = ((bf16[64,8,768]{2,1,0:T(8,128)(2,1)}), bf16[64,8,768]{2,1,0:T(8,128)(2,1)}, u32[]{:S(2)}, u32[]{:S(2)}) async-start(bf16[64,8,768]{2,1,0:T(8,128)(2,1)} %slice_bitcast_fusion), calls=%async_computation | async-start | bytes 1572864 | tf_op jit(solution)/shard_map/queries/all_to_all | solution.py:42
  16.8 2.4 %convolution_add_fusion.plain_ref = f32[64,512]{1,0:T(8,128)} fusion(bf16[3072,64]{0,1:T(8,128)(2,1)S(1)} %copy-done.3, bf16[512,3072]{1,0:T(8,128)(2,1)S(1)} %copy-done, f32[64]{0:T(128)} %param.19), kind=kOutput, calls=%fused_computation | convolution fusion | flops 201359360 | bytes 3670272 | tf_op jit(solution)/shard_map/latent_base/dot_general | solution.py:369
  21.1 5.0 %collective-permute-start = (f32[16,1024]{1,0:T(8,128)}, f32[16,1024]{1,0:T(8,128)}, u32[]{:S(2)}, u32[]{:S(2)}) collective-permute-start(f32[16,1024]{1,0:T(8,128)} %get-tuple-element.49), channel_id=1, source_target_pairs={{0,4},{4,8},{8,12},{12,16},{16,20},{20,24},{24,28},{28,32},{32,36}... | collective-permute-start | bytes 196616 | tf_op jit(solution)/shard_map/latent_base/ppermute | solution.py:376
  35.4 7.9 %all-to-all-done.got_ref = bf16[64,8,768]{2,1,0:T(8,128)(2,1)} async-done(((bf16[64,8,768]{2,1,0:T(8,128)(2,1)}), bf16[64,8,768]{2,1,0:T(8,128)(2,1)}, u32[]{:S(2)}, u32[]{:S(2)}) %all-to-all-start) | async-done | bytes 786464 | tf_op jit(solution)/shard_map/queries/all_to_all | solution.py:42
  45.1 4.0 %all-to-all-start.1 = ((bf16[4,32,768]{2,1,0:T(8,128)(2,1)}), bf16[4,32,768]{2,1,0:T(8,128)(2,1)}, u32[]{:S(2)}, u32[]{:S(2)}) async-start(bf16[4,32,768]{2,1,0:T(8,128)(2,1)} %select.1), calls=%async_computation.1 | async-start | bytes 393216 | tf_op jit(solution)/shard_map/queries/all_to_all | solution.py:42
  49.1 4.3 %fusion.5 = f32[128,768]{1,0:T(8,128)S(1)} fusion(bf16[128,3072]{1,0:T(8,128)(2,1)} %pad_maximum_fusion, bf16[768,3072]{1,0:T(8,128)(2,1)} %param.17), kind=kOutput, calls=%fused_computation.23 | convolution fusion | flops 603979776 | bytes 5898240 | tf_op jit(solution)/shard_map/keys_values/dot_general | solution.py:392
  53.4 4.5 %all-to-all-done.1 = bf16[4,32,768]{2,1,0:T(8,128)(2,1)} async-done(((bf16[4,32,768]{2,1,0:T(8,128)(2,1)}), bf16[4,32,768]{2,1,0:T(8,128)(2,1)}, u32[]{:S(2)}, u32[]{:S(2)}) %all-to-all-start.1) | async-done | bytes 196640 | tf_op jit(solution)/shard_map/queries/all_to_all | solution.py:42
  59.6 3.3 %collective-permute-start.3 = (bf16[128,384]{1,0:T(8,128)(2,1)}, bf16[128,384]{1,0:T(8,128)(2,1)}, u32[]{:S(2)}, u32[]{:S(2)}) collective-permute-start(bf16[128,384]{1,0:T(8,128)(2,1)} %get-tuple-element.56), channel_id=1, source_target_pairs={{0,128},{64,192},{128,0},{192,64},{1,129},{65,193},{129,1},{193,65... | collective-permute-start | bytes 294920 | tf_op jit(solution)/shard_map/queries/ppermute | solution.py:34
  68.8 2.4 %values.1.v_ref = bf16[6,128,512]{2,1,0:T(8,128)(2,1)} custom-call(bf16[512,768]{1,0:T(8,128)(2,1)} %get-tuple-element.55.v_ref, f32[64,768]{1,0:T(8,128)} %slice_add_fusion.w_ref), custom_call_target="tpu_custom_call" | custom-call | flops 100663296 | bytes 1572864 | tf_op jit(solution)/shard_map/keys_values/values/pallas_call | solution.py:89
  90.4 4.8 %attend.4 = (bf16[208,512]{1,0:T(8,128)(2,1)}, bf16[208,512]{1,0:T(8,128)(2,1)}) custom-call(bf16[512,384]{1,0:T(8,128)(2,1)} %constant_dynamic-update-slice_fusion.qa_ref, bf16[512,384]{1,0:T(8,128)(2,1)} %constant_dynamic-update-slice_fusion.4.qb_ref, bf16[512,768]{1,0:T(8,128)(2,1)} %get-tuple-element.64.k_ref, bf16[6,128,512]{2,1,0:T(8,128)(2,1)} %values.1.v_ref), custom_call_target="tpu_custom_call" | custom-call | flops 805306368 | bytes 3145728 | tf_op jit(solution)/shard_map/attention/attend/pallas_call | solution.py:185
  96.9 4.8 %attend.5 = (bf16[208,512]{1,0:T(8,128)(2,1)}, bf16[208,512]{1,0:T(8,128)(2,1)}) custom-call(bf16[512,384]{1,0:T(8,128)(2,1)} %copy-done.7, bf16[512,384]{1,0:T(8,128)(2,1)} %collective-permute-done.11.qb_ref, bf16[512,768]{1,0:T(8,128)(2,1)} %get-tuple-element.64.k_ref, bf16[6,128,512]{2,1,0:T(8,128)(2,1)} %values.1.v_ref), custom_call_target="tpu_custom_call" | custom-call | flops 805306368 | bytes 3145728 | tf_op jit(solution)/shard_map/attention/attend/pallas_call | solution.py:185
  105.3 4.8 %attend.6 = (bf16[208,512]{1,0:T(8,128)(2,1)}, bf16[208,512]{1,0:T(8,128)(2,1)}) custom-call(bf16[512,384]{1,0:T(8,128)(2,1)} %collective-permute-done.14.qa_ref, bf16[512,384]{1,0:T(8,128)(2,1)} %collective-permute-done.15.qb_ref, bf16[512,768]{1,0:T(8,128)(2,1)} %get-tuple-element.64.k_ref, bf16[6,128,512]{2,1,0:T(8,128)(2,1)} %values.1.v_ref), custom_call_target="tpu_custom_call" | custom-call | flops 805306368 | bytes 3145728 | tf_op jit(solution)/shard_map/attention/attend/pallas_call | solution.py:185
  110.6 4.8 %attend.7 = (bf16[208,512]{1,0:T(8,128)(2,1)}, bf16[208,512]{1,0:T(8,128)(2,1)}) custom-call(bf16[512,384]{1,0:T(8,128)(2,1)} %collective-permute-done.8.qa_ref, bf16[512,384]{1,0:T(8,128)(2,1)} %collective-permute-done.9.qb_ref, bf16[512,768]{1,0:T(8,128)(2,1)} %get-tuple-element.64.k_ref, bf16[6,128,512]{2,1,0:T(8,128)(2,1)} %values.1.v_ref), custom_call_target="tpu_custom_call" | custom-call | flops 805306368 | bytes 3145728 | tf_op jit(solution)/shard_map/attention/attend/pallas_call | solution.py:185
  115.4 2.8 %collective-permute-start.16 = (bf16[208,512]{1,0:T(8,128)(2,1)}, bf16[208,512]{1,0:T(8,128)(2,1)}, u32[]{:S(2)}, u32[]{:S(2)}) collective-permute-start(bf16[208,512]{1,0:T(8,128)(2,1)} %get-tuple-element.79), channel_id=1, source_target_pairs={{0,32},{16,48},{32,0},{48,16},{1,33},{17,49},{33,1},{49,17},{2,34}... | collective-permute-start | bytes 638984 | tf_op jit(solution)/shard_map/attention/ppermute | solution.py:34
  118.2 2.6 %collective-permute-start.18 = (bf16[208,512]{1,0:T(8,128)(2,1)}, bf16[208,512]{1,0:T(8,128)(2,1)}, u32[]{:S(2)}, u32[]{:S(2)}) collective-permute-start(bf16[208,512]{1,0:T(8,128)(2,1)} %get-tuple-element.82), channel_id=1, source_target_pairs={{0,128},{64,192},{128,0},{192,64},{1,129},{65,193},{129,1},{193,65... | collective-permute-start | bytes 638984 | tf_op jit(solution)/shard_map/attention/ppermute | solution.py:34
  123.1 2.8 %collective-permute-done.18.refs_6_ = bf16[208,512]{1,0:T(8,128)(2,1)} collective-permute-done((bf16[208,512]{1,0:T(8,128)(2,1)}, bf16[208,512]{1,0:T(8,128)(2,1)}, u32[]{:S(2)}, u32[]{:S(2)}) %collective-permute-start.18) | collective-permute-done | bytes 213024 | tf_op jit(solution)/shard_map/attention/ppermute | solution.py:34
  125.9 2.7 %merge_first.1 = (bf16[4,208,128]{2,1,0:T(8,128)(2,1)}, bf16[4,208,128]{2,1,0:T(8,128)(2,1)}) custom-call(s32[1]{0:T(128)} %bitcast.me_ref, bf16[208,512]{1,0:T(8,128)(2,1)} %get-tuple-element.68.refs_0_, bf16[208,512]{1,0:T(8,128)(2,1)} %copy-done.4, bf16[208,512]{1,0:T(8,128)(2,1)} %collective-permute-done.16.refs_2_, ...), custom_call_target="tpu_custom_call" | custom-call | flops 1703936 | bytes 2129920 | tf_op jit(solution)/shard_map/attention/merge_first/pallas_call | solution.py:228
  128.6 10.9 %all_to_all.35.a_ref = bf16[4,208,128]{2,1,0:T(8,128)(2,1)} all-to-all(bf16[4,208,128]{2,1,0:T(8,128)(2,1)} %get-tuple-element.84), channel_id=1, replica_groups=mesh['y'=4,'x'=4,'z'=4,'w'=2,'c'=2] {'y'}, dimensions={0} | all-to-all | bytes 425984 | tf_op jit(solution)/shard_map/attention/all_to_all | solution.py:42
  139.5 10.5 %all_to_all.36.b_ref = bf16[4,208,128]{2,1,0:T(8,128)(2,1)} all-to-all(bf16[4,208,128]{2,1,0:T(8,128)(2,1)} %get-tuple-element.85), channel_id=1, replica_groups=mesh['y'=4,'x'=4,'z'=4,'w'=2,'c'=2] {'x'}, dimensions={0} | all-to-all | bytes 425984 | tf_op jit(solution)/shard_map/attention/all_to_all | solution.py:42
  151.9 16.4 %all_to_all.37.p_ref = bf16[4,416,128]{2,1,0:T(8,128)(2,1)} all-to-all(bf16[4,416,128]{2,1,0:T(8,128)(2,1)} %merge_second.1), channel_id=1, replica_groups=mesh['y'=4,'x'=4,'z'=4,'w'=2,'c'=2] {'z'}, dimensions={0} | all-to-all | bytes 851968 | tf_op jit(solution)/shard_map/attention/all_to_all | solution.py:42
  170.1 5.6 %all-gather = f32[256,128]{1,0:T(8,128)S(1)} all-gather(f32[64,128]{1,0:T(8,128)} %merge_last.1), channel_id=2, replica_groups=mesh['y'=4,'x'=4,'z'=4,'w'=2,'c'=2] {'w','c'}, dimensions={0}, use_global_device_ids=true | all-gather | bytes 163840 | tf_op jit(solution)/shard_map/velocity/all_gather | solution.py:426
  175.7 8.4 %all_to_all.38 = f32[4,64,128]{2,1,0:T(8,128)S(1)} all-to-all(f32[4,64,128]{2,1,0:T(8,128)S(1)} %broadcast_in_dim.4), channel_id=1, replica_groups=mesh['y'=4,'x'=4,'z'=4,'w'=2,'c'=2] {'y'}, dimensions={0} | all-to-all | bytes 262144 | tf_op jit(solution)/shard_map/velocity/all_to_all | solution.py:42
  184.2 12.3 %all_to_all.39.v_ref = f32[4,4,64,128]{3,2,1,0:T(8,128)} all-to-all(f32[4,4,64,128]{3,2,1,0:T(8,128)S(1)} %broadcast_in_dim.5), channel_id=1, replica_groups=mesh['y'=4,'x'=4,'z'=4,'w'=2,'c'=2] {'x'}, dimensions={0} | all-to-all | bytes 1048576 | tf_op jit(solution)/shard_map/velocity/all_to_all | solution.py:42
  196.5 2.9 %decode.1 = bf16[2,128,1024]{2,1,0:T(8,128)(2,1)} custom-call(s32[4]{0:T(128)} %refresh_ref.5, s32[1]{0:T(128)} %bitcast.me_ref, f32[1]{0:T(128)S(6)} %copy.30.level_ref, f32[4,4,64,128]{3,2,1,0:T(8,128)} %all_to_all.39.v_ref, f32[32,1024]{1,0:T(8,128)} %get-tuple-element.86.base_ref, f32[16,1024]{1,0:T(8,128)} %collective-permute-done.up_ref, ...), custom_call_target="tpu_custom_call" | custom-call | flops 83886080 | bytes 2097152 | tf_op jit(solution)/shard_map/decode/decode/pallas_call | solution.py:334
  (74 shorter events, 53.7 us)
Async XLA Ops:
  0.0 16.8 %copy-start = (bf16[512,3072]{1,0:T(8,128)(2,1)S(1)}, bf16[512,3072]{1,0:T(8,128)(2,1)}, u32[]{:S(2)}) copy-start(bf16[512,3072]{1,0:T(8,128)(2,1)} %param.15) | copy-start | bytes 9437188
  0.0 16.8 %copy-start.3 = (bf16[3072,64]{0,1:T(8,128)(2,1)S(1)}, bf16[3072,64]{0,1:T(8,128)(2,1)}, u32[]{:S(2)}) copy-start(bf16[3072,64]{0,1:T(8,128)(2,1)} %param.18) | copy-start | bytes 1179652
  2.2 41.1 %all-to-all-start = ((bf16[64,8,768]{2,1,0:T(8,128)(2,1)}), bf16[64,8,768]{2,1,0:T(8,128)(2,1)}, u32[]{:S(2)}, u32[]{:S(2)}) async-start(bf16[64,8,768]{2,1,0:T(8,128)(2,1)} %slice_bitcast_fusion), calls=%async_computation | async-start | bytes 1572864 | tf_op jit(solution)/shard_map/queries/all_to_all | solution.py:42
  21.1 13.9 %collective-permute-start = (f32[16,1024]{1,0:T(8,128)}, f32[16,1024]{1,0:T(8,128)}, u32[]{:S(2)}, u32[]{:S(2)}) collective-permute-start(f32[16,1024]{1,0:T(8,128)} %get-tuple-element.49), channel_id=1, source_target_pairs={{0,4},{4,8},{8,12},{12,16},{16,20},{20,24},{24,28},{28,32},{32,36}... | collective-permute-start | bytes 196616 | tf_op jit(solution)/shard_map/latent_base/ppermute | solution.py:376
  26.1 9.2 %collective-permute-start.1 = (f32[16,1024]{1,0:T(8,128)}, f32[16,1024]{1,0:T(8,128)}, u32[]{:S(2)}, u32[]{:S(2)}) collective-permute-start(f32[16,1024]{1,0:T(8,128)} %get-tuple-element.50), channel_id=1, source_target_pairs={{4,0},{8,4},{12,8},{16,12},{20,16},{24,20},{28,24},{32,28},{36,32}... | collective-permute-start | bytes 196616 | tf_op jit(solution)/shard_map/latent_base/ppermute | solution.py:377
  45.1 12.8 %all-to-all-start.1 = ((bf16[4,32,768]{2,1,0:T(8,128)(2,1)}), bf16[4,32,768]{2,1,0:T(8,128)(2,1)}, u32[]{:S(2)}, u32[]{:S(2)}) async-start(bf16[4,32,768]{2,1,0:T(8,128)(2,1)} %select.1), calls=%async_computation.1 | async-start | bytes 393216 | tf_op jit(solution)/shard_map/queries/all_to_all | solution.py:42
  59.6 6.8 %collective-permute-start.2 = (bf16[128,384]{1,0:T(8,128)(2,1)}, bf16[128,384]{1,0:T(8,128)(2,1)}, u32[]{:S(2)}, u32[]{:S(2)}) collective-permute-start(bf16[128,384]{1,0:T(8,128)(2,1)} %get-tuple-element.56), channel_id=1, source_target_pairs={{0,64},{64,128},{128,192},{192,0},{1,65},{65,129},{129,193},{193,1... | collective-permute-start | bytes 294920 | tf_op jit(solution)/shard_map/queries/ppermute | solution.py:34
  59.6 11.6 %collective-permute-start.3 = (bf16[128,384]{1,0:T(8,128)(2,1)}, bf16[128,384]{1,0:T(8,128)(2,1)}, u32[]{:S(2)}, u32[]{:S(2)}) collective-permute-start(bf16[128,384]{1,0:T(8,128)(2,1)} %get-tuple-element.56), channel_id=1, source_target_pairs={{0,128},{64,192},{128,0},{192,64},{1,129},{65,193},{129,1},{193,65... | collective-permute-start | bytes 294920 | tf_op jit(solution)/shard_map/queries/ppermute | solution.py:34
  63.0 8.3 %collective-permute-start.4 = (bf16[128,384]{1,0:T(8,128)(2,1)}, bf16[128,384]{1,0:T(8,128)(2,1)}, u32[]{:S(2)}, u32[]{:S(2)}) collective-permute-start(bf16[128,384]{1,0:T(8,128)(2,1)} %get-tuple-element.56), channel_id=1, source_target_pairs={{0,192},{64,0},{128,64},{192,128},{1,193},{65,1},{129,65},{193,129... | collective-permute-start | bytes 294920 | tf_op jit(solution)/shard_map/queries/ppermute | solution.py:34
  63.6 7.6 %collective-permute-start.5 = (bf16[128,384]{1,0:T(8,128)(2,1)}, bf16[128,384]{1,0:T(8,128)(2,1)}, u32[]{:S(2)}, u32[]{:S(2)}) collective-permute-start(bf16[128,384]{1,0:T(8,128)(2,1)} %get-tuple-element.60), channel_id=1, source_target_pairs={{0,16},{16,32},{32,48},{48,0},{1,17},{17,33},{33,49},{49,1},{2,18}... | collective-permute-start | bytes 294920 | tf_op jit(solution)/shard_map/queries/ppermute | solution.py:34
  64.0 7.2 %collective-permute-start.6 = (bf16[128,384]{1,0:T(8,128)(2,1)}, bf16[128,384]{1,0:T(8,128)(2,1)}, u32[]{:S(2)}, u32[]{:S(2)}) collective-permute-start(bf16[128,384]{1,0:T(8,128)(2,1)} %get-tuple-element.60), channel_id=1, source_target_pairs={{0,32},{16,48},{32,0},{48,16},{1,33},{17,49},{33,1},{49,17},{2,34}... | collective-permute-start | bytes 294920 | tf_op jit(solution)/shard_map/queries/ppermute | solution.py:34
  66.3 5.3 %collective-permute-start.7 = (bf16[128,384]{1,0:T(8,128)(2,1)}, bf16[128,384]{1,0:T(8,128)(2,1)}, u32[]{:S(2)}, u32[]{:S(2)}) collective-permute-start(bf16[128,384]{1,0:T(8,128)(2,1)} %get-tuple-element.60), channel_id=1, source_target_pairs={{0,48},{16,0},{32,16},{48,32},{1,49},{17,1},{33,17},{49,33},{2,50}... | collective-permute-start | bytes 294920 | tf_op jit(solution)/shard_map/queries/ppermute | solution.py:34
  79.4 16.7 %collective-permute-start.10 = (bf16[512,384]{1,0:T(8,128)(2,1)}, bf16[512,384]{1,0:T(8,128)(2,1)S(1)}, u32[]{:S(2)}, u32[]{:S(2)}) collective-permute-start(bf16[512,384]{1,0:T(8,128)(2,1)} %constant_dynamic-update-slice_fusion.qa_ref), channel_id=1, source_target_pairs={{0,16},{16,32},{32,48},{48,0},{1,17},{17,33},{33,49},{49,1},{2,18}... | collective-permute-start | bytes 1179656 | tf_op jit(solution)/shard_map/attention/ppermute | solution.py:34
  85.2 11.5 %collective-permute-start.11 = (bf16[512,384]{1,0:T(8,128)(2,1)}, bf16[512,384]{1,0:T(8,128)(2,1)}, u32[]{:S(2)}, u32[]{:S(2)}) collective-permute-start(bf16[512,384]{1,0:T(8,128)(2,1)} %constant_dynamic-update-slice_fusion.4.qb_ref), channel_id=1, source_target_pairs={{0,64},{64,128},{128,192},{192,0},{1,65},{65,129},{129,193},{193,1... | collective-permute-start | bytes 1179656 | tf_op jit(solution)/shard_map/attention/ppermute | solution.py:34
  86.3 17.1 %collective-permute-start.14 = (bf16[512,384]{1,0:T(8,128)(2,1)}, bf16[512,384]{1,0:T(8,128)(2,1)}, u32[]{:S(2)}, u32[]{:S(2)}) collective-permute-start(bf16[512,384]{1,0:T(8,128)(2,1)} %constant_dynamic-update-slice_fusion.qa_ref), channel_id=1, source_target_pairs={{0,48},{16,0},{32,16},{48,32},{1,49},{17,1},{33,17},{49,33},{2,50}... | collective-permute-start | bytes 1179656 | tf_op jit(solution)/shard_map/attention/ppermute | solution.py:34
  88.6 16.7 %collective-permute-start.15 = (bf16[512,384]{1,0:T(8,128)(2,1)}, bf16[512,384]{1,0:T(8,128)(2,1)}, u32[]{:S(2)}, u32[]{:S(2)}) collective-permute-start(bf16[512,384]{1,0:T(8,128)(2,1)} %constant_dynamic-update-slice_fusion.4.qb_ref), channel_id=1, source_target_pairs={{0,192},{64,0},{128,64},{192,128},{1,193},{65,1},{129,65},{193,129... | collective-permute-start | bytes 1179656 | tf_op jit(solution)/shard_map/attention/ppermute | solution.py:34
  95.2 15.3 %collective-permute-start.8 = (bf16[512,384]{1,0:T(8,128)(2,1)}, bf16[512,384]{1,0:T(8,128)(2,1)}, u32[]{:S(2)}, u32[]{:S(2)}) collective-permute-start(bf16[512,384]{1,0:T(8,128)(2,1)} %constant_dynamic-update-slice_fusion.qa_ref), channel_id=1, source_target_pairs={{0,32},{16,48},{32,0},{48,16},{1,33},{17,49},{33,1},{49,17},{2,34}... | collective-permute-start | bytes 1179656 | tf_op jit(solution)/shard_map/attention/ppermute | solution.py:34
  96.1 14.5 %collective-permute-start.9 = (bf16[512,384]{1,0:T(8,128)(2,1)}, bf16[512,384]{1,0:T(8,128)(2,1)}, u32[]{:S(2)}, u32[]{:S(2)}) collective-permute-start(bf16[512,384]{1,0:T(8,128)(2,1)} %constant_dynamic-update-slice_fusion.4.qb_ref), channel_id=1, source_target_pairs={{0,128},{64,192},{128,0},{192,64},{1,129},{65,193},{129,1},{193,65... | collective-permute-start | bytes 1179656 | tf_op jit(solution)/shard_map/attention/ppermute | solution.py:34
  101.6 8.9 %collective-permute-start.12 = (bf16[208,512]{1,0:T(8,128)(2,1)}, bf16[208,512]{1,0:T(8,128)(2,1)S(1)}, u32[]{:S(2)}, u32[]{:S(2)}) collective-permute-start(bf16[208,512]{1,0:T(8,128)(2,1)} %get-tuple-element.71), channel_id=1, source_target_pairs={{0,48},{16,0},{32,16},{48,32},{1,49},{17,1},{33,17},{49,33},{2,50}... | collective-permute-start | bytes 638984 | tf_op jit(solution)/shard_map/attention/ppermute | solution.py:34
  103.5 7.1 %collective-permute-start.13 = (bf16[208,512]{1,0:T(8,128)(2,1)}, bf16[208,512]{1,0:T(8,128)(2,1)}, u32[]{:S(2)}, u32[]{:S(2)}) collective-permute-start(bf16[208,512]{1,0:T(8,128)(2,1)} %get-tuple-element.72), channel_id=1, source_target_pairs={{0,192},{64,0},{128,64},{192,128},{1,193},{65,1},{129,65},{193,129... | collective-permute-start | bytes 638984 | tf_op jit(solution)/shard_map/attention/ppermute | solution.py:34
  110.1 10.7 %collective-permute-start.17 = (bf16[208,512]{1,0:T(8,128)(2,1)}, bf16[208,512]{1,0:T(8,128)(2,1)}, u32[]{:S(2)}, u32[]{:S(2)}) collective-permute-start(bf16[208,512]{1,0:T(8,128)(2,1)} %get-tuple-element.75), channel_id=1, source_target_pairs={{0,16},{16,32},{32,48},{48,0},{1,17},{17,33},{33,49},{49,1},{2,18}... | collective-permute-start | bytes 638984 | tf_op jit(solution)/shard_map/attention/ppermute | solution.py:34
  110.6 10.2 %collective-permute-start.19 = (bf16[208,512]{1,0:T(8,128)(2,1)}, bf16[208,512]{1,0:T(8,128)(2,1)}, u32[]{:S(2)}, u32[]{:S(2)}) collective-permute-start(bf16[208,512]{1,0:T(8,128)(2,1)} %get-tuple-element.83), channel_id=1, source_target_pairs={{0,64},{64,128},{128,192},{192,0},{1,65},{65,129},{129,193},{193,1... | collective-permute-start | bytes 638984 | tf_op jit(solution)/shard_map/attention/ppermute | solution.py:34
  115.4 7.7 %collective-permute-start.16 = (bf16[208,512]{1,0:T(8,128)(2,1)}, bf16[208,512]{1,0:T(8,128)(2,1)}, u32[]{:S(2)}, u32[]{:S(2)}) collective-permute-start(bf16[208,512]{1,0:T(8,128)(2,1)} %get-tuple-element.79), channel_id=1, source_target_pairs={{0,32},{16,48},{32,0},{48,16},{1,33},{17,49},{33,1},{49,17},{2,34}... | collective-permute-start | bytes 638984 | tf_op jit(solution)/shard_map/attention/ppermute | solution.py:34
  118.2 7.7 %collective-permute-start.18 = (bf16[208,512]{1,0:T(8,128)(2,1)}, bf16[208,512]{1,0:T(8,128)(2,1)}, u32[]{:S(2)}, u32[]{:S(2)}) collective-permute-start(bf16[208,512]{1,0:T(8,128)(2,1)} %get-tuple-element.82), channel_id=1, source_target_pairs={{0,128},{64,192},{128,0},{192,64},{1,129},{65,193},{129,1},{193,65... | collective-permute-start | bytes 638984 | tf_op jit(solution)/shard_map/attention/ppermute | solution.py:34
  (6 other events, 48.4 us)
where the time goes:
time: 201 us; the launch traced here: 199 us
  blocking collectives  64.1 us (32%)
  starting transfers between devices  50.2 us (25%)
  Pallas kernels  34.6 us (17%)
  waiting for transfers between devices  19.9 us (10%)
  local copies, waits for them, and re-layouts  18.6 us (9%)
  matrix products  6.65 us (3%)
  other arithmetic  4.46 us (2%)
    all_to_all x5, blocking collectives, exchange(): return lax.all_to_all(value, axis, 0, 0)  58.5 us
    ppermute x18, starting transfers between devices, shift(): return lax.ppermute(value, axis, [(i, (i + step) % 4) for i in range(4)])  26 us
    pallas_call x4, Pallas kernels, attend(): pl.pallas_call(attend_kernel, out_shape=(out, out), cost_estimate=cost(4...  19.2 us
    all_to_all x2, starting transfers between devices, exchange(): return lax.all_to_all(value, axis, 0, 0)  17.9 us
    all_to_all x2, waiting for transfers between devices, exchange(): return lax.all_to_all(value, axis, 0, 0)  12.5 us
    unnamed x22, local copies, waits for them, and re-layouts  9.37 us
    all_gather x1, blocking collectives, on_device(): term = jnp.sum(lax.all_gather(term, HEAD), axis=0)  5.62 us
    ppermute x18, waiting for transfers between devices, shift(): return lax.ppermute(value, axis, [(i, (i + step) % 4) for i in range(4)])  5.54 us
  transfers between devices with their start and end apart: 22, of which 7 were waited for; matrix products, arithmetic and copies ran while one was open for 9% of the time, Pallas kernels for 12%

commit v1 on v0

--- a/solution.py
+++ b/solution.py
@@ -34,8 +34,8 @@
     return lax.ppermute(value, axis, [(i, (i + step) % 4) for i in range(4)])
 
 
-def spread_out(value):
-    return jnp.broadcast_to(value[None], (4,) + value.shape)
+def spread_out(value, count):
+    return jnp.broadcast_to(value[None], (count,) + value.shape)
 
 
 def exchange(value, axis):
@@ -58,7 +58,7 @@
 def select_kernel(refresh_ref, got_ref, o_ref):
     for slot in range(SLOTS):
         rows = got_ref[refresh_ref[slot]]
-        for k in range(4):
+        for k in range(o_ref.shape[0]):
             o_ref[k, slot * CHUNK : (slot + 1) * CHUNK, :] = rows
 
 
@@ -67,8 +67,8 @@
     return pl.pallas_call(
         select_kernel,
         in_specs=[SMEM, VMEM],
-        out_shape=jax.ShapeDtypeStruct((4, SLOTS * CHUNK, width), BF16),
-        cost_estimate=cost(0, 5 * SLOTS * CHUNK * width * 2),
+        out_shape=jax.ShapeDtypeStruct((16, SLOTS * CHUNK, width), BF16),
+        cost_estimate=cost(0, 17 * SLOTS * CHUNK * width * 2),
         name="select",
     )(refresh, got)
 
@@ -149,47 +149,42 @@
     return block.astype(BF16)
 
 
-def attend_kernel(qa_ref, qb_ref, k_ref, v_ref, oa_ref, ob_ref):
+def attend_kernel(q_ref, k_ref, v_ref, o_ref):
     scale = math.log2(math.e) / math.sqrt(HEAD_DIM)
-    halves = ((qa_ref, oa_ref), (qb_ref, ob_ref))
 
     def scores(head):
-        half, h = divmod(head, HALF)
+        cols = slice(head * HEAD_DIM, (head + 1) * HEAD_DIM)
         return lax.dot_general(
-            k_ref[:, head * HEAD_DIM : (head + 1) * HEAD_DIM],
-            halves[half][0][:, h * HEAD_DIM : (h + 1) * HEAD_DIM],
-            (((1,), (1,)), ((), ())),
-            preferred_element_type=F32,
+            k_ref[:, cols], q_ref[:, cols], (((1,), (1,)), ((), ())), preferred_element_type=F32
         )
 
     dots, lses = scores(0), []
     for head in range(HEADS_HERE):
         half, h = divmod(head, HALF)
-        o_ref = halves[half][1]
         following = scores(head + 1) if head + 1 < HEADS_HERE else None
         top = jnp.max(dots, axis=0, keepdims=True)
         exps = jnp.exp2((dots - top) * scale)
         total = jnp.sum(exps, axis=0, keepdims=True)
         parts = jnp.dot(v_ref[head], exps.astype(BF16), preferred_element_type=F32)
-        o_ref[h * VEC : (h + 1) * VEC, :] = ((parts[:VEC] + parts[VEC:]) * (1.0 / total)).astype(BF16)
+        row = half * PACK + h * VEC
+        o_ref[row : row + VEC, :] = ((parts[:VEC] + parts[VEC:]) * (1.0 / total)).astype(BF16)
         lses.append(top * (1.0 / math.sqrt(HEAD_DIM)) + jnp.log(total))
         if h == HALF - 1:
-            o_ref[ROWS:PACK, :] = pack_lse(lses, o_ref.shape[1])
+            o_ref[half * PACK + ROWS : (half + 1) * PACK, :] = pack_lse(lses, o_ref.shape[1])
             lses = []
         dots = following
 
 
-def attend(qa, qb, keys, values):
-    n = qa.shape[0]
-    out = jax.ShapeDtypeStruct((PACK, n), BF16)
+def attend(queries, keys, values):
+    n = queries.shape[0]
     return pl.pallas_call(
         attend_kernel,
-        out_shape=(out, out),
+        out_shape=jax.ShapeDtypeStruct((2 * PACK, n), BF16),
         cost_estimate=cost(
             4 * n * KEYS * HEAD_DIM * HEADS_HERE, 4 * n * 768 + 4 * KEYS * 768, n * KEYS * HEADS_HERE
         ),
         name="attend",
-    )(qa, qb, keys, values)
+    )(queries, keys, values)
 
 
 def merge(parts_of):
@@ -211,33 +206,30 @@
     return outs, lses
 
 
-def merge_first_kernel(me_ref, *refs):
-    for half, axis in enumerate(("y", "x")):
-        ins, o_ref = refs[half * 4 : half * 4 + 4], refs[8 + half]
-        outs, lses = merge([lambda a, b, r=r: r[a:b, :] for r in ins])
+def merge_first_kernel(*refs):
+    o_ref = refs[4]
+    for base in (0, PACK):
+        outs, lses = merge([lambda a, b, r=r: r[base + a : base + b, :] for r in refs[:4]])
         packed = pack_lse(lses, KEYS)
         for k in range(4):
-            target = ((me_ref[0] >> BITS[axis]) - k) & 3
             cols = slice(k * 128, (k + 1) * 128)
             for h in range(HALF):
-                o_ref[target, h * VEC : (h + 1) * VEC, :] = outs[h][:, cols].astype(BF16)
-            o_ref[target, ROWS:PACK, :] = packed[:, cols]
-
-
-def merge_first(me, a_parts, b_parts):
+                o_ref[k, base + h * VEC : base + (h + 1) * VEC, :] = outs[h][:, cols].astype(BF16)
+            o_ref[k, base + ROWS : base + PACK, :] = packed[:, cols]
+
+
+def merge_first(parts):
     return pl.pallas_call(
         merge_first_kernel,
-        in_specs=[SMEM] + [VMEM] * 8,
-        out_shape=(jax.ShapeDtypeStruct((4, PACK, 128), BF16),) * 2,
+        out_shape=jax.ShapeDtypeStruct((4, 2 * PACK, 128), BF16),
         cost_estimate=cost(8 * PACK * KEYS * 2, 10 * PACK * KEYS * 2),
         name="merge_first",
-    )(me, *a_parts, *b_parts)
-
-
-def merge_second_kernel(a_ref, b_ref, o_ref):
-    for half, ref in enumerate((a_ref, b_ref)):
-        outs, lses = merge([lambda a, b, k=k: ref[k, a:b, :] for k in range(4)])
-        base = half * PACK
+    )(*parts)
+
+
+def merge_second_kernel(p_ref, o_ref):
+    for base in (0, PACK):
+        outs, lses = merge([lambda a, b, k=k: p_ref[k, base + a : base + b, :] for k in range(4)])
         packed = pack_lse(lses, 128)
         for k in range(4):
             for h in range(HALF):
@@ -245,13 +237,13 @@
             o_ref[k, base + ROWS : base + PACK, :] = packed
 
 
-def merge_second(a_parts, b_parts):
+def merge_second(parts):
     return pl.pallas_call(
         merge_second_kernel,
         out_shape=jax.ShapeDtypeStruct((4, 2 * PACK, 128), BF16),
         cost_estimate=cost(8 * PACK * 128 * 2, 16 * PACK * 128 * 2),
         name="merge_second",
-    )(a_parts, b_parts)
+    )(parts)
 
 
 def merge_last_kernel(p_ref, o_ref):
@@ -291,7 +283,7 @@
                 pieces = []
                 for xs in (pair * 2, pair * 2 + 1):
                     for b in range(2):
-                        parts = [v_ref[xs, ys, pl.ds(kind * 2 + b, LAT_CH, 4), :] for kind in kinds]
+                        parts = [v_ref[ys * 4 + xs, pl.ds(kind * 2 + b, LAT_CH, 4), :] for kind in kinds]
                         pieces.append(jnp.concatenate(parts, axis=0))
                 stacked.append(jnp.concatenate(pieces, axis=1))
         high, low = split(jnp.concatenate(stacked, axis=0))
@@ -373,8 +365,6 @@
         base, edge_first, edge_last = latent_base(
             refresh, here, noise_level, plain, noisy_latent, velocity_cache
         )
-        up = lax.ppermute(edge_last, PATCH, [(p, p + 1) for p in range(PATCHES - 1)])
-        down = lax.ppermute(edge_first, PATCH, [(p + 1, p) for p in range(PATCHES - 1)])
 
     with jax.named_scope("keys_values"):
         refreshed = jnp.any(refresh == me)
@@ -385,47 +375,40 @@
         both = jnp.concatenate([high, gated - high], axis=0).astype(BF16)
 
     with jax.named_scope("queries"):
-        got, base, up, down, keys, value_rows, both = together((got, base, up, down, keys, value_rows, both))
-        held = exchange(select(refresh, got), "z")
+        got, base, keys, value_rows, both = together((got, base, keys, value_rows, both))
+        held = select(refresh, got)
+        held, edge_first, edge_last = together((held, edge_first, edge_last))
+        held = exchange(held, ("y", "z"))
 
     with jax.named_scope("keys_values"):
         mixed = lax.dot_general(both, out_weight, (((1,), (1,)), ((), ())), preferred_element_type=F32)
         values = project_values(value_rows, mixed[:VEC] + mixed[VEC:])
 
-    with jax.named_scope("queries"):
-        held, mixed = together((held, mixed))
-        held = held.reshape(SLOTS * 4 * CHUNK, HEADS_HERE * HEAD_DIM)
-        first, second = held[:, : HALF * HEAD_DIM], held[:, HALF * HEAD_DIM :]
-        qa = [shift(first, "y", k) for k in range(4)]
-        qb = [shift(second, "x", k) for k in range(4)]
-        qa, qb, values = together((qa, qb, values))
-        qa, qb = jnp.concatenate(qa, axis=0), jnp.concatenate(qb, axis=0)
+    with jax.named_scope("latent_base"):
+        up = lax.ppermute(edge_last, PATCH, [(p, p + 1) for p in range(PATCHES - 1)])
+        down = lax.ppermute(edge_first, PATCH, [(p + 1, p) for p in range(PATCHES - 1)])
 
     with jax.named_scope("attention"):
-        back_a, back_b = [None] * 4, [None] * 4
-        got_a, got_b = [qa] + [None] * 3, [qb] + [None] * 3
-        for k in (1, 3):
-            got_a[k], got_b[k] = shift(qa, "x", k), shift(qb, "y", k)
-        back_a[0], back_b[0] = attend(qa, qb, keys, values)
-        qa, qb, back_a[0], back_b[0] = together((qa, qb, back_a[0], back_b[0]))
-        got_a[2], got_b[2] = shift(qa, "x", 2), shift(qb, "y", 2)
+        held, values, up, down = together((held, values, up, down))
+        queries = held.reshape(16 * SLOTS * CHUNK, HEADS_HERE * HEAD_DIM)
+        got, back = [queries] + [None] * 3, [None] * 4
         for k in (1, 3, 2):
-            out_a, out_b = attend(got_a[k], got_b[k], keys, values)
-            back_a[k], back_b[k] = shift(out_a, "x", -k), shift(out_b, "y", -k)
+            got[k] = shift(queries, "x", k)
+        for k in (0, 1, 3, 2):
+            out = attend(got[k], keys, values)
+            back[k] = shift(out, "x", -k)
+            if k == 0:
+                got[1], _ = together((got[1], out))
             if k == 1:
-                got_a[3], got_b[3], _ = together((got_a[3], got_b[3], out_a))
+                got[3], _ = together((got[3], out))
             if k == 3:
-                got_a[2], got_b[2], back_a[1], back_b[1], _ = together(
-                    (got_a[2], got_b[2], back_a[1], back_b[1], out_a)
-                )
-        parts_a, parts_b = merge_first(here, back_a, back_b)
-        part = merge_second(exchange(parts_a, "y"), exchange(parts_b, "x"))
+                got[2], back[1], _ = together((got[2], back[1], out))
+        part = merge_second(exchange(merge_first(back), "y"))
         term = merge_last(exchange(part, "z"))
 
     with jax.named_scope("velocity"):
         term = jnp.sum(lax.all_gather(term, HEAD), axis=0)
-        term = exchange(spread_out(term), "y")
-        gathered = exchange(spread_out(term), "x")
+        gathered = exchange(spread_out(term, 16), ("y", "x"))
 
     with jax.named_scope("decode"):
         weight = conv_weight.transpose(1, 2, 3, 0)

time: 201 us -> 199 us (0.990)
  waiting for transfers between devices: 19.9 us -> 60.6 us
  starting transfers between devices: 50.2 us -> 29.3 us
  blocking collectives: 64.1 us -> 51.4 us
  local copies, waits for them, and re-layouts: 18.6 us -> 7.99 us
  other arithmetic: 4.46 us -> 6.91 us
    ppermute x18 -> x6, waiting for transfers between devices: 5.54 us -> 39.9 us  [shift(): return lax.ppermute(value, axis, [(i, (i + step) % 4) for i in range(4)])]
    ppermute x18 -> x6, starting transfers between devices: 26 us -> 5.25 us  [shift(): return lax.ppermute(value, axis, [(i, (i + step) % 4) for i in range(4)])]
    all_to_all x5 -> x3, blocking collectives: 58.5 us -> 45.8 us  [exchange(): return lax.all_to_all(value, axis, 0, 0)]
    unnamed x22 -> x18, local copies, waits for them, and re-layouts: 9.37 us -> 0.04 us
    slice x1, local copies, waits for them, and re-layouts: 2.22 us -> 5.67 us  [on_device(): value_rows = jnp.where(refreshed, fresh_qkv[:, 2], kv_cache[:, 1])]
    concatenate x2 -> x0, local copies, waits for them, and re-layouts: 3.08 us -> none  [on_device(): qa, qb = (jnp.concatenate(qa, axis=0), jnp.concatenate(qb, axis=0))]
    ppermute x1, waiting for transfers between devices: 1.54 us -> 4.34 us  [on_device(): lax.ppermute(edge_last, PATCH, [(p, p + 1) for p in range(PATCHES - 1)])]
    all_to_all x2, waiting for transfers between devices: 12.5 us -> 15.1 us  [exchange(): return lax.all_to_all(value, axis, 0, 0)]
  transfers between devices with their start and end apart: 22 -> 10, of which waited for: 7 -> 7; matrix products, arithmetic and copies ran while one was open for 9% -> 9% of each run, Pallas kernels for 12% -> 12%
where the time goes in v1:
time: 199 us; the launch traced here: 198 us
  waiting for transfers between devices  60.6 us (30%)
  blocking collectives  51.4 us (26%)
  Pallas kernels  35.1 us (18%)
  starting transfers between devices  29.3 us (15%)
  local copies, waits for them, and re-layouts  7.99 us (4%)
  other arithmetic  6.91 us (3%)
  matrix products  6 us (3%)
    all_to_all x3, blocking collectives, exchange(): return lax.all_to_all(value, axis, 0, 0)  45.8 us
    ppermute x6, waiting for transfers between devices, shift(): return lax.ppermute(value, axis, [(i, (i + step) % 4) for i in range(4)])  39.9 us
    pallas_call x4, Pallas kernels, attend(): pl.pallas_call(attend_kernel, out_shape=jax.ShapeDtypeStruct((2 * PACK, n...  19.4 us
    all_to_all x2, starting transfers between devices, exchange(): return lax.all_to_all(value, axis, 0, 0)  18.2 us
    all_to_all x2, waiting for transfers between devices, exchange(): return lax.all_to_all(value, axis, 0, 0)  15.1 us
    slice x1, local copies, waits for them, and re-layouts, on_device(): value_rows = jnp.where(refreshed, fresh_qkv[:, 2], kv_cache[:, 1])  5.67 us
    all_gather x1, blocking collectives, on_device(): term = jnp.sum(lax.all_gather(term, HEAD), axis=0)  5.62 us
    ppermute x6, starting transfers between devices, shift(): return lax.ppermute(value, axis, [(i, (i + step) % 4) for i in range(4)])  5.25 us
  transfers between devices with their start and end apart: 10, of which 7 were waited for; matrix products, arithmetic and copies ran while one was open for 9% of the time, Pallas kernels for 12%

profile of v1, /device:TPU:32, one launch (start us, length us, event | category | flops | bytes accessed | tf_op | source)
XLA Modules:
  0.0 198.1 jit_solution(9266853008156903172)
XLA Ops:
  0.0 2.2 %slice_bitcast_fusion = bf16[64,8,768]{2,1,0:T(8,128)(2,1)} fusion(bf16[512,3,768]{2,0,1:T(8,128)(2,1)} %param.13), kind=kLoop, calls=%fused_computation.10 | loop fusion | bytes 1572864 | tf_op jit(solution)/shard_map/queries/reshape;queries/squeeze | solution.py:356
  2.2 13.9 %all-to-all-start = ((bf16[64,8,768]{2,1,0:T(8,128)(2,1)}), bf16[64,8,768]{2,1,0:T(8,128)(2,1)}, u32[]{:S(2)}, u32[]{:S(2)}) async-start(bf16[64,8,768]{2,1,0:T(8,128)(2,1)} %slice_bitcast_fusion), calls=%async_computation | async-start | bytes 1572864 | tf_op jit(solution)/shard_map/queries/all_to_all | solution.py:42
  16.2 5.7 %fusion.3 = (bf16[512,1,768]{2,1,0:T(2,128)(2,1)}, bf16[512,1,768]{2,1,0:T(2,128)(2,1)}) fusion(bf16[512,2,768]{2,1,0:T(2,128)(2,1)} %param.14), kind=kLoop, calls=%fused_computation.13 | loop fusion | bytes 3145728 | tf_op jit(solution)/shard_map/keys_values/slice | solution.py:372
  26.8 4.5 %fusion.1 = (bf16[512,768]{1,0:T(8,128)(2,1)}, bf16[512,768]{1,0:T(8,128)(2,1)}) fusion(bf16[512,1,768]{2,1,0:T(2,128)(2,1)} %get-tuple-element.49, bf16[512,3,768]{2,0,1:T(8,128)(2,1)} %param.13, pred[]{:T(512)} %compare_reduce_fusion, bf16[512,1,768]{2,1,0:T(2,128)(2,1)} %get-tuple-element.50), kind=kLoop, calls=%fused_computation.6 | loop fusion | flops 786432 | bytes 4718593 | tf_op jit(solution)/shard_map/keys_values/jit(_where)/select_n | solution.py:372
  32.4 9.7 %all-to-all-done.got_ref = bf16[64,8,768]{2,1,0:T(8,128)(2,1)} async-done(((bf16[64,8,768]{2,1,0:T(8,128)(2,1)}), bf16[64,8,768]{2,1,0:T(8,128)(2,1)}, u32[]{:S(2)}, u32[]{:S(2)}) %all-to-all-start) | async-done | bytes 786464 | tf_op jit(solution)/shard_map/queries/all_to_all | solution.py:42
  44.2 4.3 %all-to-all-start.1 = ((bf16[16,32,768]{2,1,0:T(8,128)(2,1)}), bf16[16,32,768]{2,1,0:T(8,128)(2,1)}, u32[]{:S(2)}, u32[]{:S(2)}) async-start(bf16[16,32,768]{2,1,0:T(8,128)(2,1)} %select.1), calls=%async_computation.1 | async-start | bytes 1572864 | tf_op jit(solution)/shard_map/queries/all_to_all | solution.py:42
  48.5 4.6 %collective-permute-start = (f32[16,1024]{1,0:T(8,128)S(1)}, f32[16,1024]{1,0:T(8,128)S(1)}, u32[]{:S(2)}, u32[]{:S(2)}) collective-permute-start(f32[16,1024]{1,0:T(8,128)S(1)} %copy-done.8), channel_id=1, source_target_pairs={{0,4},{4,8},{8,12},{12,16},{16,20},{20,24},{24,28},{28,32},{32,36}... | collective-permute-start | bytes 196616 | tf_op jit(solution)/shard_map/latent_base/ppermute | solution.py:388
  54.4 4.3 %fusion.4 = f32[128,768]{1,0:T(8,128)S(1)} fusion(bf16[128,3072]{1,0:T(8,128)(2,1)} %pad_maximum_fusion, bf16[768,3072]{1,0:T(8,128)(2,1)} %param.17), kind=kOutput, calls=%fused_computation.14 | convolution fusion | flops 603979776 | bytes 5898240 | tf_op jit(solution)/shard_map/keys_values/dot_general | solution.py:384
  59.4 2.4 %values.1.v_ref = bf16[6,128,512]{2,1,0:T(8,128)(2,1)} custom-call(bf16[512,768]{1,0:T(8,128)(2,1)} %get-tuple-element.33.v_ref, f32[64,768]{1,0:T(8,128)} %slice_add_fusion.w_ref), custom_call_target="tpu_custom_call" | custom-call | flops 100663296 | bytes 1572864 | tf_op jit(solution)/shard_map/keys_values/values/pallas_call | solution.py:89
  61.8 4.3 %collective-permute-done.up_ref = f32[16,1024]{1,0:T(8,128)S(1)} collective-permute-done((f32[16,1024]{1,0:T(8,128)S(1)}, f32[16,1024]{1,0:T(8,128)S(1)}, u32[]{:S(2)}, u32[]{:S(2)}) %collective-permute-start) | collective-permute-done | bytes 65568 | tf_op jit(solution)/shard_map/latent_base/ppermute | solution.py:388
  67.4 5.4 %all-to-all-done.1 = bf16[16,32,768]{2,1,0:T(8,128)(2,1)} async-done(((bf16[16,32,768]{2,1,0:T(8,128)(2,1)}), bf16[16,32,768]{2,1,0:T(8,128)(2,1)}, u32[]{:S(2)}, u32[]{:S(2)}) %all-to-all-start.1) | async-done | bytes 786464 | tf_op jit(solution)/shard_map/queries/all_to_all | solution.py:42
  73.4 2.7 %collective-permute-start.5 = (bf16[512,768]{1,0:T(8,128)(2,1)}, bf16[512,768]{1,0:T(8,128)(2,1)}, u32[]{:S(2)}, u32[]{:S(2)}) collective-permute-start(bf16[512,768]{1,0:T(8,128)(2,1)} %bitcast.5.q_ref), channel_id=1, source_target_pairs={{0,48},{16,0},{32,16},{48,32},{1,49},{17,1},{33,17},{49,33},{2,50}... | collective-permute-start | bytes 2359304 | tf_op jit(solution)/shard_map/attention/ppermute | solution.py:34
  76.1 4.8 %attend.4.refs_0_ = bf16[416,512]{1,0:T(8,128)(2,1)} custom-call(bf16[512,768]{1,0:T(8,128)(2,1)} %bitcast.5.q_ref, bf16[512,768]{1,0:T(8,128)(2,1)} %get-tuple-element.38.k_ref, bf16[6,128,512]{2,1,0:T(8,128)(2,1)} %values.1.v_ref), custom_call_target="tpu_custom_call" | custom-call | flops 805306368 | bytes 3145728 | tf_op jit(solution)/shard_map/attention/attend/pallas_call | solution.py:180
  80.9 28.0 %collective-permute-done.3.q_ref = bf16[512,768]{1,0:T(8,128)(2,1)} collective-permute-done((bf16[512,768]{1,0:T(8,128)(2,1)}, bf16[512,768]{1,0:T(8,128)(2,1)}, u32[]{:S(2)}, u32[]{:S(2)}) %collective-permute-start.3) | collective-permute-done | bytes 786464 | tf_op jit(solution)/shard_map/attention/ppermute | solution.py:34
  108.9 4.9 %attend.5 = bf16[416,512]{1,0:T(8,128)(2,1)} custom-call(bf16[512,768]{1,0:T(8,128)(2,1)} %collective-permute-done.3.q_ref, bf16[512,768]{1,0:T(8,128)(2,1)} %get-tuple-element.38.k_ref, bf16[6,128,512]{2,1,0:T(8,128)(2,1)} %values.1.v_ref), custom_call_target="tpu_custom_call" | custom-call | flops 805306368 | bytes 3145728 | tf_op jit(solution)/shard_map/attention/attend/pallas_call | solution.py:180
  113.8 4.9 %attend.6 = bf16[416,512]{1,0:T(8,128)(2,1)} custom-call(bf16[512,768]{1,0:T(8,128)(2,1)} %collective-permute-done.5.q_ref, bf16[512,768]{1,0:T(8,128)(2,1)} %get-tuple-element.38.k_ref, bf16[6,128,512]{2,1,0:T(8,128)(2,1)} %values.1.v_ref), custom_call_target="tpu_custom_call" | custom-call | flops 805306368 | bytes 3145728 | tf_op jit(solution)/shard_map/attention/attend/pallas_call | solution.py:180
  122.2 4.8 %attend.7 = bf16[416,512]{1,0:T(8,128)(2,1)} custom-call(bf16[512,768]{1,0:T(8,128)(2,1)} %collective-permute-done.2.q_ref, bf16[512,768]{1,0:T(8,128)(2,1)} %get-tuple-element.38.k_ref, bf16[6,128,512]{2,1,0:T(8,128)(2,1)} %values.1.v_ref), custom_call_target="tpu_custom_call" | custom-call | flops 805306368 | bytes 3145728 | tf_op jit(solution)/shard_map/attention/attend/pallas_call | solution.py:180
  127.0 10.4 %collective-permute-done.7.refs_3_ = bf16[416,512]{1,0:T(8,128)(2,1)} collective-permute-done((bf16[416,512]{1,0:T(8,128)(2,1)}, bf16[416,512]{1,0:T(8,128)(2,1)}, u32[]{:S(2)}, u32[]{:S(2)}) %collective-permute-start.7) | collective-permute-done | bytes 426016 | tf_op jit(solution)/shard_map/attention/ppermute | solution.py:34
  137.4 2.7 %merge_first.1 = bf16[4,416,128]{2,1,0:T(8,128)(2,1)} custom-call(bf16[416,512]{1,0:T(8,128)(2,1)} %attend.4.refs_0_, bf16[416,512]{1,0:T(8,128)(2,1)} %collective-permute-done.4.refs_1_, bf16[416,512]{1,0:T(8,128)(2,1)} %collective-permute-done.6.refs_2_, bf16[416,512]{1,0:T(8,128)(2,1)} %collective-permute-done.7.refs_3_), custom_call_target="tpu_custom_call" | custom-call | flops 1703936 | bytes 2129920 | tf_op jit(solution)/shard_map/attention/merge_first/pallas_call | solution.py:222
  140.1 11.8 %all_to_all.25.p_ref = bf16[4,416,128]{2,1,0:T(8,128)(2,1)} all-to-all(bf16[4,416,128]{2,1,0:T(8,128)(2,1)} %merge_first.1), channel_id=1, replica_groups=mesh['y'=4,'x'=4,'z'=4,'w'=2,'c'=2] {'y'}, dimensions={0} | all-to-all | bytes 851968 | tf_op jit(solution)/shard_map/attention/all_to_all | solution.py:42
  153.7 18.3 %all_to_all.26.p_ref = bf16[4,416,128]{2,1,0:T(8,128)(2,1)} all-to-all(bf16[4,416,128]{2,1,0:T(8,128)(2,1)} %merge_second.1), channel_id=1, replica_groups=mesh['y'=4,'x'=4,'z'=4,'w'=2,'c'=2] {'z'}, dimensions={0} | all-to-all | bytes 851968 | tf_op jit(solution)/shard_map/attention/all_to_all | solution.py:42
  173.7 5.6 %all-gather = f32[256,128]{1,0:T(8,128)S(1)} all-gather(f32[64,128]{1,0:T(8,128)} %merge_last.1), channel_id=2, replica_groups=mesh['y'=4,'x'=4,'z'=4,'w'=2,'c'=2] {'w','c'}, dimensions={0}, use_global_device_ids=true | all-gather | bytes 163840 | tf_op jit(solution)/shard_map/velocity/all_gather | solution.py:410
  179.4 15.8 %all_to_all.27.v_ref = f32[16,64,128]{2,1,0:T(8,128)} all-to-all(f32[16,64,128]{2,1,0:T(8,128)S(1)} %broadcast_in_dim.2), channel_id=1, replica_groups=mesh['y'=4,'x'=4,'z'=4,'w'=2,'c'=2] {'y','x'}, dimensions={0} | all-to-all | bytes 1048576 | tf_op jit(solution)/shard_map/velocity/all_to_all | solution.py:42
  195.2 2.9 %decode.1 = bf16[2,128,1024]{2,1,0:T(8,128)(2,1)} custom-call(s32[4]{0:T(128)} %refresh_ref.5, s32[1]{0:T(128)} %bitcast.me_ref, f32[1]{0:T(128)S(6)} %copy.24.level_ref, f32[16,64,128]{2,1,0:T(8,128)} %all_to_all.27.v_ref, f32[32,1024]{1,0:T(8,128)} %get-tuple-element.44.base_ref, f32[16,1024]{1,0:T(8,128)} %copy-done.2, f32[16,1024]{1,0:T(8,128)} %copy-done.3, ...), custom_call_target="tpu_custom_call" | custom-call | flops 83886080 | bytes 2097152 | tf_op jit(solution)/shard_map/decode/decode/pallas_call | solution.py:326
  (40 shorter events, 18.6 us)
Async XLA Ops:
  0.0 21.8 %copy-start = (bf16[512,3072]{1,0:T(8,128)(2,1)S(1)}, bf16[512,3072]{1,0:T(8,128)(2,1)}, u32[]{:S(2)}) copy-start(bf16[512,3072]{1,0:T(8,128)(2,1)} %param.15) | copy-start | bytes 9437188
  2.2 39.9 %all-to-all-start = ((bf16[64,8,768]{2,1,0:T(8,128)(2,1)}), bf16[64,8,768]{2,1,0:T(8,128)(2,1)}, u32[]{:S(2)}, u32[]{:S(2)}) async-start(bf16[64,8,768]{2,1,0:T(8,128)(2,1)} %slice_bitcast_fusion), calls=%async_computation | async-start | bytes 1572864 | tf_op jit(solution)/shard_map/queries/all_to_all | solution.py:42
  16.1 5.7 %copy-start.1 = (bf16[3072,64]{0,1:T(8,128)(2,1)S(1)}, bf16[3072,64]{0,1:T(8,128)(2,1)}, u32[]{:S(2)}) copy-start(bf16[3072,64]{0,1:T(8,128)(2,1)} %param.18) | copy-start | bytes 1179652
  16.2 5.7 %copy-start.6 = (f32[64]{0:T(128)S(1)}, f32[64]{0:T(128)}, u32[]{:S(2)}) copy-start(f32[64]{0:T(128)} %param.19) | copy-start | bytes 772
  21.9 4.3 %copy-start.5 = (s32[4]{0:T(128)S(1)}, s32[4]{0:T(128)}, u32[]{:S(2)}) copy-start(s32[4]{0:T(128)} %refresh_ref.5) | copy-start | bytes 52
  26.8 4.5 %copy-start.4 = (f32[3072]{0:T(1024)S(1)}, f32[3072]{0:T(1024)}, u32[]{:S(2)}) copy-start(f32[3072]{0:T(1024)} %param.20) | copy-start | bytes 36868
  31.4 17.1 %copy-start.8 = (f32[16,1024]{1,0:T(8,128)S(1)}, f32[16,1024]{1,0:T(8,128)}, u32[]{:S(2)}) copy-start(f32[16,1024]{1,0:T(8,128)} %get-tuple-element.35) | copy-start | bytes 196612
  31.4 21.7 %copy-start.7 = (f32[16,1024]{1,0:T(8,128)S(1)}, f32[16,1024]{1,0:T(8,128)}, u32[]{:S(2)}) copy-start(f32[16,1024]{1,0:T(8,128)} %get-tuple-element.36) | copy-start | bytes 196612
  44.2 28.6 %all-to-all-start.1 = ((bf16[16,32,768]{2,1,0:T(8,128)(2,1)}), bf16[16,32,768]{2,1,0:T(8,128)(2,1)}, u32[]{:S(2)}, u32[]{:S(2)}) async-start(bf16[16,32,768]{2,1,0:T(8,128)(2,1)} %select.1), calls=%async_computation.1 | async-start | bytes 1572864 | tf_op jit(solution)/shard_map/queries/all_to_all | solution.py:42
  48.5 17.6 %collective-permute-start = (f32[16,1024]{1,0:T(8,128)S(1)}, f32[16,1024]{1,0:T(8,128)S(1)}, u32[]{:S(2)}, u32[]{:S(2)}) collective-permute-start(f32[16,1024]{1,0:T(8,128)S(1)} %copy-done.8), channel_id=1, source_target_pairs={{0,4},{4,8},{8,12},{12,16},{16,20},{20,24},{24,28},{28,32},{32,36}... | collective-permute-start | bytes 196616 | tf_op jit(solution)/shard_map/latent_base/ppermute | solution.py:388
  53.1 14.3 %collective-permute-start.1 = (f32[16,1024]{1,0:T(8,128)S(1)}, f32[16,1024]{1,0:T(8,128)S(1)}, u32[]{:S(2)}, u32[]{:S(2)}) collective-permute-start(f32[16,1024]{1,0:T(8,128)S(1)} %copy-done.7), channel_id=1, source_target_pairs={{4,0},{8,4},{12,8},{16,12},{20,16},{24,20},{28,24},{32,28},{36,32}... | collective-permute-start | bytes 196616 | tf_op jit(solution)/shard_map/latent_base/ppermute | solution.py:389
  66.2 47.6 %copy-start.2 = (f32[16,1024]{1,0:T(8,128)}, f32[16,1024]{1,0:T(8,128)S(1)}, u32[]{:S(2)}) copy-start(f32[16,1024]{1,0:T(8,128)S(1)} %collective-permute-done.up_ref) | copy-start | bytes 196612
  67.4 46.3 %copy-start.3 = (f32[16,1024]{1,0:T(8,128)}, f32[16,1024]{1,0:T(8,128)S(1)}, u32[]{:S(2)}) copy-start(f32[16,1024]{1,0:T(8,128)S(1)} %collective-permute-done.1.down_ref) | copy-start | bytes 196612
  72.8 36.0 %collective-permute-start.3 = (bf16[512,768]{1,0:T(8,128)(2,1)}, bf16[512,768]{1,0:T(8,128)(2,1)}, u32[]{:S(2)}, u32[]{:S(2)}) collective-permute-start(bf16[512,768]{1,0:T(8,128)(2,1)} %bitcast.5.q_ref), channel_id=1, source_target_pairs={{0,16},{16,32},{32,48},{48,0},{1,17},{17,33},{33,49},{49,1},{2,18}... | collective-permute-start | bytes 2359304 | tf_op jit(solution)/shard_map/attention/ppermute | solution.py:34
  73.4 40.3 %collective-permute-start.5 = (bf16[512,768]{1,0:T(8,128)(2,1)}, bf16[512,768]{1,0:T(8,128)(2,1)}, u32[]{:S(2)}, u32[]{:S(2)}) collective-permute-start(bf16[512,768]{1,0:T(8,128)(2,1)} %bitcast.5.q_ref), channel_id=1, source_target_pairs={{0,48},{16,0},{32,16},{48,32},{1,49},{17,1},{33,17},{49,33},{2,50}... | collective-permute-start | bytes 2359304 | tf_op jit(solution)/shard_map/attention/ppermute | solution.py:34
  76.1 44.5 %collective-permute-start.2 = (bf16[512,768]{1,0:T(8,128)(2,1)}, bf16[512,768]{1,0:T(8,128)(2,1)}, u32[]{:S(2)}, u32[]{:S(2)}) collective-permute-start(bf16[512,768]{1,0:T(8,128)(2,1)} %bitcast.5.q_ref), channel_id=1, source_target_pairs={{0,32},{16,48},{32,0},{48,16},{1,33},{17,49},{33,1},{49,17},{2,34}... | collective-permute-start | bytes 2359304 | tf_op jit(solution)/shard_map/attention/ppermute | solution.py:34
  113.7 8.4 %collective-permute-start.4 = (bf16[416,512]{1,0:T(8,128)(2,1)}, bf16[416,512]{1,0:T(8,128)(2,1)}, u32[]{:S(2)}, u32[]{:S(2)}) collective-permute-start(bf16[416,512]{1,0:T(8,128)(2,1)} %attend.5), channel_id=1, source_target_pairs={{0,48},{16,0},{32,16},{48,32},{1,49},{17,1},{33,17},{49,33},{2,50}... | collective-permute-start | bytes 1277960 | tf_op jit(solution)/shard_map/attention/ppermute | solution.py:34
  118.6 18.8 %collective-permute-start.7 = (bf16[416,512]{1,0:T(8,128)(2,1)}, bf16[416,512]{1,0:T(8,128)(2,1)}, u32[]{:S(2)}, u32[]{:S(2)}) collective-permute-start(bf16[416,512]{1,0:T(8,128)(2,1)} %attend.6), channel_id=1, source_target_pairs={{0,16},{16,32},{32,48},{48,0},{1,17},{17,33},{33,49},{49,1},{2,18}... | collective-permute-start | bytes 1277960 | tf_op jit(solution)/shard_map/attention/ppermute | solution.py:34
  127.0 10.4 %collective-permute-start.6 = (bf16[416,512]{1,0:T(8,128)(2,1)}, bf16[416,512]{1,0:T(8,128)(2,1)}, u32[]{:S(2)}, u32[]{:S(2)}) collective-permute-start(bf16[416,512]{1,0:T(8,128)(2,1)} %attend.7), channel_id=1, source_target_pairs={{0,32},{16,48},{32,0},{48,16},{1,33},{17,49},{33,1},{49,17},{2,34}... | collective-permute-start | bytes 1277960 | tf_op jit(solution)/shard_map/attention/ppermute | solution.py:34

commit v2 on v1

--- a/solution.py
+++ b/solution.py
@@ -23,15 +23,16 @@
 CHUNK = 8
 F32 = jnp.float32
 BF16 = jnp.bfloat16
-PATCH = ("y", "x", "z")
+PATCH = ("yh", "yl", "xh", "xl", "z")
 HEAD = ("w", "c")
-BITS = {"y": 4, "x": 2, "z": 0}
-
-
-def shift(value, axis, step):
-    if step == 0:
-        return value
-    return lax.ppermute(value, axis, [(i, (i + step) % 4) for i in range(4)])
+
+
+def mirror(value, flip_y, flip_x):
+    pairs = []
+    for p in range(PATCHES):
+        y, x, z = p // 16, (p // 4) % 4, p % 4
+        pairs.append((p, (3 - y if flip_y else y) * 16 + (3 - x if flip_x else x) * 4 + z))
+    return lax.ppermute(value, PATCH, pairs)
 
 
 def spread_out(value, count):
@@ -80,15 +81,13 @@
         both = lax.dot_general(
             left, v_ref[:, cols], (((1,), (1,)), ((), ())), preferred_element_type=F32
         )
-        high, low = split(both[:VEC] + both[VEC:])
-        o_ref[h, :VEC, :] = high
-        o_ref[h, VEC:, :] = low
+        o_ref[h * VEC : (h + 1) * VEC, :] = (both[:VEC] + both[VEC:]).astype(BF16)
 
 
 def project_values(value_rows, mixed):
     return pl.pallas_call(
         values_kernel,
-        out_shape=jax.ShapeDtypeStruct((HEADS_HERE, 2 * VEC, KEYS), BF16),
+        out_shape=jax.ShapeDtypeStruct((HEADS_HERE * VEC, KEYS), BF16),
         cost_estimate=cost(4 * KEYS * VEC * HEAD_DIM * HEADS_HERE, 4 * KEYS * 768),
         name="values",
     )(value_rows, mixed)
@@ -149,42 +148,71 @@
     return block.astype(BF16)
 
 
-def attend_kernel(q_ref, k_ref, v_ref, o_ref):
+def attend_kernel(first, last, *refs):
+    q_ref, v_ref, state_in, outs = refs[0], refs[1], None, refs[2:]
+    if not first:
+        state_in, outs = outs[:3], outs[3:]
+    k_refs, outs = outs[: 2 if last else 1], outs[2 if last else 1 :]
     scale = math.log2(math.e) / math.sqrt(HEAD_DIM)
 
     def scores(head):
         cols = slice(head * HEAD_DIM, (head + 1) * HEAD_DIM)
+        keys = [k[:, cols] for k in k_refs]
+        keys = keys[0] if len(keys) == 1 else jnp.concatenate(keys, axis=0)
         return lax.dot_general(
-            k_ref[:, cols], q_ref[:, cols], (((1,), (1,)), ((), ())), preferred_element_type=F32
+            keys, q_ref[:, cols], (((1,), (1,)), ((), ())), preferred_element_type=F32
         )
 
     dots, lses = scores(0), []
     for head in range(HEADS_HERE):
         half, h = divmod(head, HALF)
         following = scores(head + 1) if head + 1 < HEADS_HERE else None
+        rows = slice(head * VEC, (head + 1) * VEC)
         top = jnp.max(dots, axis=0, keepdims=True)
+        if not first:
+            old_top = state_in[1][head : head + 1, :]
+            top = jnp.maximum(top, old_top)
         exps = jnp.exp2((dots - top) * scale)
         total = jnp.sum(exps, axis=0, keepdims=True)
-        parts = jnp.dot(v_ref[head], exps.astype(BF16), preferred_element_type=F32)
-        row = half * PACK + h * VEC
-        o_ref[row : row + VEC, :] = ((parts[:VEC] + parts[VEC:]) * (1.0 / total)).astype(BF16)
-        lses.append(top * (1.0 / math.sqrt(HEAD_DIM)) + jnp.log(total))
-        if h == HALF - 1:
-            o_ref[half * PACK + ROWS : (half + 1) * PACK, :] = pack_lse(lses, o_ref.shape[1])
-            lses = []
+        acc = jnp.dot(v_ref[rows, :], exps.astype(BF16), preferred_element_type=F32)
+        if not first:
+            shrink = jnp.exp2((old_top - top) * scale)
+            total = total + state_in[2][head : head + 1, :] * shrink
+            acc = acc + state_in[0][rows, :] * shrink
+        if not last:
+            outs[0][rows, :] = acc
+            outs[1][head : head + 1, :] = top
+            outs[2][head : head + 1, :] = total
+        else:
+            out = (acc * (1.0 / total)).astype(BF16)
+            row = half * PACK + h * VEC
+            for k in range(4):
+                outs[0][k, row : row + VEC, :] = out[:, k * 128 : (k + 1) * 128]
+            lses.append(top * (1.0 / math.sqrt(HEAD_DIM)) + jnp.log(total))
+            if h == HALF - 1:
+                packed = pack_lse(lses, out.shape[1])
+                for k in range(4):
+                    outs[0][k, half * PACK + ROWS : (half + 1) * PACK, :] = packed[:, k * 128 : (k + 1) * 128]
+                lses = []
         dots = following
 
 
-def attend(queries, keys, values):
+def attend(queries, values, state, keys):
     n = queries.shape[0]
-    return pl.pallas_call(
-        attend_kernel,
-        out_shape=jax.ShapeDtypeStruct((2 * PACK, n), BF16),
+    first, last = state is None, len(keys) == 2
+    if last:
+        out = jax.ShapeDtypeStruct((4, 2 * PACK, n // 4), BF16)
+    else:
+        rows = jax.ShapeDtypeStruct((8, n), F32)
+        out = (jax.ShapeDtypeStruct((2 * ROWS, n), F32), rows, rows)
+    return pl.pallas_call(
+        functools.partial(attend_kernel, first, last),
+        out_shape=out,
         cost_estimate=cost(
             4 * n * KEYS * HEAD_DIM * HEADS_HERE, 4 * n * 768 + 4 * KEYS * 768, n * KEYS * HEADS_HERE
         ),
         name="attend",
-    )(queries, keys, values)
+    )(queries, values, *(() if first else state), *keys)
 
 
 def merge(parts_of):
@@ -204,27 +232,6 @@
         outs.append(acc)
         lses.append(top + jnp.log(total))
     return outs, lses
-
-
-def merge_first_kernel(*refs):
-    o_ref = refs[4]
-    for base in (0, PACK):
-        outs, lses = merge([lambda a, b, r=r: r[base + a : base + b, :] for r in refs[:4]])
-        packed = pack_lse(lses, KEYS)
-        for k in range(4):
-            cols = slice(k * 128, (k + 1) * 128)
-            for h in range(HALF):
-                o_ref[k, base + h * VEC : base + (h + 1) * VEC, :] = outs[h][:, cols].astype(BF16)
-            o_ref[k, base + ROWS : base + PACK, :] = packed[:, cols]
-
-
-def merge_first(parts):
-    return pl.pallas_call(
-        merge_first_kernel,
-        out_shape=jax.ShapeDtypeStruct((4, 2 * PACK, 128), BF16),
-        cost_estimate=cost(8 * PACK * KEYS * 2, 10 * PACK * KEYS * 2),
-        name="merge_first",
-    )(*parts)
 
 
 def merge_second_kernel(p_ref, o_ref):
@@ -357,58 +364,56 @@
         own, fresh_qkv = together((own, fresh_qkv))
         got = exchange(own, PATCH)
 
-    with jax.named_scope("latent_base"):
-        plain = lax.dot_general(
-            final_weight, hidden, (((0,), (1,)), ((), ())), preferred_element_type=F32
-        )
-        plain = plain + final_bias[:, None]
-        base, edge_first, edge_last = latent_base(
-            refresh, here, noise_level, plain, noisy_latent, velocity_cache
-        )
-
     with jax.named_scope("keys_values"):
         refreshed = jnp.any(refresh == me)
         keys = jnp.where(refreshed, fresh_qkv[:, 1], kv_cache[:, 0])
         value_rows = jnp.where(refreshed, fresh_qkv[:, 2], kv_cache[:, 1])
+        keys_x, keys_y = mirror(keys, 0, 1), mirror(keys, 1, 0)
+
+    with jax.named_scope("latent_base"):
+        plain = lax.dot_general(
+            final_weight, hidden, (((0,), (1,)), ((), ())), preferred_element_type=F32
+        )
+        plain = plain + final_bias[:, None]
+        base, edge_first, edge_last = latent_base(
+            refresh, here, noise_level, plain, noisy_latent, velocity_cache
+        )
+        up = lax.ppermute(edge_last, PATCH, [(p, p + 1) for p in range(PATCHES - 1)])
+        down = lax.ppermute(edge_first, PATCH, [(p + 1, p) for p in range(PATCHES - 1)])
+
+    with jax.named_scope("queries"):
+        got, base, up, down, keys_x, keys_y = together((got, base, up, down, keys_x, keys_y))
+        held = exchange(select(refresh, got), ("yl", "xl", "z"))
+
+    with jax.named_scope("keys_values"):
         gated = final_weight.T.astype(F32) * gate_scale[None, :]
         high = lax.reduce_precision(gated, 8, 7)
         both = jnp.concatenate([high, gated - high], axis=0).astype(BF16)
-
-    with jax.named_scope("queries"):
-        got, base, keys, value_rows, both = together((got, base, keys, value_rows, both))
-        held = select(refresh, got)
-        held, edge_first, edge_last = together((held, edge_first, edge_last))
-        held = exchange(held, ("y", "z"))
-
-    with jax.named_scope("keys_values"):
         mixed = lax.dot_general(both, out_weight, (((1,), (1,)), ((), ())), preferred_element_type=F32)
         values = project_values(value_rows, mixed[:VEC] + mixed[VEC:])
-
-    with jax.named_scope("latent_base"):
-        up = lax.ppermute(edge_last, PATCH, [(p, p + 1) for p in range(PATCHES - 1)])
-        down = lax.ppermute(edge_first, PATCH, [(p + 1, p) for p in range(PATCHES - 1)])
+        half = KEYS // 2
+        keys_far = mirror(keys_x[:half], 1, 0), mirror(keys_y[half:], 0, 1)
+        blocks = [
+            (values, (keys,)),
+            (mirror(values, 0, 1), (keys_x,)),
+            (mirror(values, 1, 0), (keys_y,)),
+            (mirror(values, 1, 1), keys_far),
+        ]
 
     with jax.named_scope("attention"):
-        held, values, up, down = together((held, values, up, down))
+        held, values = together((held, values))
         queries = held.reshape(16 * SLOTS * CHUNK, HEADS_HERE * HEAD_DIM)
-        got, back = [queries] + [None] * 3, [None] * 4
-        for k in (1, 3, 2):
-            got[k] = shift(queries, "x", k)
-        for k in (0, 1, 3, 2):
-            out = attend(got[k], keys, values)
-            back[k] = shift(out, "x", -k)
-            if k == 0:
-                got[1], _ = together((got[1], out))
-            if k == 1:
-                got[3], _ = together((got[3], out))
-            if k == 3:
-                got[2], back[1], _ = together((got[2], back[1], out))
-        part = merge_second(exchange(merge_first(back), "y"))
+        state = None
+        for k, (values, keys) in enumerate(blocks):
+            if k:
+                values, keys, state = together((values, keys, state))
+            state = attend(queries, values, state, keys)
+        part = merge_second(exchange(state, ("yl", "xl")))
         term = merge_last(exchange(part, "z"))
 
     with jax.named_scope("velocity"):
         term = jnp.sum(lax.all_gather(term, HEAD), axis=0)
-        gathered = exchange(spread_out(term, 16), ("y", "x"))
+        gathered = exchange(spread_out(term, 16), ("yh", "yl", "xh", "xl"))
 
     with jax.named_scope("decode"):
         weight = conv_weight.transpose(1, 2, 3, 0)
@@ -418,7 +423,7 @@
 
 
 def solution(mesh):
-    wide = Mesh(mesh.devices.reshape(4, 4, 4, 2, 2), PATCH + HEAD)
+    wide = Mesh(mesh.devices.reshape(2, 2, 2, 2, 4, 2, 2), PATCH + HEAD)
     return jax.shard_map(
         on_device,
         mesh=wide,

time: 199 us -> 161 us (0.81)
  waiting for transfers between devices: 60.6 us -> 11.2 us
  starting transfers between devices: 29.3 us -> 42 us
  other arithmetic: 6.91 us -> 3.56 us
  local copies, waits for them, and re-layouts: 7.99 us -> 10.8 us
  Pallas kernels: 35.1 us -> 32.8 us
    ppermute x6 -> x7, waiting for transfers between devices: 39.9 us -> 4.5 us  [mirror(): return lax.ppermute(value, PATCH, pairs)]
    all_to_all x2, waiting for transfers between devices: 15.1 us -> 0.01 us  [exchange(): return lax.all_to_all(value, axis, 0, 0)]
    ppermute x6 -> x7, starting transfers between devices: 5.25 us -> 16.4 us  [mirror(): return lax.ppermute(value, PATCH, pairs)]
    ppermute x1, waiting for transfers between devices: 1.24 us -> 6.4 us  [on_device(): lax.ppermute(edge_first, PATCH, [(p + 1, p) for p in range(PATCHES - 1)])]
    ppermute x1, waiting for transfers between devices: 4.34 us -> 0.31 us  [on_device(): lax.ppermute(edge_last, PATCH, [(p, p + 1) for p in range(PATCHES - 1)])]
    slice x0 -> x2, local copies, waits for them, and re-layouts: none -> 3.57 us  [on_device(): keys_far = (mirror(keys_x[:half], 1, 0), mirror(keys_y[half:], 0, 1))]
    select_n x1, other arithmetic: 4.47 us -> 2.08 us  [on_device(): value_rows = jnp.where(refreshed, fresh_qkv[:, 2], kv_cache[:, 1])]
    pallas_call x6 -> x5, Pallas kernels: 24.5 us -> 22.2 us  [the longest x4 19.9 us: attend(): pl.pallas_call(functools.partial(attend_kernel, first, last), out_shape=o...]
  transfers between devices with their start and end apart: 10 -> 11, of which waited for: 7 -> 5; matrix products, arithmetic and copies ran while one was open for 9% -> 11% of each run, Pallas kernels for 12% -> 12%
where the time goes in v2:
time: 161 us; the launch traced here: 159 us
  blocking collectives  51.9 us (32%)
  starting transfers between devices  42 us (26%)
  Pallas kernels  32.8 us (20%)
  waiting for transfers between devices  11.2 us (7%)
  local copies, waits for them, and re-layouts  10.8 us (7%)
  matrix products  5.75 us (4%)
  other arithmetic  3.56 us (2%)
    all_to_all x3, blocking collectives, exchange(): return lax.all_to_all(value, axis, 0, 0)  46.2 us
    pallas_call x4, Pallas kernels, attend(): pl.pallas_call(functools.partial(attend_kernel, first, last), out_shape=o...  19.9 us
    all_to_all x2, starting transfers between devices, exchange(): return lax.all_to_all(value, axis, 0, 0)  19.5 us
    ppermute x7, starting transfers between devices, mirror(): return lax.ppermute(value, PATCH, pairs)  16.4 us
    ppermute x1, waiting for transfers between devices, on_device(): lax.ppermute(edge_first, PATCH, [(p + 1, p) for p in range(PATCHES - 1)])  6.4 us
    all_gather x1, blocking collectives, on_device(): term = jnp.sum(lax.all_gather(term, HEAD), axis=0)  5.62 us
    ppermute x1, starting transfers between devices, on_device(): lax.ppermute(edge_last, PATCH, [(p, p + 1) for p in range(PATCHES - 1)])  4.88 us
    ppermute x7, waiting for transfers between devices, mirror(): return lax.ppermute(value, PATCH, pairs)  4.5 us
  transfers between devices with their start and end apart: 11, of which 5 were waited for; matrix products, arithmetic and copies ran while one was open for 11% of the time, Pallas kernels for 12%

profile of v2, /device:TPU:32, one launch (start us, length us, event | category | flops | bytes accessed | tf_op | source)
XLA Modules:
  0.0 158.8 jit_solution(1925261142360173997)
XLA Ops:
  0.0 2.2 %slice_bitcast_fusion = bf16[64,8,768]{2,1,0:T(8,128)(2,1)} fusion(bf16[512,3,768]{2,0,1:T(8,128)(2,1)} %param.13), kind=kLoop, calls=%fused_computation.13 | loop fusion | bytes 1572864 | tf_op jit(solution)/shard_map/queries/reshape;queries/squeeze | solution.py:363
  2.2 13.9 %all-to-all-start = ((bf16[64,8,768]{2,1,0:T(8,128)(2,1)}), bf16[64,8,768]{2,1,0:T(8,128)(2,1)}, u32[]{:S(2)}, u32[]{:S(2)}) async-start(bf16[64,8,768]{2,1,0:T(8,128)(2,1)} %slice_bitcast_fusion), calls=%async_computation | async-start | bytes 1572864 | tf_op jit(solution)/shard_map/queries/all_to_all | solution.py:43
  16.8 4.4 %fusion.8 = (bf16[512,1,768]{2,1,0:T(2,128)(2,1)S(1)}, bf16[512,1,768]{2,1,0:T(2,128)(2,1)S(1)}) fusion(bf16[512,2,768]{2,1,0:T(2,128)(2,1)} %param.14), kind=kLoop, calls=%fused_computation.17 | loop fusion | bytes 3145728 | tf_op jit(solution)/shard_map/keys_values/slice | solution.py:370
  23.3 2.7 %collective-permute-start.2 = (bf16[512,768]{1,0:T(8,128)(2,1)}, bf16[512,768]{1,0:T(8,128)(2,1)}, u32[]{:S(2)}, u32[]{:S(2)}) collective-permute-start(bf16[512,768]{1,0:T(8,128)(2,1)} %get-tuple-element.80.refs_2_), channel_id=1, source_target_pairs={{0,48},{4,52},{8,56},{12,60},{16,32},{20,36},{24,40},{28,44},{32,1... | collective-permute-start | bytes 2359304 | tf_op jit(solution)/shard_map/keys_values/ppermute | solution.py:35
  26.1 3.0 %collective-permute-start.3 = (bf16[512,768]{1,0:T(8,128)(2,1)}, bf16[512,768]{1,0:T(8,128)(2,1)}, u32[]{:S(2)}, u32[]{:S(2)}) collective-permute-start(bf16[512,768]{1,0:T(8,128)(2,1)} %get-tuple-element.80.refs_2_), channel_id=1, source_target_pairs={{0,192},{4,196},{8,200},{12,204},{16,208},{20,212},{24,216},{28,22... | collective-permute-start | bytes 2359304 | tf_op jit(solution)/shard_map/keys_values/ppermute | solution.py:35
  33.3 4.9 %collective-permute-start = (f32[16,1024]{1,0:T(8,128)}, f32[16,1024]{1,0:T(8,128)}, u32[]{:S(2)}, u32[]{:S(2)}) collective-permute-start(f32[16,1024]{1,0:T(8,128)} %get-tuple-element.44), channel_id=1, source_target_pairs={{0,4},{4,8},{8,12},{12,16},{16,20},{20,24},{24,28},{28,32},{32,36}... | collective-permute-start | bytes 196616 | tf_op jit(solution)/shard_map/latent_base/ppermute | solution.py:381
  39.8 6.4 %collective-permute-done.1.down_ref = f32[16,1024]{1,0:T(8,128)} collective-permute-done((f32[16,1024]{1,0:T(8,128)}, f32[16,1024]{1,0:T(8,128)}, u32[]{:S(2)}, u32[]{:S(2)}) %collective-permute-start.1) | collective-permute-done | bytes 65568 | tf_op jit(solution)/shard_map/latent_base/ppermute | solution.py:382
  46.2 3.5 %collective-permute-done.2.refs_5_ = bf16[512,768]{1,0:T(8,128)(2,1)} collective-permute-done((bf16[512,768]{1,0:T(8,128)(2,1)}, bf16[512,768]{1,0:T(8,128)(2,1)}, u32[]{:S(2)}, u32[]{:S(2)}) %collective-permute-start.2) | collective-permute-done | bytes 786464 | tf_op jit(solution)/shard_map/keys_values/ppermute | solution.py:35
  50.5 2.1 %select.1 = bf16[16,32,768]{2,1,0:T(8,128)(2,1)} custom-call(s32[4]{0:T(128)} %refresh_ref.5, bf16[64,8,768]{2,1,0:T(8,128)(2,1)} %all-to-all-done.got_ref), custom_call_target="tpu_custom_call" | custom-call | bytes 835584 | tf_op jit(solution)/shard_map/queries/select/pallas_call | solution.py:68
  52.6 5.6 %all-to-all-start.1 = ((bf16[16,32,768]{2,1,0:T(8,128)(2,1)}), bf16[16,32,768]{2,1,0:T(8,128)(2,1)}, u32[]{:S(2)}, u32[]{:S(2)}) async-start(bf16[16,32,768]{2,1,0:T(8,128)(2,1)} %select.1), calls=%async_computation.1 | async-start | bytes 1572864 | tf_op jit(solution)/shard_map/queries/all_to_all | solution.py:43
  58.4 4.0 %fusion.1 = f32[128,768]{1,0:T(8,128)S(1)} fusion(bf16[768,3072]{1,0:T(8,128)(2,1)} %param.17, bf16[64,3072]{1,0:T(8,128)(2,1)S(1)} %get-tuple-element.84, bf16[64,3072]{1,0:T(8,128)(2,1)S(1)} %get-tuple-element.83), kind=kOutput, calls=%fused_computation.4 | convolution fusion | flops 605552640 | bytes 5898240 | tf_op jit(solution)/shard_map/keys_values/dot_general | solution.py:392
  63.1 2.3 %values.1.refs_1_ = bf16[384,512]{1,0:T(8,128)(2,1)} custom-call(bf16[512,768]{1,0:T(8,128)(2,1)} %get-tuple-element.79.v_ref, f32[64,768]{1,0:T(8,128)} %slice_add_fusion.w_ref), custom_call_target="tpu_custom_call" | custom-call | flops 100663296 | bytes 1572864 | tf_op jit(solution)/shard_map/keys_values/values/pallas_call | solution.py:88
  65.4 2.3 %collective-permute-start.8 = (bf16[384,512]{1,0:T(8,128)(2,1)}, bf16[384,512]{1,0:T(8,128)(2,1)}, u32[]{:S(2)}, u32[]{:S(2)}) collective-permute-start(bf16[384,512]{1,0:T(8,128)(2,1)} %values.1.refs_1_), channel_id=1, source_target_pairs={{0,48},{4,52},{8,56},{12,60},{16,32},{20,36},{24,40},{28,44},{32,1... | collective-permute-start | bytes 1179656 | tf_op jit(solution)/shard_map/keys_values/ppermute | solution.py:35
  67.7 2.5 %collective-permute-start.7 = (bf16[384,512]{1,0:T(8,128)(2,1)}, bf16[384,512]{1,0:T(8,128)(2,1)}, u32[]{:S(2)}, u32[]{:S(2)}) collective-permute-start(bf16[384,512]{1,0:T(8,128)(2,1)} %values.1.refs_1_), channel_id=1, source_target_pairs={{0,192},{4,196},{8,200},{12,204},{16,208},{20,212},{24,216},{28,22... | collective-permute-start | bytes 1179656 | tf_op jit(solution)/shard_map/keys_values/ppermute | solution.py:35
  73.0 3.0 %collective-permute-start.5 = (bf16[256,768]{1,0:T(8,128)(2,1)}, bf16[256,768]{1,0:T(8,128)(2,1)}, u32[]{:S(2)}, u32[]{:S(2)}) collective-permute-start(bf16[256,768]{1,0:T(8,128)(2,1)} %slice.34), channel_id=1, source_target_pairs={{0,192},{4,196},{8,200},{12,204},{16,208},{20,212},{24,216},{28,22... | collective-permute-start | bytes 1179656 | tf_op jit(solution)/shard_map/keys_values/ppermute | solution.py:35
  79.6 4.8 %attend.4 = (f32[384,512]{1,0:T(8,128)}, f32[8,512]{1,0:T(8,128)}, f32[8,512]{1,0:T(8,128)}) custom-call(bf16[512,768]{1,0:T(8,128)(2,1)} %bitcast.5.refs_0_, bf16[384,512]{1,0:T(8,128)(2,1)} %values.1.refs_1_, bf16[512,768]{1,0:T(8,128)(2,1)} %get-tuple-element.80.refs_2_), custom_call_target="tpu_custom_call" | custom-call | flops 805306368 | bytes 3145728 | tf_op jit(solution)/shard_map/attention/attend/pallas_call | solution.py:208
  84.4 5.1 %attend.5 = (f32[384,512]{1,0:T(8,128)}, f32[8,512]{1,0:T(8,128)}, f32[8,512]{1,0:T(8,128)}) custom-call(bf16[512,768]{1,0:T(8,128)(2,1)} %bitcast.5.refs_0_, bf16[384,512]{1,0:T(8,128)(2,1)} %collective-permute-done.8.refs_1_, f32[384,512]{1,0:T(8,128)} %get-tuple-element.55.refs_2_, f32[8,512]{1,0:T(8,128)} %get-tuple-element.56.refs_3_, ...), custom_call_target="tpu_custom_call" | custom-call | flops 805306368 | bytes 3145728 | tf_op jit(solution)/shard_map/attention/attend/pallas_call | solution.py:208
  89.5 5.1 %attend.6 = (f32[384,512]{1,0:T(8,128)}, f32[8,512]{1,0:T(8,128)}, f32[8,512]{1,0:T(8,128)}) custom-call(bf16[512,768]{1,0:T(8,128)(2,1)} %bitcast.5.refs_0_, bf16[384,512]{1,0:T(8,128)(2,1)} %collective-permute-done.7.refs_1_, f32[384,512]{1,0:T(8,128)} %get-tuple-element.63.refs_2_, f32[8,512]{1,0:T(8,128)} %get-tuple-element.64.refs_3_, ...), custom_call_target="tpu_custom_call" | custom-call | flops 805306368 | bytes 3145728 | tf_op jit(solution)/shard_map/attention/attend/pallas_call | solution.py:208
  95.4 4.9 %attend.7 = bf16[4,416,128]{2,1,0:T(8,128)(2,1)} custom-call(bf16[512,768]{1,0:T(8,128)(2,1)} %bitcast.5.refs_0_, bf16[384,512]{1,0:T(8,128)(2,1)} %copy-done.3, f32[384,512]{1,0:T(8,128)} %get-tuple-element.71.refs_2_, f32[8,512]{1,0:T(8,128)} %get-tuple-element.72.refs_3_, f32[8,512]{1,0:T(8,128)} %get-tuple-element.73.refs_4_, ...), custom_call_target="tpu_custom_call" | custom-call | flops 805306368 | bytes 3145728 | tf_op jit(solution)/shard_map/attention/attend/pallas_call | solution.py:208
  100.3 11.0 %all_to_all.25.p_ref = bf16[4,416,128]{2,1,0:T(8,128)(2,1)} all-to-all(bf16[4,416,128]{2,1,0:T(8,128)(2,1)} %attend.7), channel_id=1, replica_groups=mesh['yh'=2,'yl'=2,'xh'=2,'xl'=2,'z'=4,'w'=2,'c'=2] {'yl','xl'}, dimensions={0} | all-to-all | bytes 851968 | tf_op jit(solution)/shard_map/attention/all_to_all | solution.py:43
  113.3 18.1 %all_to_all.26.p_ref = bf16[4,416,128]{2,1,0:T(8,128)(2,1)} all-to-all(bf16[4,416,128]{2,1,0:T(8,128)(2,1)} %merge_second.1), channel_id=1, replica_groups=mesh['yh'=2,'yl'=2,'xh'=2,'xl'=2,'z'=4,'w'=2,'c'=2] {'z'}, dimensions={0} | all-to-all | bytes 851968 | tf_op jit(solution)/shard_map/attention/all_to_all | solution.py:43
  133.1 5.6 %all-gather = f32[256,128]{1,0:T(8,128)S(1)} all-gather(f32[64,128]{1,0:T(8,128)} %merge_last.1), channel_id=2, replica_groups=mesh['yh'=2,'yl'=2,'xh'=2,'xl'=2,'z'=4,'w'=2,'c'=2] {'w','c'}, dimensions={0}, use_global_device_ids=true | all-gather | bytes 163840 | tf_op jit(solution)/shard_map/velocity/all_gather | solution.py:415
  138.8 17.0 %all_to_all.27.v_ref = f32[16,64,128]{2,1,0:T(8,128)} all-to-all(f32[16,64,128]{2,1,0:T(8,128)S(1)} %broadcast_in_dim.2), channel_id=1, replica_groups=mesh['yh'=2,'yl'=2,'xh'=2,'xl'=2,'z'=4,'w'=2,'c'=2] {'yh','yl','xh','xl'}, dimensions={0} | all-to-all | bytes 1048576 | tf_op jit(solution)/shard_map/velocity/all_to_all | solution.py:43
  155.9 2.9 %decode.1 = bf16[2,128,1024]{2,1,0:T(8,128)(2,1)} custom-call(s32[4]{0:T(128)} %refresh_ref.5, s32[1]{0:T(128)} %bitcast.me_ref, f32[1]{0:T(128)S(6)} %copy.24.level_ref, f32[16,64,128]{2,1,0:T(8,128)} %all_to_all.27.v_ref, f32[32,1024]{1,0:T(8,128)} %get-tuple-element.76.base_ref, f32[16,1024]{1,0:T(8,128)} %collective-permute-done.up_ref, ...), custom_call_target="tpu_custom_call" | custom-call | flops 83886080 | bytes 2097152 | tf_op jit(solution)/shard_map/decode/decode/pallas_call | solution.py:333
  (38 shorter events, 20.5 us)
Async XLA Ops:
  0.0 29.7 %copy-start = (bf16[512,3072]{1,0:T(8,128)(2,1)S(1)}, bf16[512,3072]{1,0:T(8,128)(2,1)}, u32[]{:S(2)}) copy-start(bf16[512,3072]{1,0:T(8,128)(2,1)} %param.15) | copy-start | bytes 9437188
  0.0 16.2 %copy-start.5 = (s32[4]{0:T(128)S(1)}, s32[4]{0:T(128)}, u32[]{:S(2)}) copy-start(s32[4]{0:T(128)} %refresh_ref.5) | copy-start | bytes 52
  2.2 48.3 %all-to-all-start = ((bf16[64,8,768]{2,1,0:T(8,128)(2,1)}), bf16[64,8,768]{2,1,0:T(8,128)(2,1)}, u32[]{:S(2)}, u32[]{:S(2)}) async-start(bf16[64,8,768]{2,1,0:T(8,128)(2,1)} %slice_bitcast_fusion), calls=%async_computation | async-start | bytes 1572864 | tf_op jit(solution)/shard_map/queries/all_to_all | solution.py:43
  16.8 4.4 %copy-start.1 = (bf16[512,3,768]{2,0,1:T(8,128)(2,1)S(1)}, bf16[512,3,768]{2,0,1:T(8,128)(2,1)}, u32[]{:S(2)}) copy-start(bf16[512,3,768]{2,0,1:T(8,128)(2,1)} %param.13) | copy-start | bytes 7077892
  21.2 8.4 %copy-start.2 = (bf16[3072,64]{0,1:T(8,128)(2,1)S(1)}, bf16[3072,64]{0,1:T(8,128)(2,1)}, u32[]{:S(2)}) copy-start(bf16[3072,64]{0,1:T(8,128)(2,1)} %param.18) | copy-start | bytes 1179652
  21.3 8.4 %copy-start.6 = (f32[64]{0:T(128)S(1)}, f32[64]{0:T(128)}, u32[]{:S(2)}) copy-start(f32[64]{0:T(128)} %param.19) | copy-start | bytes 772
  23.3 26.4 %collective-permute-start.2 = (bf16[512,768]{1,0:T(8,128)(2,1)}, bf16[512,768]{1,0:T(8,128)(2,1)}, u32[]{:S(2)}, u32[]{:S(2)}) collective-permute-start(bf16[512,768]{1,0:T(8,128)(2,1)} %get-tuple-element.80.refs_2_), channel_id=1, source_target_pairs={{0,48},{4,52},{8,56},{12,60},{16,32},{20,36},{24,40},{28,44},{32,1... | collective-permute-start | bytes 2359304 | tf_op jit(solution)/shard_map/keys_values/ppermute | solution.py:35
  26.1 24.4 %collective-permute-start.3 = (bf16[512,768]{1,0:T(8,128)(2,1)}, bf16[512,768]{1,0:T(8,128)(2,1)}, u32[]{:S(2)}, u32[]{:S(2)}) collective-permute-start(bf16[512,768]{1,0:T(8,128)(2,1)} %get-tuple-element.80.refs_2_), channel_id=1, source_target_pairs={{0,192},{4,196},{8,200},{12,204},{16,208},{20,212},{24,216},{28,22... | collective-permute-start | bytes 2359304 | tf_op jit(solution)/shard_map/keys_values/ppermute | solution.py:35
  31.4 26.8 %copy-start.4 = (f32[3072]{0:T(1024)S(1)}, f32[3072]{0:T(1024)}, u32[]{:S(2)}) copy-start(f32[3072]{0:T(1024)} %param.20) | copy-start | bytes 36868
  33.3 6.5 %collective-permute-start = (f32[16,1024]{1,0:T(8,128)}, f32[16,1024]{1,0:T(8,128)}, u32[]{:S(2)}, u32[]{:S(2)}) collective-permute-start(f32[16,1024]{1,0:T(8,128)} %get-tuple-element.44), channel_id=1, source_target_pairs={{0,4},{4,8},{8,12},{12,16},{16,20},{20,24},{24,28},{28,32},{32,36}... | collective-permute-start | bytes 196616 | tf_op jit(solution)/shard_map/latent_base/ppermute | solution.py:381
  38.2 8.0 %collective-permute-start.1 = (f32[16,1024]{1,0:T(8,128)}, f32[16,1024]{1,0:T(8,128)}, u32[]{:S(2)}, u32[]{:S(2)}) collective-permute-start(f32[16,1024]{1,0:T(8,128)} %get-tuple-element.45), channel_id=1, source_target_pairs={{4,0},{8,4},{12,8},{16,12},{20,16},{24,20},{28,24},{32,28},{36,32}... | collective-permute-start | bytes 196616 | tf_op jit(solution)/shard_map/latent_base/ppermute | solution.py:382
  52.6 27.0 %all-to-all-start.1 = ((bf16[16,32,768]{2,1,0:T(8,128)(2,1)}), bf16[16,32,768]{2,1,0:T(8,128)(2,1)}, u32[]{:S(2)}, u32[]{:S(2)}) async-start(bf16[16,32,768]{2,1,0:T(8,128)(2,1)} %select.1), calls=%async_computation.1 | async-start | bytes 1572864 | tf_op jit(solution)/shard_map/queries/all_to_all | solution.py:43
  65.4 19.0 %collective-permute-start.8 = (bf16[384,512]{1,0:T(8,128)(2,1)}, bf16[384,512]{1,0:T(8,128)(2,1)}, u32[]{:S(2)}, u32[]{:S(2)}) collective-permute-start(bf16[384,512]{1,0:T(8,128)(2,1)} %values.1.refs_1_), channel_id=1, source_target_pairs={{0,48},{4,52},{8,56},{12,60},{16,32},{20,36},{24,40},{28,44},{32,1... | collective-permute-start | bytes 1179656 | tf_op jit(solution)/shard_map/keys_values/ppermute | solution.py:35
  67.7 21.8 %collective-permute-start.7 = (bf16[384,512]{1,0:T(8,128)(2,1)}, bf16[384,512]{1,0:T(8,128)(2,1)}, u32[]{:S(2)}, u32[]{:S(2)}) collective-permute-start(bf16[384,512]{1,0:T(8,128)(2,1)} %values.1.refs_1_), channel_id=1, source_target_pairs={{0,192},{4,196},{8,200},{12,204},{16,208},{20,212},{24,216},{28,22... | collective-permute-start | bytes 1179656 | tf_op jit(solution)/shard_map/keys_values/ppermute | solution.py:35
  70.1 24.5 %collective-permute-start.4 = (bf16[384,512]{1,0:T(8,128)(2,1)}, bf16[384,512]{1,0:T(8,128)(2,1)S(1)}, u32[]{:S(2)}, u32[]{:S(2)}) collective-permute-start(bf16[384,512]{1,0:T(8,128)(2,1)} %values.1.refs_1_), channel_id=1, source_target_pairs={{0,240},{4,244},{8,248},{12,252},{16,224},{20,228},{24,232},{28,23... | collective-permute-start | bytes 1179656 | tf_op jit(solution)/shard_map/keys_values/ppermute | solution.py:35
  73.0 21.8 %collective-permute-start.5 = (bf16[256,768]{1,0:T(8,128)(2,1)}, bf16[256,768]{1,0:T(8,128)(2,1)}, u32[]{:S(2)}, u32[]{:S(2)}) collective-permute-start(bf16[256,768]{1,0:T(8,128)(2,1)} %slice.34), channel_id=1, source_target_pairs={{0,192},{4,196},{8,200},{12,204},{16,208},{20,212},{24,216},{28,22... | collective-permute-start | bytes 1179656 | tf_op jit(solution)/shard_map/keys_values/ppermute | solution.py:35
  77.8 17.0 %collective-permute-start.6 = (bf16[256,768]{1,0:T(8,128)(2,1)}, bf16[256,768]{1,0:T(8,128)(2,1)}, u32[]{:S(2)}, u32[]{:S(2)}) collective-permute-start(bf16[256,768]{1,0:T(8,128)(2,1)} %slice.35), channel_id=1, source_target_pairs={{0,48},{4,52},{8,56},{12,60},{16,32},{20,36},{24,40},{28,44},{32,1... | collective-permute-start | bytes 1179656 | tf_op jit(solution)/shard_map/keys_values/ppermute | solution.py:35
  94.7 0.8 copy-start.3

commit v3 on v2

--- a/solution.py
+++ b/solution.py
@@ -91,6 +91,32 @@
         cost_estimate=cost(4 * KEYS * VEC * HEAD_DIM * HEADS_HERE, 4 * KEYS * 768),
         name="values",
     )(value_rows, mixed)
+
+
+def halves_kernel(x_ref, y_ref, a_ref, b_ref, sems):
+    half = KEYS // 2
+    copies = [
+        pltpu.make_async_copy(x_ref.at[:half], a_ref, sems.at[0]),
+        pltpu.make_async_copy(y_ref.at[half:], b_ref, sems.at[1]),
+    ]
+    for copy in copies:
+        copy.start()
+    for copy in copies:
+        copy.wait()
+
+
+def halves(keys_x, keys_y):
+    anywhere = pl.BlockSpec(memory_space=pl.ANY)
+    half = jax.ShapeDtypeStruct((KEYS // 2, keys_x.shape[1]), BF16)
+    return pl.pallas_call(
+        halves_kernel,
+        in_specs=[anywhere] * 2,
+        out_specs=(anywhere, anywhere),
+        out_shape=(half, half),
+        scratch_shapes=[pltpu.SemaphoreType.DMA((2,))],
+        cost_estimate=cost(0, 2 * KEYS * keys_x.shape[1] * 2),
+        name="halves",
+    )(keys_x, keys_y)
 
 
 def base_kernel(refresh_ref, me_ref, level_ref, plain_ref, noisy_ref, cache_ref, o_ref, *rest):
@@ -382,7 +408,7 @@
         down = lax.ppermute(edge_first, PATCH, [(p + 1, p) for p in range(PATCHES - 1)])
 
     with jax.named_scope("queries"):
-        got, base, up, down, keys_x, keys_y = together((got, base, up, down, keys_x, keys_y))
+        got, base, up, down, _ = together((got, base, up, down, keys))
         held = exchange(select(refresh, got), ("yl", "xl", "z"))
 
     with jax.named_scope("keys_values"):
@@ -391,23 +417,20 @@
         both = jnp.concatenate([high, gated - high], axis=0).astype(BF16)
         mixed = lax.dot_general(both, out_weight, (((1,), (1,)), ((), ())), preferred_element_type=F32)
         values = project_values(value_rows, mixed[:VEC] + mixed[VEC:])
-        half = KEYS // 2
-        keys_far = mirror(keys_x[:half], 1, 0), mirror(keys_y[half:], 0, 1)
-        blocks = [
-            (values, (keys,)),
-            (mirror(values, 0, 1), (keys_x,)),
-            (mirror(values, 1, 0), (keys_y,)),
-            (mirror(values, 1, 1), keys_far),
-        ]
+        values_x, values_y, values_far = mirror(values, 0, 1), mirror(values, 1, 0), mirror(values, 1, 1)
 
     with jax.named_scope("attention"):
         held, values = together((held, values))
         queries = held.reshape(16 * SLOTS * CHUNK, HEADS_HERE * HEAD_DIM)
-        state = None
-        for k, (values, keys) in enumerate(blocks):
-            if k:
-                values, keys, state = together((values, keys, state))
-            state = attend(queries, values, state, keys)
+        state = attend(queries, values, None, (keys,))
+        keys_x, keys_y, state = together((keys_x, keys_y, state))
+        far_a, far_b = halves(keys_x, keys_y)
+        far_a, far_b = mirror(far_a, 1, 0), mirror(far_b, 0, 1)
+        state = attend(queries, values_x, state, (keys_x,))
+        values_y, state = together((values_y, state))
+        state = attend(queries, values_y, state, (keys_y,))
+        values_far, far_a, far_b, state = together((values_far, far_a, far_b, state))
+        state = attend(queries, values_far, state, (far_a, far_b))
         part = merge_second(exchange(state, ("yl", "xl")))
         term = merge_last(exchange(part, "z"))
 

time: 161 us -> 178 us (1.11)
  Pallas kernels: 32.8 us -> 57.7 us
  local copies, waits for them, and re-layouts: 10.8 us -> 6.96 us
  starting transfers between devices: 42 us -> 39.2 us
    pallas_call x0 -> x1, Pallas kernels: none -> 24.9 us  [halves(): pl.pallas_call(halves_kernel, in_specs=[anywhere] * 2, out_specs=(anywher...]
    all_to_all x2, waiting for transfers between devices: 0.01 us -> 10.7 us  [exchange(): return lax.all_to_all(value, axis, 0, 0)]
    ppermute x1, waiting for transfers between devices: 6.4 us -> 0.39 us  [on_device(): lax.ppermute(edge_first, PATCH, [(p + 1, p) for p in range(PATCHES - 1)])]
    ppermute x7, waiting for transfers between devices: 4.5 us -> 0.54 us  [mirror(): return lax.ppermute(value, PATCH, pairs)]
    slice x2 -> x0, local copies, waits for them, and re-layouts: 3.57 us -> none  [on_device(): keys_far = (mirror(keys_x[:half], 1, 0), mirror(keys_y[half:], 0, 1))]
    all_to_all x3, blocking collectives: 46.2 us -> 44.2 us  [exchange(): return lax.all_to_all(value, axis, 0, 0)]
  transfers between devices with their start and end apart: 11 -> 11, of which waited for: 5 -> 5; matrix products, arithmetic and copies ran while one was open for 11% -> 8% of each run, Pallas kernels for 12% -> 25%
where the time goes in v3:
time: 178 us; the launch traced here: 177 us
  Pallas kernels  57.7 us (32%)
  blocking collectives  50.3 us (28%)
  starting transfers between devices  39.2 us (22%)
  waiting for transfers between devices  12.8 us (7%)
  local copies, waits for them, and re-layouts  6.96 us (4%)
  matrix products  5.75 us (3%)
  other arithmetic  3.52 us (2%)
    all_to_all x3, blocking collectives, exchange(): return lax.all_to_all(value, axis, 0, 0)  44.2 us
    pallas_call x1, Pallas kernels, halves(): pl.pallas_call(halves_kernel, in_specs=[anywhere] * 2, out_specs=(anywher...  24.9 us
    pallas_call x4, Pallas kernels, attend(): pl.pallas_call(functools.partial(attend_kernel, first, last), out_shape=o...  20 us
    all_to_all x2, starting transfers between devices, exchange(): return lax.all_to_all(value, axis, 0, 0)  18.2 us
    ppermute x7, starting transfers between devices, mirror(): return lax.ppermute(value, PATCH, pairs)  14.8 us
    all_to_all x2, waiting for transfers between devices, exchange(): return lax.all_to_all(value, axis, 0, 0)  10.7 us
    all_gather x1, blocking collectives, on_device(): term = jnp.sum(lax.all_gather(term, HEAD), axis=0)  6.08 us
    ppermute x1, starting transfers between devices, on_device(): lax.ppermute(edge_last, PATCH, [(p, p + 1) for p in range(PATCHES - 1)])  4.92 us
  transfers between devices with their start and end apart: 11, of which 5 were waited for; matrix products, arithmetic and copies ran while one was open for 8% of the time, Pallas kernels for 25%

profile of v3, /device:TPU:32, one launch (start us, length us, event | category | flops | bytes accessed | tf_op | source)
XLA Modules:
  0.0 177.1 jit_solution(4720998013488720680)
XLA Ops:
  0.0 2.2 %slice_bitcast_fusion = bf16[64,8,768]{2,1,0:T(8,128)(2,1)} fusion(bf16[512,3,768]{2,0,1:T(8,128)(2,1)} %param.13), kind=kLoop, calls=%fused_computation.13 | loop fusion | bytes 1572864 | tf_op jit(solution)/shard_map/queries/reshape;queries/squeeze | solution.py:389
  2.3 13.9 %all-to-all-start = ((bf16[64,8,768]{2,1,0:T(8,128)(2,1)}), bf16[64,8,768]{2,1,0:T(8,128)(2,1)}, u32[]{:S(2)}, u32[]{:S(2)}) async-start(bf16[64,8,768]{2,1,0:T(8,128)(2,1)} %slice_bitcast_fusion), calls=%async_computation | async-start | bytes 1572864 | tf_op jit(solution)/shard_map/queries/all_to_all | solution.py:43
  20.5 4.9 %collective-permute-start = (f32[16,1024]{1,0:T(8,128)}, f32[16,1024]{1,0:T(8,128)}, u32[]{:S(2)}, u32[]{:S(2)}) collective-permute-start(f32[16,1024]{1,0:T(8,128)} %get-tuple-element.44), channel_id=1, source_target_pairs={{0,4},{4,8},{8,12},{12,16},{16,20},{20,24},{24,28},{28,32},{32,36}... | collective-permute-start | bytes 196616 | tf_op jit(solution)/shard_map/latent_base/ppermute | solution.py:407
  27.4 4.4 %fusion.8 = (bf16[512,1,768]{2,1,0:T(2,128)(2,1)S(1)}, bf16[512,1,768]{2,1,0:T(2,128)(2,1)S(1)}) fusion(bf16[512,2,768]{2,1,0:T(2,128)(2,1)} %param.14), kind=kLoop, calls=%fused_computation.17 | loop fusion | bytes 3145728 | tf_op jit(solution)/shard_map/keys_values/slice | solution.py:396
  31.8 2.0 %fusion.5 = (bf16[512,768]{1,0:T(8,128)(2,1)}, bf16[512,768]{1,0:T(8,128)(2,1)}) fusion(bf16[512,1,768]{2,1,0:T(2,128)(2,1)S(1)} %get-tuple-element.81, bf16[512,3,768]{2,0,1:T(8,128)(2,1)S(1)} %copy-done.1, pred[]{:T(512)} %compare_reduce_fusion, bf16[512,1,768]{2,1,0:T(2,128)(2,1)S(1)} %get-tuple-element.82), kind=kLoop, calls=%fused_computation.9 | loop fusion | flops 786432 | bytes 4718593 | tf_op jit(solution)/shard_map/keys_values/jit(_where)/select_n | solution.py:396
  35.4 8.0 %all-to-all-done.got_ref = bf16[64,8,768]{2,1,0:T(8,128)(2,1)} async-done(((bf16[64,8,768]{2,1,0:T(8,128)(2,1)}), bf16[64,8,768]{2,1,0:T(8,128)(2,1)}, u32[]{:S(2)}, u32[]{:S(2)}) %all-to-all-start) | async-done | bytes 786464 | tf_op jit(solution)/shard_map/queries/all_to_all | solution.py:43
  43.4 2.1 %select.1 = bf16[16,32,768]{2,1,0:T(8,128)(2,1)} custom-call(s32[4]{0:T(128)} %refresh_ref.5, bf16[64,8,768]{2,1,0:T(8,128)(2,1)} %all-to-all-done.got_ref), custom_call_target="tpu_custom_call" | custom-call | bytes 835584 | tf_op jit(solution)/shard_map/queries/select/pallas_call | solution.py:68
  45.5 4.3 %all-to-all-start.1 = ((bf16[16,32,768]{2,1,0:T(8,128)(2,1)}), bf16[16,32,768]{2,1,0:T(8,128)(2,1)}, u32[]{:S(2)}, u32[]{:S(2)}) async-start(bf16[16,32,768]{2,1,0:T(8,128)(2,1)} %select.1), calls=%async_computation.1 | async-start | bytes 1572864 | tf_op jit(solution)/shard_map/queries/all_to_all | solution.py:43
  50.8 2.3 %collective-permute-start.4 = (bf16[512,768]{1,0:T(8,128)(2,1)}, bf16[512,768]{1,0:T(8,128)(2,1)}, u32[]{:S(2)}, u32[]{:S(2)}) collective-permute-start(bf16[512,768]{1,0:T(8,128)(2,1)} %get-tuple-element.80.refs_2_), channel_id=1, source_target_pairs={{0,192},{4,196},{8,200},{12,204},{16,208},{20,212},{24,216},{28,22... | collective-permute-start | bytes 2359304 | tf_op jit(solution)/shard_map/keys_values/ppermute | solution.py:35
  53.3 4.0 %fusion.1 = f32[128,768]{1,0:T(8,128)S(1)} fusion(bf16[768,3072]{1,0:T(8,128)(2,1)} %param.17, bf16[64,3072]{1,0:T(8,128)(2,1)S(1)} %get-tuple-element.84, bf16[64,3072]{1,0:T(8,128)(2,1)S(1)} %get-tuple-element.83), kind=kOutput, calls=%fused_computation.4 | convolution fusion | flops 605552640 | bytes 5898240 | tf_op jit(solution)/shard_map/keys_values/dot_general | solution.py:418
  58.0 2.3 %values.1.refs_1_ = bf16[384,512]{1,0:T(8,128)(2,1)} custom-call(bf16[512,768]{1,0:T(8,128)(2,1)} %get-tuple-element.79.v_ref, f32[64,768]{1,0:T(8,128)} %slice_add_fusion.w_ref), custom_call_target="tpu_custom_call" | custom-call | flops 100663296 | bytes 1572864 | tf_op jit(solution)/shard_map/keys_values/values/pallas_call | solution.py:88
  63.5 2.7 %collective-permute-start.2 = (bf16[384,512]{1,0:T(8,128)(2,1)}, bf16[384,512]{1,0:T(8,128)(2,1)S(1)}, u32[]{:S(2)}, u32[]{:S(2)}) collective-permute-start(bf16[384,512]{1,0:T(8,128)(2,1)} %values.1.refs_1_), channel_id=1, source_target_pairs={{0,240},{4,244},{8,248},{12,252},{16,224},{20,228},{24,232},{28,23... | collective-permute-start | bytes 1179656 | tf_op jit(solution)/shard_map/keys_values/ppermute | solution.py:35
  66.2 2.7 %all-to-all-done.1 = bf16[16,32,768]{2,1,0:T(8,128)(2,1)} async-done(((bf16[16,32,768]{2,1,0:T(8,128)(2,1)}), bf16[16,32,768]{2,1,0:T(8,128)(2,1)}, u32[]{:S(2)}, u32[]{:S(2)}) %all-to-all-start.1) | async-done | bytes 786464 | tf_op jit(solution)/shard_map/queries/all_to_all | solution.py:43
  68.9 4.8 %attend.4 = (f32[384,512]{1,0:T(8,128)}, f32[8,512]{1,0:T(8,128)}, f32[8,512]{1,0:T(8,128)}) custom-call(bf16[512,768]{1,0:T(8,128)(2,1)} %bitcast.5.refs_0_, bf16[384,512]{1,0:T(8,128)(2,1)} %values.1.refs_1_, bf16[512,768]{1,0:T(8,128)(2,1)} %get-tuple-element.80.refs_2_), custom_call_target="tpu_custom_call" | custom-call | flops 805306368 | bytes 3145728 | tf_op jit(solution)/shard_map/attention/attend/pallas_call | solution.py:234
  73.7 24.9 %halves.1 = (bf16[256,768]{1,0:T(8,128)(2,1)}, bf16[256,768]{1,0:T(8,128)(2,1)}) custom-call(bf16[512,768]{1,0:T(8,128)(2,1)} %collective-permute-done.3.x_ref.refs_5_, bf16[512,768]{1,0:T(8,128)(2,1)} %collective-permute-done.4.y_ref.refs_5_), custom_call_target="tpu_custom_call" | custom-call | bytes 1572864 | tf_op jit(solution)/shard_map/attention/halves/pallas_call | solution.py:111
  98.7 4.2 %collective-permute-start.5 = (bf16[256,768]{1,0:T(8,128)(2,1)}, bf16[256,768]{1,0:T(8,128)(2,1)}, u32[]{:S(2)}, u32[]{:S(2)}) collective-permute-start(bf16[256,768]{1,0:T(8,128)(2,1)} %get-tuple-element.55), channel_id=1, source_target_pairs={{0,192},{4,196},{8,200},{12,204},{16,208},{20,212},{24,216},{28,22... | collective-permute-start | bytes 1179656 | tf_op jit(solution)/shard_map/attention/ppermute | solution.py:35
  104.2 5.2 %attend.5 = (f32[384,512]{1,0:T(8,128)}, f32[8,512]{1,0:T(8,128)}, f32[8,512]{1,0:T(8,128)}) custom-call(bf16[512,768]{1,0:T(8,128)(2,1)} %bitcast.5.refs_0_, bf16[384,512]{1,0:T(8,128)(2,1)} %collective-permute-done.8.refs_1_, f32[384,512]{1,0:T(8,128)} %get-tuple-element.57.refs_2_, f32[8,512]{1,0:T(8,128)} %get-tuple-element.58.refs_3_, ...), custom_call_target="tpu_custom_call" | custom-call | flops 805306368 | bytes 3145728 | tf_op jit(solution)/shard_map/attention/attend/pallas_call | solution.py:234
  109.4 5.1 %attend.6 = (f32[384,512]{1,0:T(8,128)}, f32[8,512]{1,0:T(8,128)}, f32[8,512]{1,0:T(8,128)}) custom-call(bf16[512,768]{1,0:T(8,128)(2,1)} %bitcast.5.refs_0_, bf16[384,512]{1,0:T(8,128)(2,1)} %collective-permute-done.7.refs_1_, f32[384,512]{1,0:T(8,128)} %get-tuple-element.64.refs_2_, f32[8,512]{1,0:T(8,128)} %get-tuple-element.65.refs_3_, ...), custom_call_target="tpu_custom_call" | custom-call | flops 805306368 | bytes 3145728 | tf_op jit(solution)/shard_map/attention/attend/pallas_call | solution.py:234
  115.3 4.9 %attend.7 = bf16[4,416,128]{2,1,0:T(8,128)(2,1)} custom-call(bf16[512,768]{1,0:T(8,128)(2,1)} %bitcast.5.refs_0_, bf16[384,512]{1,0:T(8,128)(2,1)} %copy-done.3, f32[384,512]{1,0:T(8,128)} %get-tuple-element.71.refs_2_, f32[8,512]{1,0:T(8,128)} %get-tuple-element.72.refs_3_, f32[8,512]{1,0:T(8,128)} %get-tuple-element.73.refs_4_, ...), custom_call_target="tpu_custom_call" | custom-call | flops 805306368 | bytes 3145728 | tf_op jit(solution)/shard_map/attention/attend/pallas_call | solution.py:234
  120.2 11.0 %all_to_all.25.p_ref = bf16[4,416,128]{2,1,0:T(8,128)(2,1)} all-to-all(bf16[4,416,128]{2,1,0:T(8,128)(2,1)} %attend.7), channel_id=1, replica_groups=mesh['yh'=2,'yl'=2,'xh'=2,'xl'=2,'z'=4,'w'=2,'c'=2] {'yl','xl'}, dimensions={0} | all-to-all | bytes 851968 | tf_op jit(solution)/shard_map/attention/all_to_all | solution.py:43
  133.1 15.3 %all_to_all.26.p_ref = bf16[4,416,128]{2,1,0:T(8,128)(2,1)} all-to-all(bf16[4,416,128]{2,1,0:T(8,128)(2,1)} %merge_second.1), channel_id=1, replica_groups=mesh['yh'=2,'yl'=2,'xh'=2,'xl'=2,'z'=4,'w'=2,'c'=2] {'z'}, dimensions={0} | all-to-all | bytes 851968 | tf_op jit(solution)/shard_map/attention/all_to_all | solution.py:43
  150.1 6.1 %all-gather = f32[256,128]{1,0:T(8,128)S(1)} all-gather(f32[64,128]{1,0:T(8,128)} %merge_last.1), channel_id=2, replica_groups=mesh['yh'=2,'yl'=2,'xh'=2,'xl'=2,'z'=4,'w'=2,'c'=2] {'w','c'}, dimensions={0}, use_global_device_ids=true | all-gather | bytes 163840 | tf_op jit(solution)/shard_map/velocity/all_gather | solution.py:438
  156.3 17.9 %all_to_all.27.v_ref = f32[16,64,128]{2,1,0:T(8,128)} all-to-all(f32[16,64,128]{2,1,0:T(8,128)S(1)} %broadcast_in_dim.2), channel_id=1, replica_groups=mesh['yh'=2,'yl'=2,'xh'=2,'xl'=2,'z'=4,'w'=2,'c'=2] {'yh','yl','xh','xl'}, dimensions={0} | all-to-all | bytes 1048576 | tf_op jit(solution)/shard_map/velocity/all_to_all | solution.py:43
  174.2 2.9 %decode.1 = bf16[2,128,1024]{2,1,0:T(8,128)(2,1)} custom-call(s32[4]{0:T(128)} %refresh_ref.5, s32[1]{0:T(128)} %bitcast.me_ref, f32[1]{0:T(128)S(6)} %copy.24.level_ref, f32[16,64,128]{2,1,0:T(8,128)} %all_to_all.27.v_ref, f32[32,1024]{1,0:T(8,128)} %get-tuple-element.76.base_ref, f32[16,1024]{1,0:T(8,128)} %collective-permute-done.up_ref, ...), custom_call_target="tpu_custom_call" | custom-call | flops 83886080 | bytes 2097152 | tf_op jit(solution)/shard_map/decode/decode/pallas_call | solution.py:359
  (37 shorter events, 18.0 us)
Async XLA Ops:
  0.0 16.8 %copy-start = (bf16[512,3072]{1,0:T(8,128)(2,1)S(1)}, bf16[512,3072]{1,0:T(8,128)(2,1)}, u32[]{:S(2)}) copy-start(bf16[512,3072]{1,0:T(8,128)(2,1)} %param.15) | copy-start | bytes 9437188
  0.0 16.8 %copy-start.2 = (bf16[3072,64]{0,1:T(8,128)(2,1)S(1)}, bf16[3072,64]{0,1:T(8,128)(2,1)}, u32[]{:S(2)}) copy-start(bf16[3072,64]{0,1:T(8,128)(2,1)} %param.18) | copy-start | bytes 1179652
  0.0 16.9 %copy-start.6 = (f32[64]{0:T(128)S(1)}, f32[64]{0:T(128)}, u32[]{:S(2)}) copy-start(f32[64]{0:T(128)} %param.19) | copy-start | bytes 772
  2.3 41.1 %all-to-all-start = ((bf16[64,8,768]{2,1,0:T(8,128)(2,1)}), bf16[64,8,768]{2,1,0:T(8,128)(2,1)}, u32[]{:S(2)}, u32[]{:S(2)}) async-start(bf16[64,8,768]{2,1,0:T(8,128)(2,1)} %slice_bitcast_fusion), calls=%async_computation | async-start | bytes 1572864 | tf_op jit(solution)/shard_map/queries/all_to_all | solution.py:43
  16.2 10.6 %copy-start.5 = (s32[4]{0:T(128)S(1)}, s32[4]{0:T(128)}, u32[]{:S(2)}) copy-start(s32[4]{0:T(128)} %refresh_ref.5) | copy-start | bytes 52
  20.5 14.5 %collective-permute-start = (f32[16,1024]{1,0:T(8,128)}, f32[16,1024]{1,0:T(8,128)}, u32[]{:S(2)}, u32[]{:S(2)}) collective-permute-start(f32[16,1024]{1,0:T(8,128)} %get-tuple-element.44), channel_id=1, source_target_pairs={{0,4},{4,8},{8,12},{12,16},{16,20},{20,24},{24,28},{28,32},{32,36}... | collective-permute-start | bytes 196616 | tf_op jit(solution)/shard_map/latent_base/ppermute | solution.py:407
  25.4 10.0 %collective-permute-start.1 = (f32[16,1024]{1,0:T(8,128)}, f32[16,1024]{1,0:T(8,128)}, u32[]{:S(2)}, u32[]{:S(2)}) collective-permute-start(f32[16,1024]{1,0:T(8,128)} %get-tuple-element.45), channel_id=1, source_target_pairs={{4,0},{8,4},{12,8},{16,12},{20,16},{24,20},{28,24},{32,28},{36,32}... | collective-permute-start | bytes 196616 | tf_op jit(solution)/shard_map/latent_base/ppermute | solution.py:408
  27.4 4.4 %copy-start.1 = (bf16[512,3,768]{2,0,1:T(8,128)(2,1)S(1)}, bf16[512,3,768]{2,0,1:T(8,128)(2,1)}, u32[]{:S(2)}) copy-start(bf16[512,3,768]{2,0,1:T(8,128)(2,1)} %param.13) | copy-start | bytes 7077892
  33.8 19.3 %copy-start.4 = (f32[3072]{0:T(1024)S(1)}, f32[3072]{0:T(1024)}, u32[]{:S(2)}) copy-start(f32[3072]{0:T(1024)} %param.20) | copy-start | bytes 36868
  45.5 23.4 %all-to-all-start.1 = ((bf16[16,32,768]{2,1,0:T(8,128)(2,1)}), bf16[16,32,768]{2,1,0:T(8,128)(2,1)}, u32[]{:S(2)}, u32[]{:S(2)}) async-start(bf16[16,32,768]{2,1,0:T(8,128)(2,1)} %select.1), calls=%async_computation.1 | async-start | bytes 1572864 | tf_op jit(solution)/shard_map/queries/all_to_all | solution.py:43
  49.8 23.9 %collective-permute-start.3 = (bf16[512,768]{1,0:T(8,128)(2,1)}, bf16[512,768]{1,0:T(8,128)(2,1)}, u32[]{:S(2)}, u32[]{:S(2)}) collective-permute-start(bf16[512,768]{1,0:T(8,128)(2,1)} %get-tuple-element.80.refs_2_), channel_id=1, source_target_pairs={{0,48},{4,52},{8,56},{12,60},{16,32},{20,36},{24,40},{28,44},{32,1... | collective-permute-start | bytes 2359304 | tf_op jit(solution)/shard_map/keys_values/ppermute | solution.py:35
  50.8 22.9 %collective-permute-start.4 = (bf16[512,768]{1,0:T(8,128)(2,1)}, bf16[512,768]{1,0:T(8,128)(2,1)}, u32[]{:S(2)}, u32[]{:S(2)}) collective-permute-start(bf16[512,768]{1,0:T(8,128)(2,1)} %get-tuple-element.80.refs_2_), channel_id=1, source_target_pairs={{0,192},{4,196},{8,200},{12,204},{16,208},{20,212},{24,216},{28,22... | collective-permute-start | bytes 2359304 | tf_op jit(solution)/shard_map/keys_values/ppermute | solution.py:35
  60.3 43.9 %collective-permute-start.8 = (bf16[384,512]{1,0:T(8,128)(2,1)}, bf16[384,512]{1,0:T(8,128)(2,1)}, u32[]{:S(2)}, u32[]{:S(2)}) collective-permute-start(bf16[384,512]{1,0:T(8,128)(2,1)} %values.1.refs_1_), channel_id=1, source_target_pairs={{0,48},{4,52},{8,56},{12,60},{16,32},{20,36},{24,40},{28,44},{32,1... | collective-permute-start | bytes 1179656 | tf_op jit(solution)/shard_map/keys_values/ppermute | solution.py:35
  61.8 47.6 %collective-permute-start.7 = (bf16[384,512]{1,0:T(8,128)(2,1)}, bf16[384,512]{1,0:T(8,128)(2,1)}, u32[]{:S(2)}, u32[]{:S(2)}) collective-permute-start(bf16[384,512]{1,0:T(8,128)(2,1)} %values.1.refs_1_), channel_id=1, source_target_pairs={{0,192},{4,196},{8,200},{12,204},{16,208},{20,212},{24,216},{28,22... | collective-permute-start | bytes 1179656 | tf_op jit(solution)/shard_map/keys_values/ppermute | solution.py:35
  63.5 51.0 %collective-permute-start.2 = (bf16[384,512]{1,0:T(8,128)(2,1)}, bf16[384,512]{1,0:T(8,128)(2,1)S(1)}, u32[]{:S(2)}, u32[]{:S(2)}) collective-permute-start(bf16[384,512]{1,0:T(8,128)(2,1)} %values.1.refs_1_), channel_id=1, source_target_pairs={{0,240},{4,244},{8,248},{12,252},{16,224},{20,228},{24,232},{28,23... | collective-permute-start | bytes 1179656 | tf_op jit(solution)/shard_map/keys_values/ppermute | solution.py:35
  98.7 15.9 %collective-permute-start.5 = (bf16[256,768]{1,0:T(8,128)(2,1)}, bf16[256,768]{1,0:T(8,128)(2,1)}, u32[]{:S(2)}, u32[]{:S(2)}) collective-permute-start(bf16[256,768]{1,0:T(8,128)(2,1)} %get-tuple-element.55), channel_id=1, source_target_pairs={{0,192},{4,196},{8,200},{12,204},{16,208},{20,212},{24,216},{28,22... | collective-permute-start | bytes 1179656 | tf_op jit(solution)/shard_map/attention/ppermute | solution.py:35
  102.9 12.1 %collective-permute-start.6 = (bf16[256,768]{1,0:T(8,128)(2,1)}, bf16[256,768]{1,0:T(8,128)(2,1)}, u32[]{:S(2)}, u32[]{:S(2)}) collective-permute-start(bf16[256,768]{1,0:T(8,128)(2,1)} %get-tuple-element.56), channel_id=1, source_target_pairs={{0,48},{4,52},{8,56},{12,60},{16,32},{20,36},{24,40},{28,44},{32,1... | collective-permute-start | bytes 1179656 | tf_op jit(solution)/shard_map/attention/ppermute | solution.py:35
  114.5 0.8 copy-start.3

commit v4 on v3

--- a/solution.py
+++ b/solution.py
@@ -14,10 +14,7 @@
 PATCHES = 64
 SLOTS = 4
 HEADS_HERE = 6
-HALF = 3
 VEC = 64
-ROWS = HALF * VEC
-PACK = ROWS + 16
 KEYS = 512
 COLS = 1024
 CHUNK = 8
@@ -93,27 +90,20 @@
     )(value_rows, mixed)
 
 
-def halves_kernel(x_ref, y_ref, a_ref, b_ref, sems):
-    half = KEYS // 2
-    copies = [
-        pltpu.make_async_copy(x_ref.at[:half], a_ref, sems.at[0]),
-        pltpu.make_async_copy(y_ref.at[half:], b_ref, sems.at[1]),
-    ]
-    for copy in copies:
-        copy.start()
-    for copy in copies:
-        copy.wait()
+def halves_kernel(x_ref, y_ref, a_ref, b_ref):
+    a_ref[...] = x_ref[...]
+    b_ref[...] = y_ref[...]
 
 
 def halves(keys_x, keys_y):
-    anywhere = pl.BlockSpec(memory_space=pl.ANY)
-    half = jax.ShapeDtypeStruct((KEYS // 2, keys_x.shape[1]), BF16)
+    block = (KEYS // 2, keys_x.shape[1])
+    whole = pl.BlockSpec(block, lambda i: (0, 0))
     return pl.pallas_call(
         halves_kernel,
-        in_specs=[anywhere] * 2,
-        out_specs=(anywhere, anywhere),
-        out_shape=(half, half),
-        scratch_shapes=[pltpu.SemaphoreType.DMA((2,))],
+        grid=(1,),
+        in_specs=[whole, pl.BlockSpec(block, lambda i: (1, 0))],
+        out_specs=(whole, whole),
+        out_shape=(jax.ShapeDtypeStruct(block, BF16),) * 2,
         cost_estimate=cost(0, 2 * KEYS * keys_x.shape[1] * 2),
         name="halves",
     )(keys_x, keys_y)
@@ -161,17 +151,15 @@
     )(refresh, me, level, plain, noisy, cache)
 
 
-def pack_lse(entries, width):
-    row = lax.broadcasted_iota(jnp.int32, (16, width), 0)
-    block = jnp.zeros((16, width), F32)
-    for h, lse in enumerate(entries):
+def lse_rows(lses, width):
+    row = lax.broadcasted_iota(jnp.int32, (128, width), 0)
+    block = jnp.zeros((128, width), F32)
+    for h, lse in enumerate(lses):
         high = lse.astype(BF16).astype(F32)
-        rest = lse - high
-        mid = rest.astype(BF16).astype(F32)
-        low = rest - mid
-        for part, value in enumerate((high, mid, low)):
-            block = jnp.where(row == part * HALF + h, jnp.broadcast_to(value, block.shape), block)
-    return block.astype(BF16)
+        mid = (lse - high).astype(BF16).astype(F32)
+        for part, value in enumerate((high, mid, lse - high - mid)):
+            block = jnp.where(row == part * HEADS_HERE + h, jnp.broadcast_to(value, block.shape), block)
+    return block
 
 
 def attend_kernel(first, last, *refs):
@@ -189,9 +177,13 @@
             keys, q_ref[:, cols], (((1,), (1,)), ((), ())), preferred_element_type=F32
         )
 
-    dots, lses = scores(0), []
+    def store(place, block):
+        flat = jnp.transpose(block).astype(BF16)
+        outs[0][:, :, place * 128 : (place + 1) * 128] = flat.reshape(outs[0].shape[:2] + (128,))
+
+    dots, lses, pair = scores(0), [], []
+    dots_width = dots.shape[1]
     for head in range(HEADS_HERE):
-        half, h = divmod(head, HALF)
         following = scores(head + 1) if head + 1 < HEADS_HERE else None
         rows = slice(head * VEC, (head + 1) * VEC)
         top = jnp.max(dots, axis=0, keepdims=True)
@@ -210,27 +202,24 @@
             outs[1][head : head + 1, :] = top
             outs[2][head : head + 1, :] = total
         else:
-            out = (acc * (1.0 / total)).astype(BF16)
-            row = half * PACK + h * VEC
-            for k in range(4):
-                outs[0][k, row : row + VEC, :] = out[:, k * 128 : (k + 1) * 128]
+            pair.append(acc * (1.0 / total))
             lses.append(top * (1.0 / math.sqrt(HEAD_DIM)) + jnp.log(total))
-            if h == HALF - 1:
-                packed = pack_lse(lses, out.shape[1])
-                for k in range(4):
-                    outs[0][k, half * PACK + ROWS : (half + 1) * PACK, :] = packed[:, k * 128 : (k + 1) * 128]
-                lses = []
+            if head % 2:
+                store(head // 2, jnp.concatenate(pair, axis=0))
+                pair = []
         dots = following
+    if last:
+        store(HEADS_HERE // 2, lse_rows(lses, dots_width))
 
 
 def attend(queries, values, state, keys):
     n = queries.shape[0]
     first, last = state is None, len(keys) == 2
     if last:
-        out = jax.ShapeDtypeStruct((4, 2 * PACK, n // 4), BF16)
+        out = jax.ShapeDtypeStruct((16, n // 16, 512), BF16)
     else:
         rows = jax.ShapeDtypeStruct((8, n), F32)
-        out = (jax.ShapeDtypeStruct((2 * ROWS, n), F32), rows, rows)
+        out = (jax.ShapeDtypeStruct((HEADS_HERE * VEC, n), F32), rows, rows)
     return pl.pallas_call(
         functools.partial(attend_kernel, first, last),
         out_shape=out,
@@ -241,94 +230,73 @@
     )(queries, values, *(() if first else state), *keys)
 
 
-def merge(parts_of):
-    blocks = [p(ROWS, PACK).astype(F32) for p in parts_of]
-    outs, lses = [], []
-    for h in range(HALF):
-        parts = [
-            b[h : h + 1] + b[HALF + h : HALF + h + 1] + b[2 * HALF + h : 2 * HALF + h + 1] for b in blocks
-        ]
-        top = functools.reduce(jnp.maximum, parts)
-        weights = [jnp.exp(p - top) for p in parts]
-        total = sum(weights)
-        inverse = 1.0 / total
-        acc = 0.0
-        for p, w in zip(parts_of, weights):
-            acc = acc + p(h * VEC, (h + 1) * VEC).astype(F32) * (w * inverse)
-        outs.append(acc)
-        lses.append(top + jnp.log(total))
-    return outs, lses
-
-
-def merge_second_kernel(p_ref, o_ref):
-    for base in (0, PACK):
-        outs, lses = merge([lambda a, b, k=k: p_ref[k, base + a : base + b, :] for k in range(4)])
-        packed = pack_lse(lses, 128)
-        for k in range(4):
-            for h in range(HALF):
-                o_ref[k, base + h * VEC : base + (h + 1) * VEC, :] = outs[h].astype(BF16)
-            o_ref[k, base + ROWS : base + PACK, :] = packed
-
-
-def merge_second(parts):
-    return pl.pallas_call(
-        merge_second_kernel,
-        out_shape=jax.ShapeDtypeStruct((4, 2 * PACK, 128), BF16),
-        cost_estimate=cost(8 * PACK * 128 * 2, 16 * PACK * 128 * 2),
-        name="merge_second",
+def merge_kernel(p_ref, o_ref):
+    parts, rows = p_ref.shape[:2]
+    width = HEADS_HERE * VEC
+    lse = p_ref[:, :, width:].astype(F32).reshape(parts * rows, 128)
+    lse = lse + pltpu.roll(lse, 128 - HEADS_HERE, 1) + pltpu.roll(lse, 128 - 2 * HEADS_HERE, 1)
+    lse = lse.reshape(parts, rows, 128)
+    weights = jnp.exp(lse - jnp.max(lse, axis=0, keepdims=True))
+    weights = weights * (1.0 / jnp.sum(weights, axis=0, keepdims=True))
+    lane = lax.broadcasted_iota(jnp.int32, (128, width), 0)
+    col = lax.broadcasted_iota(jnp.int32, (128, width), 1)
+    wide = (col // VEC == lane).astype(F32).astype(BF16)
+    high, low = split(weights.reshape(parts * rows, 128))
+    weights = jnp.dot(high, wide, preferred_element_type=F32) + jnp.dot(low, wide, preferred_element_type=F32)
+    weights = weights.reshape(parts, rows, width)
+    acc = jnp.sum(p_ref[:, :, :width].astype(F32) * weights, axis=0)
+    acc = acc[:, :128] + acc[:, 128:256] + acc[:, 256:]
+    acc = acc + pltpu.roll(acc, VEC, 1)
+    even = lax.broadcasted_iota(jnp.int32, (CHUNK, 128), 1) < VEC
+    for pair in range(SLOTS // 2):
+        first = acc[pair * 2 * CHUNK : (pair * 2 + 1) * CHUNK]
+        second = acc[(pair * 2 + 1) * CHUNK : (pair * 2 + 2) * CHUNK]
+        o_ref[pair * CHUNK : (pair + 1) * CHUNK, :] = jnp.where(even, first, second)
+
+
+def merge(parts):
+    return pl.pallas_call(
+        merge_kernel,
+        out_shape=jax.ShapeDtypeStruct((SLOTS // 2 * CHUNK, 128), F32),
+        cost_estimate=cost(1 << 25, parts.size * 2),
+        name="merge",
     )(parts)
 
 
-def merge_last_kernel(p_ref, o_ref):
-    outs = []
-    for base in (0, PACK):
-        outs += merge([lambda a, b, k=k: p_ref[k, base + a : base + b, :] for k in range(4)])[0]
-    o_ref[...] = sum(outs[1:], outs[0])
-
-
-def merge_last(parts):
-    return pl.pallas_call(
-        merge_last_kernel,
-        out_shape=jax.ShapeDtypeStruct((VEC, 128), F32),
-        cost_estimate=cost(8 * PACK * 128 * 2, 10 * PACK * 128),
-        name="merge_last",
-    )(parts)
-
-
-def decode_kernel(refresh_ref, me_ref, level_ref, v_ref, base_ref, up_ref, down_ref, w_ref, b_ref, o_ref):
+def decode_kernel(refresh_ref, me_ref, level_ref, v_ref, base_ref, up_ref, down_ref, w_ref, b_ref, o_ref, block_ref):
     level, me = level_ref[0], me_ref[0]
-    row = lax.broadcasted_iota(jnp.int32, (512, 128), 0)
-    col = lax.broadcasted_iota(jnp.int32, (512, 128), 1)
-    lane = row % 128
-    target = (row // 256) * 64 + ((lane // 32) * 8 + lane % 8) * 2 + (row // 128) % 2
-
-    def attention_rows(near, kinds):
+    row = lax.broadcasted_iota(jnp.int32, (256, 256), 0)
+    col = lax.broadcasted_iota(jnp.int32, (256, 256), 1)
+    choose = ((row % 128) * 2 + row // 128 == col).astype(F32).astype(BF16)
+
+    def attention_rows(which, near, kinds):
         slot, on = 0, 0
         for s in range(SLOTS):
             hit = refresh_ref[s] == me + near
             slot = jnp.where(hit, s, slot)
             on = jnp.where(hit, 1, on)
-        choose = (((lane // 8) % 4 == slot) & (target == col)).astype(F32).astype(BF16)
-        count = LAT_CH * len(kinds)
+        tokens = v_ref[:, pl.ds(pl.multiple_of((slot >> 1) * CHUNK, CHUNK), CHUNK), :].reshape(KEYS, 128)
+        tokens = jnp.transpose(tokens)
+        tokens = jnp.where((slot & 1) == 0, tokens[:VEC], tokens[VEC:])
         stacked = []
-        for ys in range(4):
-            for pair in range(2):
-                pieces = []
-                for xs in (pair * 2, pair * 2 + 1):
-                    for b in range(2):
-                        parts = [v_ref[ys * 4 + xs, pl.ds(kind * 2 + b, LAT_CH, 4), :] for kind in kinds]
-                        pieces.append(jnp.concatenate(parts, axis=0))
-                stacked.append(jnp.concatenate(pieces, axis=1))
+        for i in range(4):
+            block_ref[which, i] = tokens[:, i * 128 : (i + 1) * 128]
+            pieces = []
+            for b in range(2):
+                parts = [block_ref[which, i, pl.ds(kind * 2 + b, LAT_CH, 4), :] for kind in kinds]
+                pieces.append(jnp.concatenate(parts, axis=0))
+            stacked.append(jnp.concatenate(pieces, axis=1))
         high, low = split(jnp.concatenate(stacked, axis=0))
         field = jnp.dot(high, choose, preferred_element_type=F32) + jnp.dot(
             low, choose, preferred_element_type=F32
         )
-        field = jnp.concatenate([field[i * count : (i + 1) * count] for i in range(8)], axis=1)
+        count = LAT_CH * len(kinds)
+        field = jnp.concatenate([field[i * count : (i + 1) * count] for i in range(4)], axis=1)
         return jnp.where(on > 0, field, 0.0)
 
-    own = base_ref[...] - level * attention_rows(0, (0, 1))
-    up = up_ref[...] - level * attention_rows(-1, (1,))
-    down = down_ref[...] - level * attention_rows(1, (0,))
+    own = base_ref[...] - level * attention_rows(0, 0, (0, 1))
+    up = up_ref[...] - level * attention_rows(1, -1, (1,))
+    down = down_ref[...] - level * attention_rows(2, 1, (0,))
     latent = jnp.concatenate([up, own, down], axis=0) / 0.3611 + 0.1159
     line = lax.broadcasted_iota(jnp.int32, latent.shape, 0)
     column = lax.broadcasted_iota(jnp.int32, latent.shape, 1)
@@ -361,6 +329,7 @@
         out_shape=jax.ShapeDtypeStruct((2, weight.shape[3], COLS), BF16),
         in_specs=[SMEM] * 3 + [VMEM] * 6,
         out_specs=VMEM,
+        scratch_shapes=[pltpu.VMEM((3, 4, VEC, 128), F32)],
         cost_estimate=cost(4 * 128 * 160 * 1024, 2 << 20),
         name="decode",
     )(refresh, me, level, gathered, base, up, down, weight, bias)
@@ -431,12 +400,11 @@
         state = attend(queries, values_y, state, (keys_y,))
         values_far, far_a, far_b, state = together((values_far, far_a, far_b, state))
         state = attend(queries, values_far, state, (far_a, far_b))
-        part = merge_second(exchange(state, ("yl", "xl")))
-        term = merge_last(exchange(part, "z"))
+        term = merge(exchange(state, ("yl", "xl", "z")))
 
     with jax.named_scope("velocity"):
         term = jnp.sum(lax.all_gather(term, HEAD), axis=0)
-        gathered = exchange(spread_out(term, 16), ("yh", "yl", "xh", "xl"))
+        gathered = exchange(spread_out(term, PATCHES), PATCH)
 
     with jax.named_scope("decode"):
         weight = conv_weight.transpose(1, 2, 3, 0)

time: 178 us -> 163 us (0.916)
  Pallas kernels: 57.7 us -> 33.5 us
  blocking collectives: 50.3 us -> 55.6 us
  waiting for transfers between devices: 12.8 us -> 16.9 us
    pallas_call x3 -> x2, Pallas kernels: 28.6 us -> 4.32 us  [the longest x1 2.25 us: merge(): pl.pallas_call(merge_kernel, out_shape=jax.ShapeDtypeStruct((SLOTS // 2 *...]
    all_to_all x3 -> x2, blocking collectives: 44.2 us -> 50.2 us  [exchange(): return lax.all_to_all(value, axis, 0, 0)]
    ppermute x7, waiting for transfers between devices: 0.54 us -> 4.58 us  [mirror(): return lax.ppermute(value, PATCH, pairs)]
  transfers between devices with their start and end apart: 11 -> 11, of which waited for: 5 -> 6; matrix products, arithmetic and copies ran while one was open for 8% -> 8% of each run, Pallas kernels for 25% -> 13%
where the time goes in v4:
time: 163 us; the launch traced here: 162 us
  blocking collectives  55.6 us (34%)
  starting transfers between devices  39.1 us (24%)
  Pallas kernels  33.5 us (21%)
  waiting for transfers between devices  16.9 us (10%)
  local copies, waits for them, and re-layouts  6.74 us (4%)
  matrix products  5.75 us (4%)
  other arithmetic  3.51 us (2%)
    all_to_all x2, blocking collectives, exchange(): return lax.all_to_all(value, axis, 0, 0)  50.2 us
    pallas_call x4, Pallas kernels, attend(): pl.pallas_call(functools.partial(attend_kernel, first, last), out_shape=o...  20.1 us
    all_to_all x2, starting transfers between devices, exchange(): return lax.all_to_all(value, axis, 0, 0)  18.2 us
    ppermute x7, starting transfers between devices, mirror(): return lax.ppermute(value, PATCH, pairs)  14.7 us
    all_to_all x2, waiting for transfers between devices, exchange(): return lax.all_to_all(value, axis, 0, 0)  10.7 us
    all_gather x1, blocking collectives, on_device(): term = jnp.sum(lax.all_gather(term, HEAD), axis=0)  5.39 us
    ppermute x1, starting transfers between devices, on_device(): lax.ppermute(edge_last, PATCH, [(p, p + 1) for p in range(PATCHES - 1)])  4.92 us
    ppermute x7, waiting for transfers between devices, mirror(): return lax.ppermute(value, PATCH, pairs)  4.58 us
  transfers between devices with their start and end apart: 11, of which 6 were waited for; matrix products, arithmetic and copies ran while one was open for 8% of the time, Pallas kernels for 13%

profile of v4, /device:TPU:32, one launch (start us, length us, event | category | flops | bytes accessed | tf_op | source)
XLA Modules:
  0.0 161.8 jit_solution(2529548757003300930)
XLA Ops:
  0.0 2.2 %slice_bitcast_fusion = bf16[64,8,768]{2,1,0:T(8,128)(2,1)} fusion(bf16[512,3,768]{2,0,1:T(8,128)(2,1)} %param.13), kind=kLoop, calls=%fused_computation.13 | loop fusion | bytes 1572864 | tf_op jit(solution)/shard_map/queries/reshape;queries/squeeze | solution.py:358
  2.3 13.9 %all-to-all-start = ((bf16[64,8,768]{2,1,0:T(8,128)(2,1)}), bf16[64,8,768]{2,1,0:T(8,128)(2,1)}, u32[]{:S(2)}, u32[]{:S(2)}) async-start(bf16[64,8,768]{2,1,0:T(8,128)(2,1)} %slice_bitcast_fusion), calls=%async_computation | async-start | bytes 1572864 | tf_op jit(solution)/shard_map/queries/all_to_all | solution.py:40
  20.5 4.9 %collective-permute-start = (f32[16,1024]{1,0:T(8,128)}, f32[16,1024]{1,0:T(8,128)}, u32[]{:S(2)}, u32[]{:S(2)}) collective-permute-start(f32[16,1024]{1,0:T(8,128)} %get-tuple-element.44), channel_id=1, source_target_pairs={{0,4},{4,8},{8,12},{12,16},{16,20},{20,24},{24,28},{28,32},{32,36}... | collective-permute-start | bytes 196616 | tf_op jit(solution)/shard_map/latent_base/ppermute | solution.py:376
  27.4 4.4 %fusion.8 = (bf16[512,1,768]{2,1,0:T(2,128)(2,1)S(1)}, bf16[512,1,768]{2,1,0:T(2,128)(2,1)S(1)}) fusion(bf16[512,2,768]{2,1,0:T(2,128)(2,1)} %param.14), kind=kLoop, calls=%fused_computation.17 | loop fusion | bytes 3145728 | tf_op jit(solution)/shard_map/keys_values/slice | solution.py:365
  35.4 8.0 %all-to-all-done.got_ref = bf16[64,8,768]{2,1,0:T(8,128)(2,1)} async-done(((bf16[64,8,768]{2,1,0:T(8,128)(2,1)}), bf16[64,8,768]{2,1,0:T(8,128)(2,1)}, u32[]{:S(2)}, u32[]{:S(2)}) %all-to-all-start) | async-done | bytes 786464 | tf_op jit(solution)/shard_map/queries/all_to_all | solution.py:40
  43.4 2.1 %select.1 = bf16[16,32,768]{2,1,0:T(8,128)(2,1)} custom-call(s32[4]{0:T(128)} %refresh_ref.5, bf16[64,8,768]{2,1,0:T(8,128)(2,1)} %all-to-all-done.got_ref), custom_call_target="tpu_custom_call" | custom-call | bytes 835584 | tf_op jit(solution)/shard_map/queries/select/pallas_call | solution.py:65
  45.5 4.3 %all-to-all-start.1 = ((bf16[16,32,768]{2,1,0:T(8,128)(2,1)}), bf16[16,32,768]{2,1,0:T(8,128)(2,1)}, u32[]{:S(2)}, u32[]{:S(2)}) async-start(bf16[16,32,768]{2,1,0:T(8,128)(2,1)} %select.1), calls=%async_computation.1 | async-start | bytes 1572864 | tf_op jit(solution)/shard_map/queries/all_to_all | solution.py:40
  50.8 2.3 %collective-permute-start.4 = (bf16[512,768]{1,0:T(8,128)(2,1)}, bf16[512,768]{1,0:T(8,128)(2,1)}, u32[]{:S(2)}, u32[]{:S(2)}) collective-permute-start(bf16[512,768]{1,0:T(8,128)(2,1)} %get-tuple-element.80.refs_2_), channel_id=1, source_target_pairs={{0,192},{4,196},{8,200},{12,204},{16,208},{20,212},{24,216},{28,22... | collective-permute-start | bytes 2359304 | tf_op jit(solution)/shard_map/keys_values/ppermute | solution.py:32
  53.3 4.0 %fusion.1 = f32[128,768]{1,0:T(8,128)S(1)} fusion(bf16[768,3072]{1,0:T(8,128)(2,1)} %param.17, bf16[64,3072]{1,0:T(8,128)(2,1)S(1)} %get-tuple-element.84, bf16[64,3072]{1,0:T(8,128)(2,1)S(1)} %get-tuple-element.83), kind=kOutput, calls=%fused_computation.4 | convolution fusion | flops 605552640 | bytes 5898240 | tf_op jit(solution)/shard_map/keys_values/dot_general | solution.py:387
  58.0 2.3 %values.1.refs_1_ = bf16[384,512]{1,0:T(8,128)(2,1)} custom-call(bf16[512,768]{1,0:T(8,128)(2,1)} %get-tuple-element.79.v_ref, f32[64,768]{1,0:T(8,128)} %slice_add_fusion.w_ref), custom_call_target="tpu_custom_call" | custom-call | flops 100663296 | bytes 1572864 | tf_op jit(solution)/shard_map/keys_values/values/pallas_call | solution.py:85
  63.5 2.7 %collective-permute-start.2 = (bf16[384,512]{1,0:T(8,128)(2,1)}, bf16[384,512]{1,0:T(8,128)(2,1)S(1)}, u32[]{:S(2)}, u32[]{:S(2)}) collective-permute-start(bf16[384,512]{1,0:T(8,128)(2,1)} %values.1.refs_1_), channel_id=1, source_target_pairs={{0,240},{4,244},{8,248},{12,252},{16,224},{20,228},{24,232},{28,23... | collective-permute-start | bytes 1179656 | tf_op jit(solution)/shard_map/keys_values/ppermute | solution.py:32
  66.2 2.7 %all-to-all-done.1 = bf16[16,32,768]{2,1,0:T(8,128)(2,1)} async-done(((bf16[16,32,768]{2,1,0:T(8,128)(2,1)}), bf16[16,32,768]{2,1,0:T(8,128)(2,1)}, u32[]{:S(2)}, u32[]{:S(2)}) %all-to-all-start.1) | async-done | bytes 786464 | tf_op jit(solution)/shard_map/queries/all_to_all | solution.py:40
  68.9 4.8 %attend.4 = (f32[384,512]{1,0:T(8,128)}, f32[8,512]{1,0:T(8,128)}, f32[8,512]{1,0:T(8,128)}) custom-call(bf16[512,768]{1,0:T(8,128)(2,1)} %bitcast.5.refs_0_, bf16[384,512]{1,0:T(8,128)(2,1)} %values.1.refs_1_, bf16[512,768]{1,0:T(8,128)(2,1)} %get-tuple-element.80.refs_2_), custom_call_target="tpu_custom_call" | custom-call | flops 805306368 | bytes 3145728 | tf_op jit(solution)/shard_map/attention/attend/pallas_call | solution.py:223
  73.7 2.1 %halves.1 = (bf16[256,768]{1,0:T(8,128)(2,1)}, bf16[256,768]{1,0:T(8,128)(2,1)}) custom-call(bf16[512,768]{1,0:T(8,128)(2,1)} %collective-permute-done.3.x_ref.refs_5_, bf16[512,768]{1,0:T(8,128)(2,1)} %collective-permute-done.4.y_ref.refs_5_), custom_call_target="tpu_custom_call" | custom-call | bytes 1572864 | tf_op jit(solution)/shard_map/attention/halves/pallas_call | solution.py:101
  75.8 4.2 %collective-permute-start.5 = (bf16[256,768]{1,0:T(8,128)(2,1)}, bf16[256,768]{1,0:T(8,128)(2,1)}, u32[]{:S(2)}, u32[]{:S(2)}) collective-permute-start(bf16[256,768]{1,0:T(8,128)(2,1)} %get-tuple-element.55), channel_id=1, source_target_pairs={{0,192},{4,196},{8,200},{12,204},{16,208},{20,212},{24,216},{28,22... | collective-permute-start | bytes 1179656 | tf_op jit(solution)/shard_map/attention/ppermute | solution.py:32
  81.2 5.1 %attend.5 = (f32[384,512]{1,0:T(8,128)}, f32[8,512]{1,0:T(8,128)}, f32[8,512]{1,0:T(8,128)}) custom-call(bf16[512,768]{1,0:T(8,128)(2,1)} %bitcast.5.refs_0_, bf16[384,512]{1,0:T(8,128)(2,1)} %collective-permute-done.8.refs_1_, f32[384,512]{1,0:T(8,128)} %get-tuple-element.57.refs_2_, f32[8,512]{1,0:T(8,128)} %get-tuple-element.58.refs_3_, ...), custom_call_target="tpu_custom_call" | custom-call | flops 805306368 | bytes 3145728 | tf_op jit(solution)/shard_map/attention/attend/pallas_call | solution.py:223
  88.3 5.1 %attend.6 = (f32[384,512]{1,0:T(8,128)}, f32[8,512]{1,0:T(8,128)}, f32[8,512]{1,0:T(8,128)}) custom-call(bf16[512,768]{1,0:T(8,128)(2,1)} %bitcast.5.refs_0_, bf16[384,512]{1,0:T(8,128)(2,1)} %collective-permute-done.7.refs_1_, f32[384,512]{1,0:T(8,128)} %get-tuple-element.64.refs_2_, f32[8,512]{1,0:T(8,128)} %get-tuple-element.65.refs_3_, ...), custom_call_target="tpu_custom_call" | custom-call | flops 805306368 | bytes 3145728 | tf_op jit(solution)/shard_map/attention/attend/pallas_call | solution.py:223
  93.4 2.7 %collective-permute-done.5.refs_5_ = bf16[256,768]{1,0:T(8,128)(2,1)} collective-permute-done((bf16[256,768]{1,0:T(8,128)(2,1)}, bf16[256,768]{1,0:T(8,128)(2,1)}, u32[]{:S(2)}, u32[]{:S(2)}) %collective-permute-start.5) | collective-permute-done | bytes 393248 | tf_op jit(solution)/shard_map/attention/ppermute | solution.py:32
  96.1 5.1 %attend.7 = bf16[16,32,512]{2,1,0:T(8,128)(2,1)} custom-call(bf16[512,768]{1,0:T(8,128)(2,1)} %bitcast.5.refs_0_, bf16[384,512]{1,0:T(8,128)(2,1)} %copy-done.3, f32[384,512]{1,0:T(8,128)} %get-tuple-element.71.refs_2_, f32[8,512]{1,0:T(8,128)} %get-tuple-element.72.refs_3_, f32[8,512]{1,0:T(8,128)} %get-tuple-element.73.refs_4_, ...), custom_call_target="tpu_custom_call" | custom-call | flops 805306368 | bytes 3145728 | tf_op jit(solution)/shard_map/attention/attend/pallas_call | solution.py:223
  101.2 21.7 %all_to_all.20.p_ref = bf16[16,32,512]{2,1,0:T(8,128)(2,1)} all-to-all(bf16[16,32,512]{2,1,0:T(8,128)(2,1)} %attend.7), channel_id=1, replica_groups=mesh['yh'=2,'yl'=2,'xh'=2,'xl'=2,'z'=4,'w'=2,'c'=2] {'yl','xl','z'}, dimensions={0} | all-to-all | bytes 1048576 | tf_op jit(solution)/shard_map/attention/all_to_all | solution.py:40
  122.9 2.2 %merge.1 = f32[16,128]{1,0:T(8,128)} custom-call(bf16[16,32,512]{2,1,0:T(8,128)(2,1)} %all_to_all.20.p_ref), custom_call_target="tpu_custom_call" | custom-call | flops 33554432 | bytes 524288 | tf_op jit(solution)/shard_map/attention/merge/pallas_call | solution.py:258
  125.2 5.4 %all-gather = f32[64,128]{1,0:T(8,128)S(1)} all-gather(f32[16,128]{1,0:T(8,128)} %merge.1), channel_id=2, replica_groups=mesh['yh'=2,'yl'=2,'xh'=2,'xl'=2,'z'=4,'w'=2,'c'=2] {'w','c'}, dimensions={0}, use_global_device_ids=true | all-gather | bytes 40960 | tf_op jit(solution)/shard_map/velocity/all_gather | solution.py:406
  130.6 28.5 %all_to_all.21.v_ref = f32[64,16,128]{2,1,0:T(8,128)} all-to-all(f32[64,16,128]{2,1,0:T(8,128)S(1)} %broadcast_in_dim.2), channel_id=1, replica_groups=mesh['yh'=2,'yl'=2,'xh'=2,'xl'=2,'z'=4,'w'=2,'c'=2] {'yh','yl','xh','xl'..., dimensions={0} | all-to-all | bytes 1048576 | tf_op jit(solution)/shard_map/velocity/all_to_all | solution.py:40
  159.1 2.7 %decode.1 = bf16[2,128,1024]{2,1,0:T(8,128)(2,1)} custom-call(s32[4]{0:T(128)} %refresh_ref.5, s32[1]{0:T(128)} %bitcast.me_ref, f32[1]{0:T(128)S(6)} %copy.24.level_ref, f32[64,16,128]{2,1,0:T(8,128)} %all_to_all.21.v_ref, f32[32,1024]{1,0:T(8,128)} %get-tuple-element.76.base_ref, f32[16,1024]{1,0:T(8,128)} %collective-permute-done.up_ref, ...), custom_call_target="tpu_custom_call" | custom-call | flops 83886080 | bytes 2097152 | tf_op jit(solution)/shard_map/decode/decode/pallas_call | solution.py:327
  (35 shorter events, 17.5 us)
Async XLA Ops:
  0.0 16.8 %copy-start = (bf16[512,3072]{1,0:T(8,128)(2,1)S(1)}, bf16[512,3072]{1,0:T(8,128)(2,1)}, u32[]{:S(2)}) copy-start(bf16[512,3072]{1,0:T(8,128)(2,1)} %param.15) | copy-start | bytes 9437188
  0.0 16.8 %copy-start.2 = (bf16[3072,64]{0,1:T(8,128)(2,1)S(1)}, bf16[3072,64]{0,1:T(8,128)(2,1)}, u32[]{:S(2)}) copy-start(bf16[3072,64]{0,1:T(8,128)(2,1)} %param.18) | copy-start | bytes 1179652
  0.0 16.9 %copy-start.6 = (f32[64]{0:T(128)S(1)}, f32[64]{0:T(128)}, u32[]{:S(2)}) copy-start(f32[64]{0:T(128)} %param.19) | copy-start | bytes 772
  2.3 41.1 %all-to-all-start = ((bf16[64,8,768]{2,1,0:T(8,128)(2,1)}), bf16[64,8,768]{2,1,0:T(8,128)(2,1)}, u32[]{:S(2)}, u32[]{:S(2)}) async-start(bf16[64,8,768]{2,1,0:T(8,128)(2,1)} %slice_bitcast_fusion), calls=%async_computation | async-start | bytes 1572864 | tf_op jit(solution)/shard_map/queries/all_to_all | solution.py:40
  16.2 10.6 %copy-start.5 = (s32[4]{0:T(128)S(1)}, s32[4]{0:T(128)}, u32[]{:S(2)}) copy-start(s32[4]{0:T(128)} %refresh_ref.5) | copy-start | bytes 52
  20.5 14.5 %collective-permute-start = (f32[16,1024]{1,0:T(8,128)}, f32[16,1024]{1,0:T(8,128)}, u32[]{:S(2)}, u32[]{:S(2)}) collective-permute-start(f32[16,1024]{1,0:T(8,128)} %get-tuple-element.44), channel_id=1, source_target_pairs={{0,4},{4,8},{8,12},{12,16},{16,20},{20,24},{24,28},{28,32},{32,36}... | collective-permute-start | bytes 196616 | tf_op jit(solution)/shard_map/latent_base/ppermute | solution.py:376
  25.4 10.0 %collective-permute-start.1 = (f32[16,1024]{1,0:T(8,128)}, f32[16,1024]{1,0:T(8,128)}, u32[]{:S(2)}, u32[]{:S(2)}) collective-permute-start(f32[16,1024]{1,0:T(8,128)} %get-tuple-element.45), channel_id=1, source_target_pairs={{4,0},{8,4},{12,8},{16,12},{20,16},{24,20},{28,24},{32,28},{36,32}... | collective-permute-start | bytes 196616 | tf_op jit(solution)/shard_map/latent_base/ppermute | solution.py:377
  27.4 4.4 %copy-start.1 = (bf16[512,3,768]{2,0,1:T(8,128)(2,1)S(1)}, bf16[512,3,768]{2,0,1:T(8,128)(2,1)}, u32[]{:S(2)}) copy-start(bf16[512,3,768]{2,0,1:T(8,128)(2,1)} %param.13) | copy-start | bytes 7077892
  33.8 19.3 %copy-start.4 = (f32[3072]{0:T(1024)S(1)}, f32[3072]{0:T(1024)}, u32[]{:S(2)}) copy-start(f32[3072]{0:T(1024)} %param.20) | copy-start | bytes 36868
  45.5 23.4 %all-to-all-start.1 = ((bf16[16,32,768]{2,1,0:T(8,128)(2,1)}), bf16[16,32,768]{2,1,0:T(8,128)(2,1)}, u32[]{:S(2)}, u32[]{:S(2)}) async-start(bf16[16,32,768]{2,1,0:T(8,128)(2,1)} %select.1), calls=%async_computation.1 | async-start | bytes 1572864 | tf_op jit(solution)/shard_map/queries/all_to_all | solution.py:40
  49.8 23.9 %collective-permute-start.3 = (bf16[512,768]{1,0:T(8,128)(2,1)}, bf16[512,768]{1,0:T(8,128)(2,1)}, u32[]{:S(2)}, u32[]{:S(2)}) collective-permute-start(bf16[512,768]{1,0:T(8,128)(2,1)} %get-tuple-element.80.refs_2_), channel_id=1, source_target_pairs={{0,48},{4,52},{8,56},{12,60},{16,32},{20,36},{24,40},{28,44},{32,1... | collective-permute-start | bytes 2359304 | tf_op jit(solution)/shard_map/keys_values/ppermute | solution.py:32
  50.8 22.9 %collective-permute-start.4 = (bf16[512,768]{1,0:T(8,128)(2,1)}, bf16[512,768]{1,0:T(8,128)(2,1)}, u32[]{:S(2)}, u32[]{:S(2)}) collective-permute-start(bf16[512,768]{1,0:T(8,128)(2,1)} %get-tuple-element.80.refs_2_), channel_id=1, source_target_pairs={{0,192},{4,196},{8,200},{12,204},{16,208},{20,212},{24,216},{28,22... | collective-permute-start | bytes 2359304 | tf_op jit(solution)/shard_map/keys_values/ppermute | solution.py:32
  60.3 21.0 %collective-permute-start.8 = (bf16[384,512]{1,0:T(8,128)(2,1)}, bf16[384,512]{1,0:T(8,128)(2,1)}, u32[]{:S(2)}, u32[]{:S(2)}) collective-permute-start(bf16[384,512]{1,0:T(8,128)(2,1)} %values.1.refs_1_), channel_id=1, source_target_pairs={{0,48},{4,52},{8,56},{12,60},{16,32},{20,36},{24,40},{28,44},{32,1... | collective-permute-start | bytes 1179656 | tf_op jit(solution)/shard_map/keys_values/ppermute | solution.py:32
  61.8 26.5 %collective-permute-start.7 = (bf16[384,512]{1,0:T(8,128)(2,1)}, bf16[384,512]{1,0:T(8,128)(2,1)}, u32[]{:S(2)}, u32[]{:S(2)}) collective-permute-start(bf16[384,512]{1,0:T(8,128)(2,1)} %values.1.refs_1_), channel_id=1, source_target_pairs={{0,192},{4,196},{8,200},{12,204},{16,208},{20,212},{24,216},{28,22... | collective-permute-start | bytes 1179656 | tf_op jit(solution)/shard_map/keys_values/ppermute | solution.py:32
  63.5 29.9 %collective-permute-start.2 = (bf16[384,512]{1,0:T(8,128)(2,1)}, bf16[384,512]{1,0:T(8,128)(2,1)S(1)}, u32[]{:S(2)}, u32[]{:S(2)}) collective-permute-start(bf16[384,512]{1,0:T(8,128)(2,1)} %values.1.refs_1_), channel_id=1, source_target_pairs={{0,240},{4,244},{8,248},{12,252},{16,224},{20,228},{24,232},{28,23... | collective-permute-start | bytes 1179656 | tf_op jit(solution)/shard_map/keys_values/ppermute | solution.py:32
  75.8 20.3 %collective-permute-start.5 = (bf16[256,768]{1,0:T(8,128)(2,1)}, bf16[256,768]{1,0:T(8,128)(2,1)}, u32[]{:S(2)}, u32[]{:S(2)}) collective-permute-start(bf16[256,768]{1,0:T(8,128)(2,1)} %get-tuple-element.55), channel_id=1, source_target_pairs={{0,192},{4,196},{8,200},{12,204},{16,208},{20,212},{24,216},{28,22... | collective-permute-start | bytes 1179656 | tf_op jit(solution)/shard_map/attention/ppermute | solution.py:32
  79.9 16.2 %collective-permute-start.6 = (bf16[256,768]{1,0:T(8,128)(2,1)}, bf16[256,768]{1,0:T(8,128)(2,1)}, u32[]{:S(2)}, u32[]{:S(2)}) collective-permute-start(bf16[256,768]{1,0:T(8,128)(2,1)} %get-tuple-element.56), channel_id=1, source_target_pairs={{0,48},{4,52},{8,56},{12,60},{16,32},{20,36},{24,40},{28,44},{32,1... | collective-permute-start | bytes 1179656 | tf_op jit(solution)/shard_map/attention/ppermute | solution.py:32
  93.4 2.7 %copy-start.3 = (bf16[384,512]{1,0:T(8,128)(2,1)}, bf16[384,512]{1,0:T(8,128)(2,1)S(1)}, u32[]{:S(2)}) copy-start(bf16[384,512]{1,0:T(8,128)(2,1)S(1)} %collective-permute-done.2.refs_1_) | copy-start | bytes 1179652

commit v5 on v2

--- a/solution.py
+++ b/solution.py
@@ -91,6 +91,25 @@
         cost_estimate=cost(4 * KEYS * VEC * HEAD_DIM * HEADS_HERE, 4 * KEYS * 768),
         name="values",
     )(value_rows, mixed)
+
+
+def halves_kernel(x_ref, y_ref, a_ref, b_ref):
+    a_ref[...] = x_ref[...]
+    b_ref[...] = y_ref[...]
+
+
+def halves(keys_x, keys_y):
+    block = (KEYS // 2, keys_x.shape[1])
+    whole = pl.BlockSpec(block, lambda i: (0, 0))
+    return pl.pallas_call(
+        halves_kernel,
+        grid=(1,),
+        in_specs=[whole, pl.BlockSpec(block, lambda i: (1, 0))],
+        out_specs=(whole, whole),
+        out_shape=(jax.ShapeDtypeStruct(block, BF16),) * 2,
+        cost_estimate=cost(0, 2 * KEYS * keys_x.shape[1] * 2),
+        name="halves",
+    )(keys_x, keys_y)
 
 
 def base_kernel(refresh_ref, me_ref, level_ref, plain_ref, noisy_ref, cache_ref, o_ref, *rest):
@@ -269,8 +288,9 @@
     )(parts)
 
 
-def decode_kernel(refresh_ref, me_ref, level_ref, v_ref, base_ref, up_ref, down_ref, w_ref, b_ref, o_ref):
+def decode_kernel(refresh_ref, me_ref, level_ref, v_ref, base_ref, up_ref, down_ref, w_ref, b_ref, o_ref, all_ref):
     level, me = level_ref[0], me_ref[0]
+    all_ref[...] = v_ref[...].astype(F32)
     row = lax.broadcasted_iota(jnp.int32, (512, 128), 0)
     col = lax.broadcasted_iota(jnp.int32, (512, 128), 1)
     lane = row % 128
@@ -290,13 +310,11 @@
                 pieces = []
                 for xs in (pair * 2, pair * 2 + 1):
                     for b in range(2):
-                        parts = [v_ref[ys * 4 + xs, pl.ds(kind * 2 + b, LAT_CH, 4), :] for kind in kinds]
+                        parts = [all_ref[ys * 4 + xs, pl.ds(kind * 2 + b, LAT_CH, 4), :] for kind in kinds]
                         pieces.append(jnp.concatenate(parts, axis=0))
                 stacked.append(jnp.concatenate(pieces, axis=1))
-        high, low = split(jnp.concatenate(stacked, axis=0))
-        field = jnp.dot(high, choose, preferred_element_type=F32) + jnp.dot(
-            low, choose, preferred_element_type=F32
-        )
+        left = jnp.concatenate(stacked, axis=0).astype(BF16)
+        field = jnp.dot(left, choose, preferred_element_type=F32)
         field = jnp.concatenate([field[i * count : (i + 1) * count] for i in range(8)], axis=1)
         return jnp.where(on > 0, field, 0.0)
 
@@ -335,6 +353,7 @@
         out_shape=jax.ShapeDtypeStruct((2, weight.shape[3], COLS), BF16),
         in_specs=[SMEM] * 3 + [VMEM] * 6,
         out_specs=VMEM,
+        scratch_shapes=[pltpu.VMEM((16, VEC, 128), F32)],
         cost_estimate=cost(4 * 128 * 160 * 1024, 2 << 20),
         name="decode",
     )(refresh, me, level, gathered, base, up, down, weight, bias)
@@ -368,51 +387,50 @@
         refreshed = jnp.any(refresh == me)
         keys = jnp.where(refreshed, fresh_qkv[:, 1], kv_cache[:, 0])
         value_rows = jnp.where(refreshed, fresh_qkv[:, 2], kv_cache[:, 1])
-        keys_x, keys_y = mirror(keys, 0, 1), mirror(keys, 1, 0)
-
-    with jax.named_scope("latent_base"):
-        plain = lax.dot_general(
-            final_weight, hidden, (((0,), (1,)), ((), ())), preferred_element_type=F32
-        )
-        plain = plain + final_bias[:, None]
-        base, edge_first, edge_last = latent_base(
-            refresh, here, noise_level, plain, noisy_latent, velocity_cache
-        )
-        up = lax.ppermute(edge_last, PATCH, [(p, p + 1) for p in range(PATCHES - 1)])
-        down = lax.ppermute(edge_first, PATCH, [(p + 1, p) for p in range(PATCHES - 1)])
-
-    with jax.named_scope("queries"):
-        got, base, up, down, keys_x, keys_y = together((got, base, up, down, keys_x, keys_y))
-        held = exchange(select(refresh, got), ("yl", "xl", "z"))
-
-    with jax.named_scope("keys_values"):
         gated = final_weight.T.astype(F32) * gate_scale[None, :]
         high = lax.reduce_precision(gated, 8, 7)
         both = jnp.concatenate([high, gated - high], axis=0).astype(BF16)
         mixed = lax.dot_general(both, out_weight, (((1,), (1,)), ((), ())), preferred_element_type=F32)
         values = project_values(value_rows, mixed[:VEC] + mixed[VEC:])
-        half = KEYS // 2
-        keys_far = mirror(keys_x[:half], 1, 0), mirror(keys_y[half:], 0, 1)
-        blocks = [
-            (values, (keys,)),
-            (mirror(values, 0, 1), (keys_x,)),
-            (mirror(values, 1, 0), (keys_y,)),
-            (mirror(values, 1, 1), keys_far),
-        ]
+
+    with jax.named_scope("queries"):
+        got, keys, values = together((got, keys, values))
+        held = exchange(select(refresh, got), ("yl", "xl", "z"))
+
+    with jax.named_scope("keys_values"):
+        keys_x, keys_y = mirror(keys, 0, 1), mirror(keys, 1, 0)
+        values_x, values_y, values_far = mirror(values, 0, 1), mirror(values, 1, 0), mirror(values, 1, 1)
 
     with jax.named_scope("attention"):
-        held, values = together((held, values))
         queries = held.reshape(16 * SLOTS * CHUNK, HEADS_HERE * HEAD_DIM)
-        state = None
-        for k, (values, keys) in enumerate(blocks):
-            if k:
-                values, keys, state = together((values, keys, state))
-            state = attend(queries, values, state, keys)
+        state = attend(queries, values, None, (keys,))
+        keys_x, keys_y, state = together((keys_x, keys_y, state))
+        far_a, far_b = halves(keys_x, keys_y)
+        far_a, far_b = mirror(far_a, 1, 0), mirror(far_b, 0, 1)
+        state = attend(queries, values_x, state, (keys_x,))
+        values_y, state = together((values_y, state))
+        state = attend(queries, values_y, state, (keys_y,))
+        values_far, far_a, far_b, state = together((values_far, far_a, far_b, state))
+        state = attend(queries, values_far, state, (far_a, far_b))
         part = merge_second(exchange(state, ("yl", "xl")))
-        term = merge_last(exchange(part, "z"))
+        part, hidden = together((part, hidden))
+        parts = exchange(part, "z")
+
+    with jax.named_scope("latent_base"):
+        plain = lax.dot_general(
+            final_weight, hidden, (((0,), (1,)), ((), ())), preferred_element_type=F32
+        )
+        plain = plain + final_bias[:, None]
+        base, edge_first, edge_last = latent_base(
+            refresh, here, noise_level, plain, noisy_latent, velocity_cache
+        )
+        up = lax.ppermute(edge_last, PATCH, [(p, p + 1) for p in range(PATCHES - 1)])
+        down = lax.ppermute(edge_first, PATCH, [(p + 1, p) for p in range(PATCHES - 1)])
 
     with jax.named_scope("velocity"):
-        term = jnp.sum(lax.all_gather(term, HEAD), axis=0)
+        parts, up, down = together((parts, up, down))
+        term = merge_last(parts)
+        term = jnp.sum(lax.all_gather(term, HEAD), axis=0).astype(BF16)
         gathered = exchange(spread_out(term, 16), ("yh", "yl", "xh", "xl"))
 
     with jax.named_scope("decode"):

time: 161 us -> 161 us (level)
  waiting for transfers between devices: 11.2 us -> 39.4 us
  blocking collectives: 51.9 us -> 31.8 us
  local copies, waits for them, and re-layouts: 10.8 us -> 4.58 us
  starting transfers between devices: 42 us -> 38.1 us
  Pallas kernels: 32.8 us -> 34.6 us
    all_to_all x2 -> x3, waiting for transfers between devices: 0.01 us -> 27.7 us  [exchange(): return lax.all_to_all(value, axis, 0, 0)]
    all_to_all x3 -> x2, blocking collectives: 46.2 us -> 26.1 us  [exchange(): return lax.all_to_all(value, axis, 0, 0)]
    ppermute x7, starting transfers between devices: 16.4 us -> 8.51 us  [mirror(): return lax.ppermute(value, PATCH, pairs)]
    all_to_all x2 -> x3, starting transfers between devices: 19.5 us -> 23.5 us  [exchange(): return lax.all_to_all(value, axis, 0, 0)]
    slice x2 -> x0, local copies, waits for them, and re-layouts: 3.57 us -> none  [on_device(): keys_far = (mirror(keys_x[:half], 1, 0), mirror(keys_y[half:], 0, 1))]
    slice x1, local copies, waits for them, and re-layouts: 4.42 us -> 2.22 us  [on_device(): value_rows = jnp.where(refreshed, fresh_qkv[:, 2], kv_cache[:, 1])]
    pallas_call x0 -> x1, Pallas kernels: none -> 2.05 us  [halves(): pl.pallas_call(halves_kernel, grid=(1,), in_specs=[whole, pl.BlockSpec(bl...]
  transfers between devices with their start and end apart: 11 -> 12, of which waited for: 5 -> 6; matrix products, arithmetic and copies ran while one was open for 11% -> 7% of each run, Pallas kernels for 12% -> 13%
where the time goes in v5:
time: 161 us; the launch traced here: 159 us
  waiting for transfers between devices  39.4 us (24%)
  starting transfers between devices  38.1 us (24%)
  Pallas kernels  34.6 us (21%)
  blocking collectives  31.8 us (20%)
  matrix products  5.87 us (4%)
  local copies, waits for them, and re-layouts  4.58 us (3%)
  other arithmetic  3.51 us (2%)
    all_to_all x3, waiting for transfers between devices, exchange(): return lax.all_to_all(value, axis, 0, 0)  27.7 us
    all_to_all x2, blocking collectives, exchange(): return lax.all_to_all(value, axis, 0, 0)  26.1 us
    all_to_all x3, starting transfers between devices, exchange(): return lax.all_to_all(value, axis, 0, 0)  23.5 us
    pallas_call x4, Pallas kernels, attend(): pl.pallas_call(functools.partial(attend_kernel, first, last), out_shape=o...  19.9 us
    ppermute x7, starting transfers between devices, mirror(): return lax.ppermute(value, PATCH, pairs)  8.51 us
    ppermute x1, waiting for transfers between devices, on_device(): lax.ppermute(edge_first, PATCH, [(p + 1, p) for p in range(PATCHES - 1)])  5.83 us
    all_gather x1, blocking collectives, on_device(): term = jnp.sum(lax.all_gather(term, HEAD), axis=0).astype(BF16)  5.71 us
    ppermute x7, waiting for transfers between devices, mirror(): return lax.ppermute(value, PATCH, pairs)  4.99 us
  transfers between devices with their start and end apart: 12, of which 6 were waited for; matrix products, arithmetic and copies ran while one was open for 7% of the time, Pallas kernels for 13%

profile of v5, /device:TPU:32, one launch (start us, length us, event | category | flops | bytes accessed | tf_op | source)
XLA Modules:
  0.0 158.7 jit_solution(8024828988740335539)
XLA Ops:
  0.0 2.3 %slice_bitcast_fusion = bf16[64,8,768]{2,1,0:T(8,128)(2,1)} fusion(bf16[512,3,768]{2,0,1:T(8,128)(2,1)} %param.13), kind=kLoop, calls=%fused_computation.14 | loop fusion | bytes 1572864 | tf_op jit(solution)/shard_map/queries/reshape;queries/squeeze | solution.py:382
  2.3 13.9 %all-to-all-start = ((bf16[64,8,768]{2,1,0:T(8,128)(2,1)}), bf16[64,8,768]{2,1,0:T(8,128)(2,1)}, u32[]{:S(2)}, u32[]{:S(2)}) async-start(bf16[64,8,768]{2,1,0:T(8,128)(2,1)} %slice_bitcast_fusion), calls=%async_computation | async-start | bytes 1572864 | tf_op jit(solution)/shard_map/queries/all_to_all | solution.py:43
  17.0 4.1 %fusion.2 = f32[128,768]{1,0:T(8,128)S(1)} fusion(bf16[768,3072]{1,0:T(8,128)(2,1)} %param.17, bf16[64,3072]{1,0:T(8,128)(2,1)S(1)} %get-tuple-element.88, bf16[64,3072]{1,0:T(8,128)(2,1)S(1)} %get-tuple-element.87), kind=kOutput, calls=%fused_computation.5 | convolution fusion | flops 605552640 | bytes 5898240 | tf_op jit(solution)/shard_map/keys_values/dot_general | solution.py:393
  21.9 2.2 %fusion.9 = (bf16[512,1,768]{2,1,0:T(2,128)(2,1)S(1)}, bf16[512,1,768]{2,1,0:T(2,128)(2,1)S(1)}) fusion(bf16[512,2,768]{2,1,0:T(2,128)(2,1)S(1)} %copy-done.1), kind=kLoop, calls=%fused_computation.18 | loop fusion | bytes 3145728 | tf_op jit(solution)/shard_map/keys_values/slice | solution.py:389
  26.1 2.3 %values.1.refs_1_ = bf16[384,512]{1,0:T(8,128)(2,1)} custom-call(bf16[512,768]{1,0:T(8,128)(2,1)} %get-tuple-element.83.v_ref, f32[64,768]{1,0:T(8,128)} %slice_add_fusion.w_ref), custom_call_target="tpu_custom_call" | custom-call | flops 100663296 | bytes 1572864 | tf_op jit(solution)/shard_map/keys_values/values/pallas_call | solution.py:88
  28.4 13.8 %all-to-all-done.got_ref = bf16[64,8,768]{2,1,0:T(8,128)(2,1)} async-done(((bf16[64,8,768]{2,1,0:T(8,128)(2,1)}), bf16[64,8,768]{2,1,0:T(8,128)(2,1)}, u32[]{:S(2)}, u32[]{:S(2)}) %all-to-all-start) | async-done | bytes 786464 | tf_op jit(solution)/shard_map/queries/all_to_all | solution.py:43
  42.2 2.1 %select.1 = bf16[16,32,768]{2,1,0:T(8,128)(2,1)} custom-call(s32[4]{0:T(128)} %refresh_ref.5, bf16[64,8,768]{2,1,0:T(8,128)(2,1)} %all-to-all-done.got_ref), custom_call_target="tpu_custom_call" | custom-call | bytes 835584 | tf_op jit(solution)/shard_map/queries/select/pallas_call | solution.py:68
  44.3 4.3 %all-to-all-start.1 = ((bf16[16,32,768]{2,1,0:T(8,128)(2,1)}), bf16[16,32,768]{2,1,0:T(8,128)(2,1)}, u32[]{:S(2)}, u32[]{:S(2)}) async-start(bf16[16,32,768]{2,1,0:T(8,128)(2,1)} %select.1), calls=%async_computation.1 | async-start | bytes 1572864 | tf_op jit(solution)/shard_map/queries/all_to_all | solution.py:43
  50.5 2.2 %collective-permute-start.6 = (bf16[384,512]{1,0:T(8,128)(2,1)}, bf16[384,512]{1,0:T(8,128)(2,1)}, u32[]{:S(2)}, u32[]{:S(2)}) collective-permute-start(bf16[384,512]{1,0:T(8,128)(2,1)} %values.1.refs_1_), channel_id=1, source_target_pairs={{0,48},{4,52},{8,56},{12,60},{16,32},{20,36},{24,40},{28,44},{32,1... | collective-permute-start | bytes 1179656 | tf_op jit(solution)/shard_map/keys_values/ppermute | solution.py:35
  52.8 2.3 %collective-permute-start.5 = (bf16[384,512]{1,0:T(8,128)(2,1)}, bf16[384,512]{1,0:T(8,128)(2,1)}, u32[]{:S(2)}, u32[]{:S(2)}) collective-permute-start(bf16[384,512]{1,0:T(8,128)(2,1)} %values.1.refs_1_), channel_id=1, source_target_pairs={{0,192},{4,196},{8,200},{12,204},{16,208},{20,212},{24,216},{28,22... | collective-permute-start | bytes 1179656 | tf_op jit(solution)/shard_map/keys_values/ppermute | solution.py:35
  56.5 13.9 %all-to-all-done.1 = bf16[16,32,768]{2,1,0:T(8,128)(2,1)} async-done(((bf16[16,32,768]{2,1,0:T(8,128)(2,1)}), bf16[16,32,768]{2,1,0:T(8,128)(2,1)}, u32[]{:S(2)}, u32[]{:S(2)}) %all-to-all-start.1) | async-done | bytes 786464 | tf_op jit(solution)/shard_map/queries/all_to_all | solution.py:43
  70.4 4.8 %attend.4 = (f32[384,512]{1,0:T(8,128)}, f32[8,512]{1,0:T(8,128)}, f32[8,512]{1,0:T(8,128)}) custom-call(bf16[512,768]{1,0:T(8,128)(2,1)} %bitcast.5.refs_0_, bf16[384,512]{1,0:T(8,128)(2,1)} %values.1.refs_1_, bf16[512,768]{1,0:T(8,128)(2,1)} %get-tuple-element.48.refs_2_), custom_call_target="tpu_custom_call" | custom-call | flops 805306368 | bytes 3145728 | tf_op jit(solution)/shard_map/attention/attend/pallas_call | solution.py:227
  75.2 2.0 %halves.1 = (bf16[256,768]{1,0:T(8,128)(2,1)}, bf16[256,768]{1,0:T(8,128)(2,1)}) custom-call(bf16[512,768]{1,0:T(8,128)(2,1)} %collective-permute-done.1.x_ref.refs_5_, bf16[512,768]{1,0:T(8,128)(2,1)} %collective-permute-done.2.y_ref.refs_5_), custom_call_target="tpu_custom_call" | custom-call | bytes 1572864 | tf_op jit(solution)/shard_map/attention/halves/pallas_call | solution.py:104
  79.1 5.1 %attend.5 = (f32[384,512]{1,0:T(8,128)}, f32[8,512]{1,0:T(8,128)}, f32[8,512]{1,0:T(8,128)}) custom-call(bf16[512,768]{1,0:T(8,128)(2,1)} %bitcast.5.refs_0_, bf16[384,512]{1,0:T(8,128)(2,1)} %collective-permute-done.6.refs_1_, f32[384,512]{1,0:T(8,128)} %get-tuple-element.56.refs_2_, f32[8,512]{1,0:T(8,128)} %get-tuple-element.57.refs_3_, ...), custom_call_target="tpu_custom_call" | custom-call | flops 805306368 | bytes 3145728 | tf_op jit(solution)/shard_map/attention/attend/pallas_call | solution.py:227
  84.2 5.1 %attend.6 = (f32[384,512]{1,0:T(8,128)}, f32[8,512]{1,0:T(8,128)}, f32[8,512]{1,0:T(8,128)}) custom-call(bf16[512,768]{1,0:T(8,128)(2,1)} %bitcast.5.refs_0_, bf16[384,512]{1,0:T(8,128)(2,1)} %collective-permute-done.5.refs_1_, f32[384,512]{1,0:T(8,128)} %get-tuple-element.63.refs_2_, f32[8,512]{1,0:T(8,128)} %get-tuple-element.64.refs_3_, ...), custom_call_target="tpu_custom_call" | custom-call | flops 805306368 | bytes 3145728 | tf_op jit(solution)/shard_map/attention/attend/pallas_call | solution.py:227
  89.4 3.7 %collective-permute-done.3.refs_5_ = bf16[256,768]{1,0:T(8,128)(2,1)} collective-permute-done((bf16[256,768]{1,0:T(8,128)(2,1)}, bf16[256,768]{1,0:T(8,128)(2,1)}, u32[]{:S(2)}, u32[]{:S(2)}) %collective-permute-start.3) | collective-permute-done | bytes 393248 | tf_op jit(solution)/shard_map/attention/ppermute | solution.py:35
  93.1 4.9 %attend.7 = bf16[4,416,128]{2,1,0:T(8,128)(2,1)} custom-call(bf16[512,768]{1,0:T(8,128)(2,1)} %bitcast.5.refs_0_, bf16[384,512]{1,0:T(8,128)(2,1)} %collective-permute-done.refs_1_, f32[384,512]{1,0:T(8,128)} %get-tuple-element.70.refs_2_, f32[8,512]{1,0:T(8,128)} %get-tuple-element.71.refs_3_, f32[8,512]{1,0:T(8,128)} %get-tuple-element.72.refs_4_, ...), custom_call_target="tpu_custom_call" | custom-call | flops 805306368 | bytes 3145728 | tf_op jit(solution)/shard_map/attention/attend/pallas_call | solution.py:227
  98.0 12.4 %all_to_all.25.p_ref = bf16[4,416,128]{2,1,0:T(8,128)(2,1)} all-to-all(bf16[4,416,128]{2,1,0:T(8,128)(2,1)} %attend.7), channel_id=1, replica_groups=mesh['yh'=2,'yl'=2,'xh'=2,'xl'=2,'z'=4,'w'=2,'c'=2] {'yl','xl'}, dimensions={0} | all-to-all | bytes 851968 | tf_op jit(solution)/shard_map/attention/all_to_all | solution.py:43
  112.3 5.3 %all-to-all-start.3 = ((bf16[4,416,128]{2,1,0:T(8,128)(2,1)}), bf16[4,416,128]{2,1,0:T(8,128)(2,1)}, u32[]{:S(2)}, u32[]{:S(2)}) async-start(bf16[4,416,128]{2,1,0:T(8,128)(2,1)} %merge_second.1), calls=%async_computation.3 | async-start | bytes 851968 | tf_op jit(solution)/shard_map/attention/all_to_all | solution.py:43
  121.9 4.8 %collective-permute-start.7 = (f32[16,1024]{1,0:T(8,128)}, f32[16,1024]{1,0:T(8,128)S(1)}, u32[]{:S(2)}, u32[]{:S(2)}) collective-permute-start(f32[16,1024]{1,0:T(8,128)} %get-tuple-element.77), channel_id=1, source_target_pairs={{0,4},{4,8},{8,12},{12,16},{16,20},{20,24},{24,28},{28,32},{32,36}... | collective-permute-start | bytes 196616 | tf_op jit(solution)/shard_map/latent_base/ppermute | solution.py:427
  128.9 5.8 %collective-permute-done.8.down_ref = f32[16,1024]{1,0:T(8,128)S(1)} collective-permute-done((f32[16,1024]{1,0:T(8,128)}, f32[16,1024]{1,0:T(8,128)S(1)}, u32[]{:S(2)}, u32[]{:S(2)}) %collective-permute-start.8) | collective-permute-done | bytes 65568 | tf_op jit(solution)/shard_map/latent_base/ppermute | solution.py:428
  136.5 5.7 %all-gather = f32[256,128]{1,0:T(8,128)S(1)} all-gather(f32[64,128]{1,0:T(8,128)} %merge_last.1), channel_id=2, replica_groups=mesh['yh'=2,'yl'=2,'xh'=2,'xl'=2,'z'=4,'w'=2,'c'=2] {'w','c'}, dimensions={0}, use_global_device_ids=true | all-gather | bytes 163840 | tf_op jit(solution)/shard_map/velocity/all_gather | solution.py:433
  142.3 13.7 %all_to_all.26.v_ref = bf16[16,64,128]{2,1,0:T(8,128)(2,1)} all-to-all(bf16[16,64,128]{2,1,0:T(8,128)(2,1)S(1)} %broadcast_in_dim.2), channel_id=1, replica_groups=mesh['yh'=2,'yl'=2,'xh'=2,'xl'=2,'z'=4,'w'=2,'c'=2] {'yh','yl','xh','xl'}, dimensions={0} | all-to-all | bytes 524288 | tf_op jit(solution)/shard_map/velocity/all_to_all | solution.py:43
  156.0 2.7 %decode.1 = bf16[2,128,1024]{2,1,0:T(8,128)(2,1)} custom-call(s32[4]{0:T(128)} %refresh_ref.5, s32[1]{0:T(128)} %bitcast.me_ref, f32[1]{0:T(128)S(6)} %copy.24.level_ref, bf16[16,64,128]{2,1,0:T(8,128)(2,1)} %all_to_all.26.v_ref, f32[32,1024]{1,0:T(8,128)} %get-tuple-element.80.base_ref, f32[16,1024]{1,0:T(8,128)} %copy-done.4, f32[16,1024]{1,0:T(8,128)} %copy-done.5, ...), custom_call_target="tpu_custom_call" | custom-call | flops 83886080 | bytes 2097152 | tf_op jit(solution)/shard_map/decode/decode/pallas_call | solution.py:351
  (42 shorter events, 18.3 us)
Async XLA Ops:
  0.0 118.3 %copy-start = (bf16[512,3072]{1,0:T(8,128)(2,1)S(1)}, bf16[512,3072]{1,0:T(8,128)(2,1)}, u32[]{:S(2)}) copy-start(bf16[512,3072]{1,0:T(8,128)(2,1)} %param.15) | copy-start | bytes 9437188
  0.0 16.2 %copy-start.3 = (bf16[3072,64]{0,1:T(8,128)(2,1)S(1)}, bf16[3072,64]{0,1:T(8,128)(2,1)}, u32[]{:S(2)}) copy-start(bf16[3072,64]{0,1:T(8,128)(2,1)} %param.18) | copy-start | bytes 1179652
  0.0 16.2 %copy-start.6 = (f32[3072]{0:T(1024)S(1)}, f32[3072]{0:T(1024)}, u32[]{:S(2)}) copy-start(f32[3072]{0:T(1024)} %param.20) | copy-start | bytes 36868
  0.0 16.4 %copy-start.7 = (s32[4]{0:T(128)S(1)}, s32[4]{0:T(128)}, u32[]{:S(2)}) copy-start(s32[4]{0:T(128)} %refresh_ref.5) | copy-start | bytes 52
  2.3 39.9 %all-to-all-start = ((bf16[64,8,768]{2,1,0:T(8,128)(2,1)}), bf16[64,8,768]{2,1,0:T(8,128)(2,1)}, u32[]{:S(2)}, u32[]{:S(2)}) async-start(bf16[64,8,768]{2,1,0:T(8,128)(2,1)} %slice_bitcast_fusion), calls=%async_computation | async-start | bytes 1572864 | tf_op jit(solution)/shard_map/queries/all_to_all | solution.py:43
  17.0 4.8 %copy-start.1 = (bf16[512,2,768]{2,1,0:T(2,128)(2,1)S(1)}, bf16[512,2,768]{2,1,0:T(2,128)(2,1)}, u32[]{:S(2)}) copy-start(bf16[512,2,768]{2,1,0:T(2,128)(2,1)} %param.14) | copy-start | bytes 4718596
  21.9 2.2 %copy-start.2 = (bf16[512,3,768]{2,0,1:T(8,128)(2,1)S(1)}, bf16[512,3,768]{2,0,1:T(8,128)(2,1)}, u32[]{:S(2)}) copy-start(bf16[512,3,768]{2,0,1:T(8,128)(2,1)} %param.13) | copy-start | bytes 7077892
  44.3 26.1 %all-to-all-start.1 = ((bf16[16,32,768]{2,1,0:T(8,128)(2,1)}), bf16[16,32,768]{2,1,0:T(8,128)(2,1)}, u32[]{:S(2)}, u32[]{:S(2)}) async-start(bf16[16,32,768]{2,1,0:T(8,128)(2,1)} %select.1), calls=%async_computation.1 | async-start | bytes 1572864 | tf_op jit(solution)/shard_map/queries/all_to_all | solution.py:43
  48.6 26.6 %collective-permute-start.1 = (bf16[512,768]{1,0:T(8,128)(2,1)}, bf16[512,768]{1,0:T(8,128)(2,1)}, u32[]{:S(2)}, u32[]{:S(2)}) collective-permute-start(bf16[512,768]{1,0:T(8,128)(2,1)} %get-tuple-element.48.refs_2_), channel_id=1, source_target_pairs={{0,48},{4,52},{8,56},{12,60},{16,32},{20,36},{24,40},{28,44},{32,1... | collective-permute-start | bytes 2359304 | tf_op jit(solution)/shard_map/keys_values/ppermute | solution.py:35
  49.0 26.1 %collective-permute-start.2 = (bf16[512,768]{1,0:T(8,128)(2,1)}, bf16[512,768]{1,0:T(8,128)(2,1)}, u32[]{:S(2)}, u32[]{:S(2)}) collective-permute-start(bf16[512,768]{1,0:T(8,128)(2,1)} %get-tuple-element.48.refs_2_), channel_id=1, source_target_pairs={{0,192},{4,196},{8,200},{12,204},{16,208},{20,212},{24,216},{28,22... | collective-permute-start | bytes 2359304 | tf_op jit(solution)/shard_map/keys_values/ppermute | solution.py:35
  50.5 28.5 %collective-permute-start.6 = (bf16[384,512]{1,0:T(8,128)(2,1)}, bf16[384,512]{1,0:T(8,128)(2,1)}, u32[]{:S(2)}, u32[]{:S(2)}) collective-permute-start(bf16[384,512]{1,0:T(8,128)(2,1)} %values.1.refs_1_), channel_id=1, source_target_pairs={{0,48},{4,52},{8,56},{12,60},{16,32},{20,36},{24,40},{28,44},{32,1... | collective-permute-start | bytes 1179656 | tf_op jit(solution)/shard_map/keys_values/ppermute | solution.py:35
  52.8 31.4 %collective-permute-start.5 = (bf16[384,512]{1,0:T(8,128)(2,1)}, bf16[384,512]{1,0:T(8,128)(2,1)}, u32[]{:S(2)}, u32[]{:S(2)}) collective-permute-start(bf16[384,512]{1,0:T(8,128)(2,1)} %values.1.refs_1_), channel_id=1, source_target_pairs={{0,192},{4,196},{8,200},{12,204},{16,208},{20,212},{24,216},{28,22... | collective-permute-start | bytes 1179656 | tf_op jit(solution)/shard_map/keys_values/ppermute | solution.py:35
  55.1 34.2 %collective-permute-start = (bf16[384,512]{1,0:T(8,128)(2,1)}, bf16[384,512]{1,0:T(8,128)(2,1)}, u32[]{:S(2)}, u32[]{:S(2)}) collective-permute-start(bf16[384,512]{1,0:T(8,128)(2,1)} %values.1.refs_1_), channel_id=1, source_target_pairs={{0,240},{4,244},{8,248},{12,252},{16,224},{20,228},{24,232},{28,23... | collective-permute-start | bytes 1179656 | tf_op jit(solution)/shard_map/keys_values/ppermute | solution.py:35
  77.2 15.9 %collective-permute-start.3 = (bf16[256,768]{1,0:T(8,128)(2,1)}, bf16[256,768]{1,0:T(8,128)(2,1)}, u32[]{:S(2)}, u32[]{:S(2)}) collective-permute-start(bf16[256,768]{1,0:T(8,128)(2,1)} %get-tuple-element.54), channel_id=1, source_target_pairs={{0,192},{4,196},{8,200},{12,204},{16,208},{20,212},{24,216},{28,22... | collective-permute-start | bytes 1179656 | tf_op jit(solution)/shard_map/attention/ppermute | solution.py:35
  77.8 15.3 %collective-permute-start.4 = (bf16[256,768]{1,0:T(8,128)(2,1)}, bf16[256,768]{1,0:T(8,128)(2,1)}, u32[]{:S(2)}, u32[]{:S(2)}) collective-permute-start(bf16[256,768]{1,0:T(8,128)(2,1)} %get-tuple-element.55), channel_id=1, source_target_pairs={{0,48},{4,52},{8,56},{12,60},{16,32},{20,36},{24,40},{28,44},{32,1... | collective-permute-start | bytes 1179656 | tf_op jit(solution)/shard_map/attention/ppermute | solution.py:35
  93.1 25.2 %copy-start.8 = (f32[64]{0:T(128)S(1)}, f32[64]{0:T(128)}, u32[]{:S(2)}) copy-start(f32[64]{0:T(128)} %param.19) | copy-start | bytes 772
  112.3 22.5 %all-to-all-start.3 = ((bf16[4,416,128]{2,1,0:T(8,128)(2,1)}), bf16[4,416,128]{2,1,0:T(8,128)(2,1)}, u32[]{:S(2)}, u32[]{:S(2)}) async-start(bf16[4,416,128]{2,1,0:T(8,128)(2,1)} %merge_second.1), calls=%async_computation.3 | async-start | bytes 851968 | tf_op jit(solution)/shard_map/attention/all_to_all | solution.py:43
  121.9 7.0 %collective-permute-start.7 = (f32[16,1024]{1,0:T(8,128)}, f32[16,1024]{1,0:T(8,128)S(1)}, u32[]{:S(2)}, u32[]{:S(2)}) collective-permute-start(f32[16,1024]{1,0:T(8,128)} %get-tuple-element.77), channel_id=1, source_target_pairs={{0,4},{4,8},{8,12},{12,16},{16,20},{20,24},{24,28},{28,32},{32,36}... | collective-permute-start | bytes 196616 | tf_op jit(solution)/shard_map/latent_base/ppermute | solution.py:427
  126.7 8.0 %collective-permute-start.8 = (f32[16,1024]{1,0:T(8,128)}, f32[16,1024]{1,0:T(8,128)S(1)}, u32[]{:S(2)}, u32[]{:S(2)}) collective-permute-start(f32[16,1024]{1,0:T(8,128)} %get-tuple-element.78), channel_id=1, source_target_pairs={{4,0},{8,4},{12,8},{16,12},{20,16},{24,20},{28,24},{32,28},{36,32}... | collective-permute-start | bytes 196616 | tf_op jit(solution)/shard_map/latent_base/ppermute | solution.py:428
  128.9 27.1 %copy-start.4 = (f32[16,1024]{1,0:T(8,128)}, f32[16,1024]{1,0:T(8,128)S(1)}, u32[]{:S(2)}) copy-start(f32[16,1024]{1,0:T(8,128)S(1)} %collective-permute-done.7.up_ref) | copy-start | bytes 196612
  134.8 21.2 %copy-start.5 = (f32[16,1024]{1,0:T(8,128)}, f32[16,1024]{1,0:T(8,128)S(1)}, u32[]{:S(2)}) copy-start(f32[16,1024]{1,0:T(8,128)S(1)} %collective-permute-done.8.down_ref) | copy-start | bytes 196612

commit v6 on v5

--- a/solution.py
+++ b/solution.py
@@ -393,8 +393,19 @@
         mixed = lax.dot_general(both, out_weight, (((1,), (1,)), ((), ())), preferred_element_type=F32)
         values = project_values(value_rows, mixed[:VEC] + mixed[VEC:])
 
+    with jax.named_scope("latent_base"):
+        plain = lax.dot_general(
+            final_weight, hidden, (((0,), (1,)), ((), ())), preferred_element_type=F32
+        )
+        plain = plain + final_bias[:, None]
+        base, edge_first, edge_last = latent_base(
+            refresh, here, noise_level, plain, noisy_latent, velocity_cache
+        )
+
     with jax.named_scope("queries"):
-        got, keys, values = together((got, keys, values))
+        got, keys, values, base, edge_first, edge_last = together(
+            (got, keys, values, base, edge_first, edge_last)
+        )
         held = exchange(select(refresh, got), ("yl", "xl", "z"))
 
     with jax.named_scope("keys_values"):
@@ -413,24 +424,14 @@
         values_far, far_a, far_b, state = together((values_far, far_a, far_b, state))
         state = attend(queries, values_far, state, (far_a, far_b))
         part = merge_second(exchange(state, ("yl", "xl")))
-        part, hidden = together((part, hidden))
         parts = exchange(part, "z")
 
-    with jax.named_scope("latent_base"):
-        plain = lax.dot_general(
-            final_weight, hidden, (((0,), (1,)), ((), ())), preferred_element_type=F32
-        )
-        plain = plain + final_bias[:, None]
-        base, edge_first, edge_last = latent_base(
-            refresh, here, noise_level, plain, noisy_latent, velocity_cache
-        )
+    with jax.named_scope("velocity"):
+        term = merge_last(parts)
+        term = jnp.sum(lax.all_gather(term, HEAD), axis=0).astype(BF16)
+        term, edge_first, edge_last = together((term, edge_first, edge_last))
         up = lax.ppermute(edge_last, PATCH, [(p, p + 1) for p in range(PATCHES - 1)])
         down = lax.ppermute(edge_first, PATCH, [(p + 1, p) for p in range(PATCHES - 1)])
-
-    with jax.named_scope("velocity"):
-        parts, up, down = together((parts, up, down))
-        term = merge_last(parts)
-        term = jnp.sum(lax.all_gather(term, HEAD), axis=0).astype(BF16)
         gathered = exchange(spread_out(term, 16), ("yh", "yl", "xh", "xl"))
 
     with jax.named_scope("decode"):

time: 161 us -> 162 us (level)
  the two profiles are of different devices: /device:TPU:32 before, /device:TPU:8 now
where the time goes in v6:
time: 162 us; the launch traced here: 161 us
  starting transfers between devices  45.5 us (28%)
  blocking collectives  36.3 us (22%)
  Pallas kernels  34.6 us (21%)
  waiting for transfers between devices  25.9 us (16%)
  matrix products  6.98 us (4%)
  local copies, waits for them, and re-layouts  5.93 us (4%)
  other arithmetic  5.27 us (3%)
    all_to_all x2, blocking collectives, exchange(): return lax.all_to_all(value, axis, 0, 0)  30.6 us
    all_to_all x3, starting transfers between devices, exchange(): return lax.all_to_all(value, axis, 0, 0)  25.5 us
    all_to_all x3, waiting for transfers between devices, exchange(): return lax.all_to_all(value, axis, 0, 0)  20 us
    pallas_call x4, Pallas kernels, attend(): pl.pallas_call(functools.partial(attend_kernel, first, last), out_shape=o...  20 us
    ppermute x7, starting transfers between devices, mirror(): return lax.ppermute(value, PATCH, pairs)  9.06 us
    ppermute x1, starting transfers between devices, on_device(): lax.ppermute(edge_first, PATCH, [(p + 1, p) for p in range(PATCHES - 1)])  7.8 us
    all_gather x1, blocking collectives, on_device(): term = jnp.sum(lax.all_gather(term, HEAD), axis=0).astype(BF16)  5.62 us
    dot_general x1, matrix products, on_device(): lax.dot_general(both, out_weight, (((1,), (1,)), ((), ())), preferred_ele...  4.25 us
  transfers between devices with their start and end apart: 12, of which 7 were waited for; matrix products, arithmetic and copies ran while one was open for 9% of the time, Pallas kernels for 13%

profile of v6, /device:TPU:8, one launch (start us, length us, event | category | flops | bytes accessed | tf_op | source)
XLA Modules:
  0.0 161.3 jit_solution(17990201587378410771)
XLA Ops:
  0.0 2.2 %slice_bitcast_fusion = bf16[64,8,768]{2,1,0:T(8,128)(2,1)} fusion(bf16[512,3,768]{2,0,1:T(8,128)(2,1)} %param.13), kind=kLoop, calls=%fused_computation.13 | loop fusion | bytes 1572864 | tf_op jit(solution)/shard_map/queries/reshape;queries/squeeze | solution.py:382
  2.2 14.7 %all-to-all-start = ((bf16[64,8,768]{2,1,0:T(8,128)(2,1)}), bf16[64,8,768]{2,1,0:T(8,128)(2,1)}, u32[]{:S(2)}, u32[]{:S(2)}) async-start(bf16[64,8,768]{2,1,0:T(8,128)(2,1)} %slice_bitcast_fusion), calls=%async_computation | async-start | bytes 1572864 | tf_op jit(solution)/shard_map/queries/all_to_all | solution.py:43
  19.5 2.7 %convolution_add_fusion.plain_ref = f32[64,512]{1,0:T(8,128)} fusion(bf16[3072,64]{0,1:T(8,128)(2,1)} %param.18, bf16[512,3072]{1,0:T(8,128)(2,1)S(1)} %copy-done, f32[64]{0:T(128)} %param.19), kind=kOutput, calls=%fused_computation | convolution fusion | flops 201359360 | bytes 3670272 | tf_op jit(solution)/shard_map/latent_base/dot_general | solution.py:397
  24.9 4.2 %fusion.1 = f32[128,768]{1,0:T(8,128)S(1)} fusion(bf16[768,3072]{1,0:T(8,128)(2,1)} %param.17, bf16[64,3072]{1,0:T(8,128)(2,1)} %get-tuple-element.90, bf16[64,3072]{1,0:T(8,128)(2,1)S(1)} %get-tuple-element.89), kind=kOutput, calls=%fused_computation.4 | convolution fusion | flops 605552640 | bytes 5898240 | tf_op jit(solution)/shard_map/keys_values/dot_general | solution.py:393
  29.8 2.2 %fusion.8 = (bf16[512,1,768]{2,1,0:T(2,128)(2,1)S(1)}, bf16[512,1,768]{2,1,0:T(2,128)(2,1)S(1)}) fusion(bf16[512,2,768]{2,1,0:T(2,128)(2,1)S(1)} %copy-done.1), kind=kLoop, calls=%fused_computation.17 | loop fusion | bytes 3145728 | tf_op jit(solution)/shard_map/keys_values/slice | solution.py:389
  32.0 2.0 %fusion.5 = (bf16[512,768]{1,0:T(8,128)(2,1)}, bf16[512,768]{1,0:T(8,128)(2,1)}) fusion(bf16[512,1,768]{2,1,0:T(2,128)(2,1)S(1)} %get-tuple-element.87, bf16[512,3,768]{2,0,1:T(8,128)(2,1)S(1)} %copy-done.2, pred[]{:T(512)} %compare_reduce_fusion, bf16[512,1,768]{2,1,0:T(2,128)(2,1)S(1)} %get-tuple-element.88), kind=kLoop, calls=%fused_computation.9 | loop fusion | flops 786432 | bytes 4718593 | tf_op jit(solution)/shard_map/keys_values/jit(_where)/select_n | solution.py:389
  34.0 2.3 %values.1.refs_1_ = bf16[384,512]{1,0:T(8,128)(2,1)} custom-call(bf16[512,768]{1,0:T(8,128)(2,1)} %get-tuple-element.85.v_ref, f32[64,768]{1,0:T(8,128)} %slice_add_fusion.w_ref), custom_call_target="tpu_custom_call" | custom-call | flops 100663296 | bytes 1572864 | tf_op jit(solution)/shard_map/keys_values/values/pallas_call | solution.py:88
  36.3 5.7 %all-to-all-done.got_ref = bf16[64,8,768]{2,1,0:T(8,128)(2,1)} async-done(((bf16[64,8,768]{2,1,0:T(8,128)(2,1)}), bf16[64,8,768]{2,1,0:T(8,128)(2,1)}, u32[]{:S(2)}, u32[]{:S(2)}) %all-to-all-start) | async-done | bytes 786464 | tf_op jit(solution)/shard_map/queries/all_to_all | solution.py:43
  42.0 2.1 %select.1 = bf16[16,32,768]{2,1,0:T(8,128)(2,1)} custom-call(s32[4]{0:T(128)} %refresh_ref.5, bf16[64,8,768]{2,1,0:T(8,128)(2,1)} %all-to-all-done.got_ref), custom_call_target="tpu_custom_call" | custom-call | bytes 835584 | tf_op jit(solution)/shard_map/queries/select/pallas_call | solution.py:68
  44.2 5.9 %all-to-all-start.1 = ((bf16[16,32,768]{2,1,0:T(8,128)(2,1)}), bf16[16,32,768]{2,1,0:T(8,128)(2,1)}, u32[]{:S(2)}, u32[]{:S(2)}) async-start(bf16[16,32,768]{2,1,0:T(8,128)(2,1)} %select.1), calls=%async_computation.1 | async-start | bytes 1572864 | tf_op jit(solution)/shard_map/queries/all_to_all | solution.py:43
  53.3 2.0 %collective-permute-start.5 = (bf16[384,512]{1,0:T(8,128)(2,1)}, bf16[384,512]{1,0:T(8,128)(2,1)}, u32[]{:S(2)}, u32[]{:S(2)}) collective-permute-start(bf16[384,512]{1,0:T(8,128)(2,1)} %values.1.refs_1_), channel_id=1, source_target_pairs={{0,192},{4,196},{8,200},{12,204},{16,208},{20,212},{24,216},{28,22... | collective-permute-start | bytes 1179656 | tf_op jit(solution)/shard_map/keys_values/ppermute | solution.py:35
  56.3 14.3 %all-to-all-done.1 = bf16[16,32,768]{2,1,0:T(8,128)(2,1)} async-done(((bf16[16,32,768]{2,1,0:T(8,128)(2,1)}), bf16[16,32,768]{2,1,0:T(8,128)(2,1)}, u32[]{:S(2)}, u32[]{:S(2)}) %all-to-all-start.1) | async-done | bytes 786464 | tf_op jit(solution)/shard_map/queries/all_to_all | solution.py:43
  70.6 4.8 %attend.4 = (f32[384,512]{1,0:T(8,128)}, f32[8,512]{1,0:T(8,128)}, f32[8,512]{1,0:T(8,128)}) custom-call(bf16[512,768]{1,0:T(8,128)(2,1)} %bitcast.5.refs_0_, bf16[384,512]{1,0:T(8,128)(2,1)} %values.1.refs_1_, bf16[512,768]{1,0:T(8,128)(2,1)} %get-tuple-element.52.refs_2_), custom_call_target="tpu_custom_call" | custom-call | flops 805306368 | bytes 3145728 | tf_op jit(solution)/shard_map/attention/attend/pallas_call | solution.py:227
  75.4 2.0 %halves.1 = (bf16[256,768]{1,0:T(8,128)(2,1)}, bf16[256,768]{1,0:T(8,128)(2,1)}) custom-call(bf16[512,768]{1,0:T(8,128)(2,1)} %collective-permute-done.1.x_ref.refs_5_, bf16[512,768]{1,0:T(8,128)(2,1)} %collective-permute-done.2.y_ref.refs_5_), custom_call_target="tpu_custom_call" | custom-call | bytes 1572864 | tf_op jit(solution)/shard_map/attention/halves/pallas_call | solution.py:104
  80.5 5.1 %attend.5 = (f32[384,512]{1,0:T(8,128)}, f32[8,512]{1,0:T(8,128)}, f32[8,512]{1,0:T(8,128)}) custom-call(bf16[512,768]{1,0:T(8,128)(2,1)} %bitcast.5.refs_0_, bf16[384,512]{1,0:T(8,128)(2,1)} %collective-permute-done.6.refs_1_, f32[384,512]{1,0:T(8,128)} %get-tuple-element.60.refs_2_, f32[8,512]{1,0:T(8,128)} %get-tuple-element.61.refs_3_, ...), custom_call_target="tpu_custom_call" | custom-call | flops 805306368 | bytes 3145728 | tf_op jit(solution)/shard_map/attention/attend/pallas_call | solution.py:227
  87.3 5.1 %attend.6 = (f32[384,512]{1,0:T(8,128)}, f32[8,512]{1,0:T(8,128)}, f32[8,512]{1,0:T(8,128)}) custom-call(bf16[512,768]{1,0:T(8,128)(2,1)} %bitcast.5.refs_0_, bf16[384,512]{1,0:T(8,128)(2,1)} %collective-permute-done.5.refs_1_, f32[384,512]{1,0:T(8,128)} %get-tuple-element.67.refs_2_, f32[8,512]{1,0:T(8,128)} %get-tuple-element.68.refs_3_, ...), custom_call_target="tpu_custom_call" | custom-call | flops 805306368 | bytes 3145728 | tf_op jit(solution)/shard_map/attention/attend/pallas_call | solution.py:227
  93.7 4.9 %attend.7 = bf16[4,416,128]{2,1,0:T(8,128)(2,1)} custom-call(bf16[512,768]{1,0:T(8,128)(2,1)} %bitcast.5.refs_0_, bf16[384,512]{1,0:T(8,128)(2,1)} %copy-done.4, f32[384,512]{1,0:T(8,128)} %get-tuple-element.74.refs_2_, f32[8,512]{1,0:T(8,128)} %get-tuple-element.75.refs_3_, f32[8,512]{1,0:T(8,128)} %get-tuple-element.76.refs_4_, ...), custom_call_target="tpu_custom_call" | custom-call | flops 805306368 | bytes 3145728 | tf_op jit(solution)/shard_map/attention/attend/pallas_call | solution.py:227
  98.6 11.5 %all_to_all.25.p_ref = bf16[4,416,128]{2,1,0:T(8,128)(2,1)} all-to-all(bf16[4,416,128]{2,1,0:T(8,128)(2,1)} %attend.7), channel_id=1, replica_groups=mesh['yh'=2,'yl'=2,'xh'=2,'xl'=2,'z'=4,'w'=2,'c'=2] {'yl','xl'}, dimensions={0} | all-to-all | bytes 851968 | tf_op jit(solution)/shard_map/attention/all_to_all | solution.py:43
  112.0 19.2 %all_to_all.26.p_ref = bf16[4,416,128]{2,1,0:T(8,128)(2,1)} all-to-all(bf16[4,416,128]{2,1,0:T(8,128)(2,1)} %merge_second.1), channel_id=1, replica_groups=mesh['yh'=2,'yl'=2,'xh'=2,'xl'=2,'z'=4,'w'=2,'c'=2] {'z'}, dimensions={0} | all-to-all | bytes 851968 | tf_op jit(solution)/shard_map/attention/all_to_all | solution.py:43
  132.9 5.6 %all-gather = f32[256,128]{1,0:T(8,128)S(1)} all-gather(f32[64,128]{1,0:T(8,128)} %merge_last.1), channel_id=2, replica_groups=mesh['yh'=2,'yl'=2,'xh'=2,'xl'=2,'z'=4,'w'=2,'c'=2] {'w','c'}, dimensions={0}, use_global_device_ids=true | all-gather | bytes 163840 | tf_op jit(solution)/shard_map/velocity/all_gather | solution.py:431
  139.3 4.9 %all-to-all-start.4 = ((bf16[16,64,128]{2,1,0:T(8,128)(2,1)}), bf16[16,64,128]{2,1,0:T(8,128)(2,1)S(1)}, u32[]{:S(2)}, u32[]{:S(2)}) async-start(bf16[16,64,128]{2,1,0:T(8,128)(2,1)} %broadcast_in_dim.2), calls=%async_computation.4 | async-start | bytes 524288 | tf_op jit(solution)/shard_map/velocity/all_to_all | solution.py:43
  144.2 3.1 %collective-permute-start.7 = (f32[16,1024]{1,0:T(8,128)}, f32[16,1024]{1,0:T(8,128)S(1)}, u32[]{:S(2)}, u32[]{:S(2)}) collective-permute-start(f32[16,1024]{1,0:T(8,128)} %get-tuple-element.83), channel_id=1, source_target_pairs={{0,4},{4,8},{8,12},{12,16},{16,20},{20,24},{24,28},{28,32},{32,36}... | collective-permute-start | bytes 196616 | tf_op jit(solution)/shard_map/velocity/ppermute | solution.py:433
  147.3 7.8 %collective-permute-start.8 = (f32[16,1024]{1,0:T(8,128)}, f32[16,1024]{1,0:T(8,128)S(1)}, u32[]{:S(2)}, u32[]{:S(2)}) collective-permute-start(f32[16,1024]{1,0:T(8,128)} %get-tuple-element.84), channel_id=1, source_target_pairs={{4,0},{8,4},{12,8},{16,12},{20,16},{24,20},{28,24},{32,28},{36,32}... | collective-permute-start | bytes 196616 | tf_op jit(solution)/shard_map/velocity/ppermute | solution.py:434
  158.6 2.7 %decode.1 = bf16[2,128,1024]{2,1,0:T(8,128)(2,1)} custom-call(s32[4]{0:T(128)} %refresh_ref.5, s32[1]{0:T(128)} %bitcast.me_ref, f32[1]{0:T(128)S(6)} %copy.24.level_ref, bf16[16,64,128]{2,1,0:T(8,128)(2,1)} %copy-done.3, f32[32,1024]{1,0:T(8,128)} %get-tuple-element.82.base_ref, f32[16,1024]{1,0:T(8,128)} %copy-done.5, f32[16,1024]{1,0:T(8,128)} %copy-done.6, ...), custom_call_target="tpu_custom_call" | custom-call | flops 83886080 | bytes 2097152 | tf_op jit(solution)/shard_map/decode/decode/pallas_call | solution.py:351
  (42 shorter events, 23.2 us)
Async XLA Ops:
  0.0 19.5 %copy-start = (bf16[512,3072]{1,0:T(8,128)(2,1)S(1)}, bf16[512,3072]{1,0:T(8,128)(2,1)}, u32[]{:S(2)}) copy-start(bf16[512,3072]{1,0:T(8,128)(2,1)} %param.15) | copy-start | bytes 9437188
  0.0 17.6 %copy-start.7 = (f32[3072]{0:T(1024)S(1)}, f32[3072]{0:T(1024)}, u32[]{:S(2)}) copy-start(f32[3072]{0:T(1024)} %param.20) | copy-start | bytes 36868
  2.2 39.8 %all-to-all-start = ((bf16[64,8,768]{2,1,0:T(8,128)(2,1)}), bf16[64,8,768]{2,1,0:T(8,128)(2,1)}, u32[]{:S(2)}, u32[]{:S(2)}) async-start(bf16[64,8,768]{2,1,0:T(8,128)(2,1)} %slice_bitcast_fusion), calls=%async_computation | async-start | bytes 1572864 | tf_op jit(solution)/shard_map/queries/all_to_all | solution.py:43
  17.6 6.5 %copy-start.8 = (s32[4]{0:T(128)S(1)}, s32[4]{0:T(128)}, u32[]{:S(2)}) copy-start(s32[4]{0:T(128)} %refresh_ref.5) | copy-start | bytes 52
  24.9 5.0 %copy-start.1 = (bf16[512,2,768]{2,1,0:T(2,128)(2,1)S(1)}, bf16[512,2,768]{2,1,0:T(2,128)(2,1)}, u32[]{:S(2)}) copy-start(bf16[512,2,768]{2,1,0:T(2,128)(2,1)} %param.14) | copy-start | bytes 4718596
  29.8 2.2 %copy-start.2 = (bf16[512,3,768]{2,0,1:T(8,128)(2,1)S(1)}, bf16[512,3,768]{2,0,1:T(8,128)(2,1)}, u32[]{:S(2)}) copy-start(bf16[512,3,768]{2,0,1:T(8,128)(2,1)} %param.13) | copy-start | bytes 7077892
  44.2 26.4 %all-to-all-start.1 = ((bf16[16,32,768]{2,1,0:T(8,128)(2,1)}), bf16[16,32,768]{2,1,0:T(8,128)(2,1)}, u32[]{:S(2)}, u32[]{:S(2)}) async-start(bf16[16,32,768]{2,1,0:T(8,128)(2,1)} %select.1), calls=%async_computation.1 | async-start | bytes 1572864 | tf_op jit(solution)/shard_map/queries/all_to_all | solution.py:43
  50.1 25.3 %collective-permute-start.1 = (bf16[512,768]{1,0:T(8,128)(2,1)}, bf16[512,768]{1,0:T(8,128)(2,1)}, u32[]{:S(2)}, u32[]{:S(2)}) collective-permute-start(bf16[512,768]{1,0:T(8,128)(2,1)} %get-tuple-element.52.refs_2_), channel_id=1, source_target_pairs={{0,48},{4,52},{8,56},{12,60},{16,32},{20,36},{24,40},{28,44},{32,1... | collective-permute-start | bytes 2359304 | tf_op jit(solution)/shard_map/keys_values/ppermute | solution.py:35
  50.2 25.2 %collective-permute-start.2 = (bf16[512,768]{1,0:T(8,128)(2,1)}, bf16[512,768]{1,0:T(8,128)(2,1)}, u32[]{:S(2)}, u32[]{:S(2)}) collective-permute-start(bf16[512,768]{1,0:T(8,128)(2,1)} %get-tuple-element.52.refs_2_), channel_id=1, source_target_pairs={{0,192},{4,196},{8,200},{12,204},{16,208},{20,212},{24,216},{28,22... | collective-permute-start | bytes 2359304 | tf_op jit(solution)/shard_map/keys_values/ppermute | solution.py:35
  51.6 28.9 %collective-permute-start.6 = (bf16[384,512]{1,0:T(8,128)(2,1)}, bf16[384,512]{1,0:T(8,128)(2,1)}, u32[]{:S(2)}, u32[]{:S(2)}) collective-permute-start(bf16[384,512]{1,0:T(8,128)(2,1)} %values.1.refs_1_), channel_id=1, source_target_pairs={{0,48},{4,52},{8,56},{12,60},{16,32},{20,36},{24,40},{28,44},{32,1... | collective-permute-start | bytes 1179656 | tf_op jit(solution)/shard_map/keys_values/ppermute | solution.py:35
  53.3 34.0 %collective-permute-start.5 = (bf16[384,512]{1,0:T(8,128)(2,1)}, bf16[384,512]{1,0:T(8,128)(2,1)}, u32[]{:S(2)}, u32[]{:S(2)}) collective-permute-start(bf16[384,512]{1,0:T(8,128)(2,1)} %values.1.refs_1_), channel_id=1, source_target_pairs={{0,192},{4,196},{8,200},{12,204},{16,208},{20,212},{24,216},{28,22... | collective-permute-start | bytes 1179656 | tf_op jit(solution)/shard_map/keys_values/ppermute | solution.py:35
  55.3 37.1 %collective-permute-start = (bf16[384,512]{1,0:T(8,128)(2,1)}, bf16[384,512]{1,0:T(8,128)(2,1)S(1)}, u32[]{:S(2)}, u32[]{:S(2)}) collective-permute-start(bf16[384,512]{1,0:T(8,128)(2,1)} %values.1.refs_1_), channel_id=1, source_target_pairs={{0,240},{4,244},{8,248},{12,252},{16,224},{20,228},{24,232},{28,23... | collective-permute-start | bytes 1179656 | tf_op jit(solution)/shard_map/keys_values/ppermute | solution.py:35
  77.5 16.2 %collective-permute-start.3 = (bf16[256,768]{1,0:T(8,128)(2,1)}, bf16[256,768]{1,0:T(8,128)(2,1)}, u32[]{:S(2)}, u32[]{:S(2)}) collective-permute-start(bf16[256,768]{1,0:T(8,128)(2,1)} %get-tuple-element.58), channel_id=1, source_target_pairs={{0,192},{4,196},{8,200},{12,204},{16,208},{20,212},{24,216},{28,22... | collective-permute-start | bytes 1179656 | tf_op jit(solution)/shard_map/attention/ppermute | solution.py:35
  78.3 15.4 %collective-permute-start.4 = (bf16[256,768]{1,0:T(8,128)(2,1)}, bf16[256,768]{1,0:T(8,128)(2,1)}, u32[]{:S(2)}, u32[]{:S(2)}) collective-permute-start(bf16[256,768]{1,0:T(8,128)(2,1)} %get-tuple-element.59), channel_id=1, source_target_pairs={{0,48},{4,52},{8,56},{12,60},{16,32},{20,36},{24,40},{28,44},{32,1... | collective-permute-start | bytes 1179656 | tf_op jit(solution)/shard_map/attention/ppermute | solution.py:35
  92.4 1.3 copy-start.4
  139.3 18.6 %all-to-all-start.4 = ((bf16[16,64,128]{2,1,0:T(8,128)(2,1)}), bf16[16,64,128]{2,1,0:T(8,128)(2,1)S(1)}, u32[]{:S(2)}, u32[]{:S(2)}) async-start(bf16[16,64,128]{2,1,0:T(8,128)(2,1)} %broadcast_in_dim.2), calls=%async_computation.4 | async-start | bytes 524288 | tf_op jit(solution)/shard_map/velocity/all_to_all | solution.py:43
  144.2 11.8 %collective-permute-start.7 = (f32[16,1024]{1,0:T(8,128)}, f32[16,1024]{1,0:T(8,128)S(1)}, u32[]{:S(2)}, u32[]{:S(2)}) collective-permute-start(f32[16,1024]{1,0:T(8,128)} %get-tuple-element.83), channel_id=1, source_target_pairs={{0,4},{4,8},{8,12},{12,16},{16,20},{20,24},{24,28},{28,32},{32,36}... | collective-permute-start | bytes 196616 | tf_op jit(solution)/shard_map/velocity/ppermute | solution.py:433
  147.3 10.6 %collective-permute-start.8 = (f32[16,1024]{1,0:T(8,128)}, f32[16,1024]{1,0:T(8,128)S(1)}, u32[]{:S(2)}, u32[]{:S(2)}) collective-permute-start(f32[16,1024]{1,0:T(8,128)} %get-tuple-element.84), channel_id=1, source_target_pairs={{4,0},{8,4},{12,8},{16,12},{20,16},{24,20},{28,24},{32,28},{36,32}... | collective-permute-start | bytes 196616 | tf_op jit(solution)/shard_map/velocity/ppermute | solution.py:434
  156.0 1.9 %copy-start.5 = (f32[16,1024]{1,0:T(8,128)}, f32[16,1024]{1,0:T(8,128)S(1)}, u32[]{:S(2)}) copy-start(f32[16,1024]{1,0:T(8,128)S(1)} %collective-permute-done.7.up_ref) | copy-start | bytes 196612
  157.9 0.6 copy-start.6
  157.9 0.7 copy-start.3

commit v7 on v6

--- a/solution.py
+++ b/solution.py
@@ -387,29 +387,29 @@
         refreshed = jnp.any(refresh == me)
         keys = jnp.where(refreshed, fresh_qkv[:, 1], kv_cache[:, 0])
         value_rows = jnp.where(refreshed, fresh_qkv[:, 2], kv_cache[:, 1])
+
+    with jax.named_scope("latent_base"):
+        plain = lax.dot_general(
+            final_weight, hidden, (((0,), (1,)), ((), ())), preferred_element_type=F32
+        )
+        plain = plain + final_bias[:, None]
+        base, edge_first, edge_last = latent_base(
+            refresh, here, noise_level, plain, noisy_latent, velocity_cache
+        )
+        up = lax.ppermute(edge_last, PATCH, [(p, p + 1) for p in range(PATCHES - 1)])
+        down = lax.ppermute(edge_first, PATCH, [(p + 1, p) for p in range(PATCHES - 1)])
+
+    with jax.named_scope("queries"):
+        got, base, up, down, _, _ = together((got, base, up, down, keys, value_rows))
+        held = exchange(select(refresh, got), ("yl", "xl", "z"))
+
+    with jax.named_scope("keys_values"):
+        keys_x, keys_y = mirror(keys, 0, 1), mirror(keys, 1, 0)
         gated = final_weight.T.astype(F32) * gate_scale[None, :]
         high = lax.reduce_precision(gated, 8, 7)
         both = jnp.concatenate([high, gated - high], axis=0).astype(BF16)
         mixed = lax.dot_general(both, out_weight, (((1,), (1,)), ((), ())), preferred_element_type=F32)
         values = project_values(value_rows, mixed[:VEC] + mixed[VEC:])
-
-    with jax.named_scope("latent_base"):
-        plain = lax.dot_general(
-            final_weight, hidden, (((0,), (1,)), ((), ())), preferred_element_type=F32
-        )
-        plain = plain + final_bias[:, None]
-        base, edge_first, edge_last = latent_base(
-            refresh, here, noise_level, plain, noisy_latent, velocity_cache
-        )
-
-    with jax.named_scope("queries"):
-        got, keys, values, base, edge_first, edge_last = together(
-            (got, keys, values, base, edge_first, edge_last)
-        )
-        held = exchange(select(refresh, got), ("yl", "xl", "z"))
-
-    with jax.named_scope("keys_values"):
-        keys_x, keys_y = mirror(keys, 0, 1), mirror(keys, 1, 0)
         values_x, values_y, values_far = mirror(values, 0, 1), mirror(values, 1, 0), mirror(values, 1, 1)
 
     with jax.named_scope("attention"):
@@ -429,9 +429,6 @@
     with jax.named_scope("velocity"):
         term = merge_last(parts)
         term = jnp.sum(lax.all_gather(term, HEAD), axis=0).astype(BF16)
-        term, edge_first, edge_last = together((term, edge_first, edge_last))
-        up = lax.ppermute(edge_last, PATCH, [(p, p + 1) for p in range(PATCHES - 1)])
-        down = lax.ppermute(edge_first, PATCH, [(p + 1, p) for p in range(PATCHES - 1)])
         gathered = exchange(spread_out(term, 16), ("yh", "yl", "xh", "xl"))
 
     with jax.named_scope("decode"):

time: 162 us -> 158 us (0.975)
  the two profiles are of different devices: /device:TPU:8 before, /device:TPU:32 now
where the time goes in v7:
time: 158 us; the launch traced here: 155 us
  blocking collectives  47.8 us (30%)
  starting transfers between devices  39.1 us (25%)
  Pallas kernels  34.7 us (22%)
  waiting for transfers between devices  16.9 us (11%)
  local copies, waits for them, and re-layouts  6.74 us (4%)
  matrix products  5.75 us (4%)
  other arithmetic  3.52 us (2%)
    all_to_all x3, blocking collectives, exchange(): return lax.all_to_all(value, axis, 0, 0)  42.2 us
    pallas_call x4, Pallas kernels, attend(): pl.pallas_call(functools.partial(attend_kernel, first, last), out_shape=o...  20 us
    all_to_all x2, starting transfers between devices, exchange(): return lax.all_to_all(value, axis, 0, 0)  18.2 us
    ppermute x7, starting transfers between devices, mirror(): return lax.ppermute(value, PATCH, pairs)  14.7 us
    all_to_all x2, waiting for transfers between devices, exchange(): return lax.all_to_all(value, axis, 0, 0)  10.7 us
    all_gather x1, blocking collectives, on_device(): term = jnp.sum(lax.all_gather(term, HEAD), axis=0).astype(BF16)  5.62 us
    ppermute x1, starting transfers between devices, on_device(): lax.ppermute(edge_last, PATCH, [(p, p + 1) for p in range(PATCHES - 1)])  4.92 us
    ppermute x7, waiting for transfers between devices, mirror(): return lax.ppermute(value, PATCH, pairs)  4.58 us
  transfers between devices with their start and end apart: 11, of which 6 were waited for; matrix products, arithmetic and copies ran while one was open for 9% of the time, Pallas kernels for 14%

profile of v7, /device:TPU:32, one launch (start us, length us, event | category | flops | bytes accessed | tf_op | source)
XLA Modules:
  0.0 155.2 jit_solution(6000783622903392280)
XLA Ops:
  0.0 2.2 %slice_bitcast_fusion = bf16[64,8,768]{2,1,0:T(8,128)(2,1)} fusion(bf16[512,3,768]{2,0,1:T(8,128)(2,1)} %param.13), kind=kLoop, calls=%fused_computation.13 | loop fusion | bytes 1572864 | tf_op jit(solution)/shard_map/queries/reshape;queries/squeeze | solution.py:382
  2.3 13.9 %all-to-all-start = ((bf16[64,8,768]{2,1,0:T(8,128)(2,1)}), bf16[64,8,768]{2,1,0:T(8,128)(2,1)}, u32[]{:S(2)}, u32[]{:S(2)}) async-start(bf16[64,8,768]{2,1,0:T(8,128)(2,1)} %slice_bitcast_fusion), calls=%async_computation | async-start | bytes 1572864 | tf_op jit(solution)/shard_map/queries/all_to_all | solution.py:43
  20.5 4.9 %collective-permute-start = (f32[16,1024]{1,0:T(8,128)}, f32[16,1024]{1,0:T(8,128)}, u32[]{:S(2)}, u32[]{:S(2)}) collective-permute-start(f32[16,1024]{1,0:T(8,128)} %get-tuple-element.42), channel_id=1, source_target_pairs={{0,4},{4,8},{8,12},{12,16},{16,20},{20,24},{24,28},{28,32},{32,36}... | collective-permute-start | bytes 196616 | tf_op jit(solution)/shard_map/latent_base/ppermute | solution.py:399
  27.4 4.4 %fusion.8 = (bf16[512,1,768]{2,1,0:T(2,128)(2,1)S(1)}, bf16[512,1,768]{2,1,0:T(2,128)(2,1)S(1)}) fusion(bf16[512,2,768]{2,1,0:T(2,128)(2,1)} %param.14), kind=kLoop, calls=%fused_computation.17 | loop fusion | bytes 3145728 | tf_op jit(solution)/shard_map/keys_values/slice | solution.py:389
  35.4 8.0 %all-to-all-done.got_ref = bf16[64,8,768]{2,1,0:T(8,128)(2,1)} async-done(((bf16[64,8,768]{2,1,0:T(8,128)(2,1)}), bf16[64,8,768]{2,1,0:T(8,128)(2,1)}, u32[]{:S(2)}, u32[]{:S(2)}) %all-to-all-start) | async-done | bytes 786464 | tf_op jit(solution)/shard_map/queries/all_to_all | solution.py:43
  43.4 2.1 %select.1 = bf16[16,32,768]{2,1,0:T(8,128)(2,1)} custom-call(s32[4]{0:T(128)} %refresh_ref.5, bf16[64,8,768]{2,1,0:T(8,128)(2,1)} %all-to-all-done.got_ref), custom_call_target="tpu_custom_call" | custom-call | bytes 835584 | tf_op jit(solution)/shard_map/queries/select/pallas_call | solution.py:68
  45.5 4.3 %all-to-all-start.1 = ((bf16[16,32,768]{2,1,0:T(8,128)(2,1)}), bf16[16,32,768]{2,1,0:T(8,128)(2,1)}, u32[]{:S(2)}, u32[]{:S(2)}) async-start(bf16[16,32,768]{2,1,0:T(8,128)(2,1)} %select.1), calls=%async_computation.1 | async-start | bytes 1572864 | tf_op jit(solution)/shard_map/queries/all_to_all | solution.py:43
  50.8 2.3 %collective-permute-start.4 = (bf16[512,768]{1,0:T(8,128)(2,1)}, bf16[512,768]{1,0:T(8,128)(2,1)}, u32[]{:S(2)}, u32[]{:S(2)}) collective-permute-start(bf16[512,768]{1,0:T(8,128)(2,1)} %get-tuple-element.76.refs_2_), channel_id=1, source_target_pairs={{0,192},{4,196},{8,200},{12,204},{16,208},{20,212},{24,216},{28,22... | collective-permute-start | bytes 2359304 | tf_op jit(solution)/shard_map/keys_values/ppermute | solution.py:35
  53.3 4.0 %fusion.1 = f32[128,768]{1,0:T(8,128)S(1)} fusion(bf16[768,3072]{1,0:T(8,128)(2,1)} %param.17, bf16[64,3072]{1,0:T(8,128)(2,1)S(1)} %get-tuple-element.80, bf16[64,3072]{1,0:T(8,128)(2,1)S(1)} %get-tuple-element.79), kind=kOutput, calls=%fused_computation.4 | convolution fusion | flops 605552640 | bytes 5898240 | tf_op jit(solution)/shard_map/keys_values/dot_general | solution.py:411
  58.0 2.3 %values.1.refs_1_ = bf16[384,512]{1,0:T(8,128)(2,1)} custom-call(bf16[512,768]{1,0:T(8,128)(2,1)} %get-tuple-element.75.v_ref, f32[64,768]{1,0:T(8,128)} %slice_add_fusion.w_ref), custom_call_target="tpu_custom_call" | custom-call | flops 100663296 | bytes 1572864 | tf_op jit(solution)/shard_map/keys_values/values/pallas_call | solution.py:88
  63.5 2.7 %collective-permute-start.2 = (bf16[384,512]{1,0:T(8,128)(2,1)}, bf16[384,512]{1,0:T(8,128)(2,1)S(1)}, u32[]{:S(2)}, u32[]{:S(2)}) collective-permute-start(bf16[384,512]{1,0:T(8,128)(2,1)} %values.1.refs_1_), channel_id=1, source_target_pairs={{0,240},{4,244},{8,248},{12,252},{16,224},{20,228},{24,232},{28,23... | collective-permute-start | bytes 1179656 | tf_op jit(solution)/shard_map/keys_values/ppermute | solution.py:35
  66.2 2.7 %all-to-all-done.1 = bf16[16,32,768]{2,1,0:T(8,128)(2,1)} async-done(((bf16[16,32,768]{2,1,0:T(8,128)(2,1)}), bf16[16,32,768]{2,1,0:T(8,128)(2,1)}, u32[]{:S(2)}, u32[]{:S(2)}) %all-to-all-start.1) | async-done | bytes 786464 | tf_op jit(solution)/shard_map/queries/all_to_all | solution.py:43
  68.9 4.8 %attend.4 = (f32[384,512]{1,0:T(8,128)}, f32[8,512]{1,0:T(8,128)}, f32[8,512]{1,0:T(8,128)}) custom-call(bf16[512,768]{1,0:T(8,128)(2,1)} %bitcast.4.refs_0_, bf16[384,512]{1,0:T(8,128)(2,1)} %values.1.refs_1_, bf16[512,768]{1,0:T(8,128)(2,1)} %get-tuple-element.76.refs_2_), custom_call_target="tpu_custom_call" | custom-call | flops 805306368 | bytes 3145728 | tf_op jit(solution)/shard_map/attention/attend/pallas_call | solution.py:227
  73.7 2.1 %halves.1 = (bf16[256,768]{1,0:T(8,128)(2,1)}, bf16[256,768]{1,0:T(8,128)(2,1)}) custom-call(bf16[512,768]{1,0:T(8,128)(2,1)} %collective-permute-done.3.x_ref.refs_5_, bf16[512,768]{1,0:T(8,128)(2,1)} %collective-permute-done.4.y_ref.refs_5_), custom_call_target="tpu_custom_call" | custom-call | bytes 1572864 | tf_op jit(solution)/shard_map/attention/halves/pallas_call | solution.py:104
  75.8 4.2 %collective-permute-start.5 = (bf16[256,768]{1,0:T(8,128)(2,1)}, bf16[256,768]{1,0:T(8,128)(2,1)}, u32[]{:S(2)}, u32[]{:S(2)}) collective-permute-start(bf16[256,768]{1,0:T(8,128)(2,1)} %get-tuple-element.51), channel_id=1, source_target_pairs={{0,192},{4,196},{8,200},{12,204},{16,208},{20,212},{24,216},{28,22... | collective-permute-start | bytes 1179656 | tf_op jit(solution)/shard_map/attention/ppermute | solution.py:35
  81.2 5.1 %attend.5 = (f32[384,512]{1,0:T(8,128)}, f32[8,512]{1,0:T(8,128)}, f32[8,512]{1,0:T(8,128)}) custom-call(bf16[512,768]{1,0:T(8,128)(2,1)} %bitcast.4.refs_0_, bf16[384,512]{1,0:T(8,128)(2,1)} %collective-permute-done.8.refs_1_, f32[384,512]{1,0:T(8,128)} %get-tuple-element.53.refs_2_, f32[8,512]{1,0:T(8,128)} %get-tuple-element.54.refs_3_, ...), custom_call_target="tpu_custom_call" | custom-call | flops 805306368 | bytes 3145728 | tf_op jit(solution)/shard_map/attention/attend/pallas_call | solution.py:227
  88.3 5.1 %attend.6 = (f32[384,512]{1,0:T(8,128)}, f32[8,512]{1,0:T(8,128)}, f32[8,512]{1,0:T(8,128)}) custom-call(bf16[512,768]{1,0:T(8,128)(2,1)} %bitcast.4.refs_0_, bf16[384,512]{1,0:T(8,128)(2,1)} %collective-permute-done.7.refs_1_, f32[384,512]{1,0:T(8,128)} %get-tuple-element.60.refs_2_, f32[8,512]{1,0:T(8,128)} %get-tuple-element.61.refs_3_, ...), custom_call_target="tpu_custom_call" | custom-call | flops 805306368 | bytes 3145728 | tf_op jit(solution)/shard_map/attention/attend/pallas_call | solution.py:227
  93.4 2.7 %collective-permute-done.5.refs_5_ = bf16[256,768]{1,0:T(8,128)(2,1)} collective-permute-done((bf16[256,768]{1,0:T(8,128)(2,1)}, bf16[256,768]{1,0:T(8,128)(2,1)}, u32[]{:S(2)}, u32[]{:S(2)}) %collective-permute-start.5) | collective-permute-done | bytes 393248 | tf_op jit(solution)/shard_map/attention/ppermute | solution.py:35
  96.1 4.9 %attend.7 = bf16[4,416,128]{2,1,0:T(8,128)(2,1)} custom-call(bf16[512,768]{1,0:T(8,128)(2,1)} %bitcast.4.refs_0_, bf16[384,512]{1,0:T(8,128)(2,1)} %copy-done.3, f32[384,512]{1,0:T(8,128)} %get-tuple-element.67.refs_2_, f32[8,512]{1,0:T(8,128)} %get-tuple-element.68.refs_3_, f32[8,512]{1,0:T(8,128)} %get-tuple-element.69.refs_4_, ...), custom_call_target="tpu_custom_call" | custom-call | flops 805306368 | bytes 3145728 | tf_op jit(solution)/shard_map/attention/attend/pallas_call | solution.py:227
  101.0 12.2 %all_to_all.25.p_ref = bf16[4,416,128]{2,1,0:T(8,128)(2,1)} all-to-all(bf16[4,416,128]{2,1,0:T(8,128)(2,1)} %attend.7), channel_id=1, replica_groups=mesh['yh'=2,'yl'=2,'xh'=2,'xl'=2,'z'=4,'w'=2,'c'=2] {'yl','xl'}, dimensions={0} | all-to-all | bytes 851968 | tf_op jit(solution)/shard_map/attention/all_to_all | solution.py:43
  115.2 17.0 %all_to_all.26.p_ref = bf16[4,416,128]{2,1,0:T(8,128)(2,1)} all-to-all(bf16[4,416,128]{2,1,0:T(8,128)(2,1)} %merge_second.1), channel_id=1, replica_groups=mesh['yh'=2,'yl'=2,'xh'=2,'xl'=2,'z'=4,'w'=2,'c'=2] {'z'}, dimensions={0} | all-to-all | bytes 851968 | tf_op jit(solution)/shard_map/attention/all_to_all | solution.py:43
  133.9 5.6 %all-gather = f32[256,128]{1,0:T(8,128)S(1)} all-gather(f32[64,128]{1,0:T(8,128)} %merge_last.1), channel_id=2, replica_groups=mesh['yh'=2,'yl'=2,'xh'=2,'xl'=2,'z'=4,'w'=2,'c'=2] {'w','c'}, dimensions={0}, use_global_device_ids=true | all-gather | bytes 163840 | tf_op jit(solution)/shard_map/velocity/all_gather | solution.py:431
  139.6 12.9 %all_to_all.27.v_ref = bf16[16,64,128]{2,1,0:T(8,128)(2,1)} all-to-all(bf16[16,64,128]{2,1,0:T(8,128)(2,1)S(1)} %broadcast_in_dim.2), channel_id=1, replica_groups=mesh['yh'=2,'yl'=2,'xh'=2,'xl'=2,'z'=4,'w'=2,'c'=2] {'yh','yl','xh','xl'}, dimensions={0} | all-to-all | bytes 524288 | tf_op jit(solution)/shard_map/velocity/all_to_all | solution.py:43
  152.5 2.7 %decode.1 = bf16[2,128,1024]{2,1,0:T(8,128)(2,1)} custom-call(s32[4]{0:T(128)} %refresh_ref.5, s32[1]{0:T(128)} %bitcast.me_ref, f32[1]{0:T(128)S(6)} %copy.24.level_ref, bf16[16,64,128]{2,1,0:T(8,128)(2,1)} %all_to_all.27.v_ref, f32[32,1024]{1,0:T(8,128)} %get-tuple-element.72.base_ref, f32[16,1024]{1,0:T(8,128)} %collective-permute-done.up_ref, ...), custom_call_target="tpu_custom_call" | custom-call | flops 83886080 | bytes 2097152 | tf_op jit(solution)/shard_map/decode/decode/pallas_call | solution.py:351
  (37 shorter events, 21.2 us)
Async XLA Ops:
  0.0 16.8 %copy-start = (bf16[512,3072]{1,0:T(8,128)(2,1)S(1)}, bf16[512,3072]{1,0:T(8,128)(2,1)}, u32[]{:S(2)}) copy-start(bf16[512,3072]{1,0:T(8,128)(2,1)} %param.15) | copy-start | bytes 9437188
  0.0 16.8 %copy-start.2 = (bf16[3072,64]{0,1:T(8,128)(2,1)S(1)}, bf16[3072,64]{0,1:T(8,128)(2,1)}, u32[]{:S(2)}) copy-start(bf16[3072,64]{0,1:T(8,128)(2,1)} %param.18) | copy-start | bytes 1179652
  0.0 16.9 %copy-start.6 = (f32[64]{0:T(128)S(1)}, f32[64]{0:T(128)}, u32[]{:S(2)}) copy-start(f32[64]{0:T(128)} %param.19) | copy-start | bytes 772
  2.3 41.1 %all-to-all-start = ((bf16[64,8,768]{2,1,0:T(8,128)(2,1)}), bf16[64,8,768]{2,1,0:T(8,128)(2,1)}, u32[]{:S(2)}, u32[]{:S(2)}) async-start(bf16[64,8,768]{2,1,0:T(8,128)(2,1)} %slice_bitcast_fusion), calls=%async_computation | async-start | bytes 1572864 | tf_op jit(solution)/shard_map/queries/all_to_all | solution.py:43
  16.2 10.6 %copy-start.5 = (s32[4]{0:T(128)S(1)}, s32[4]{0:T(128)}, u32[]{:S(2)}) copy-start(s32[4]{0:T(128)} %refresh_ref.5) | copy-start | bytes 52
  20.5 14.5 %collective-permute-start = (f32[16,1024]{1,0:T(8,128)}, f32[16,1024]{1,0:T(8,128)}, u32[]{:S(2)}, u32[]{:S(2)}) collective-permute-start(f32[16,1024]{1,0:T(8,128)} %get-tuple-element.42), channel_id=1, source_target_pairs={{0,4},{4,8},{8,12},{12,16},{16,20},{20,24},{24,28},{28,32},{32,36}... | collective-permute-start | bytes 196616 | tf_op jit(solution)/shard_map/latent_base/ppermute | solution.py:399
  25.4 10.0 %collective-permute-start.1 = (f32[16,1024]{1,0:T(8,128)}, f32[16,1024]{1,0:T(8,128)}, u32[]{:S(2)}, u32[]{:S(2)}) collective-permute-start(f32[16,1024]{1,0:T(8,128)} %get-tuple-element.43), channel_id=1, source_target_pairs={{4,0},{8,4},{12,8},{16,12},{20,16},{24,20},{28,24},{32,28},{36,32}... | collective-permute-start | bytes 196616 | tf_op jit(solution)/shard_map/latent_base/ppermute | solution.py:400
  27.4 4.4 %copy-start.1 = (bf16[512,3,768]{2,0,1:T(8,128)(2,1)S(1)}, bf16[512,3,768]{2,0,1:T(8,128)(2,1)}, u32[]{:S(2)}) copy-start(bf16[512,3,768]{2,0,1:T(8,128)(2,1)} %param.13) | copy-start | bytes 7077892
  33.8 19.3 %copy-start.4 = (f32[3072]{0:T(1024)S(1)}, f32[3072]{0:T(1024)}, u32[]{:S(2)}) copy-start(f32[3072]{0:T(1024)} %param.20) | copy-start | bytes 36868
  45.5 23.4 %all-to-all-start.1 = ((bf16[16,32,768]{2,1,0:T(8,128)(2,1)}), bf16[16,32,768]{2,1,0:T(8,128)(2,1)}, u32[]{:S(2)}, u32[]{:S(2)}) async-start(bf16[16,32,768]{2,1,0:T(8,128)(2,1)} %select.1), calls=%async_computation.1 | async-start | bytes 1572864 | tf_op jit(solution)/shard_map/queries/all_to_all | solution.py:43
  49.8 23.9 %collective-permute-start.3 = (bf16[512,768]{1,0:T(8,128)(2,1)}, bf16[512,768]{1,0:T(8,128)(2,1)}, u32[]{:S(2)}, u32[]{:S(2)}) collective-permute-start(bf16[512,768]{1,0:T(8,128)(2,1)} %get-tuple-element.76.refs_2_), channel_id=1, source_target_pairs={{0,48},{4,52},{8,56},{12,60},{16,32},{20,36},{24,40},{28,44},{32,1... | collective-permute-start | bytes 2359304 | tf_op jit(solution)/shard_map/keys_values/ppermute | solution.py:35
  50.8 22.9 %collective-permute-start.4 = (bf16[512,768]{1,0:T(8,128)(2,1)}, bf16[512,768]{1,0:T(8,128)(2,1)}, u32[]{:S(2)}, u32[]{:S(2)}) collective-permute-start(bf16[512,768]{1,0:T(8,128)(2,1)} %get-tuple-element.76.refs_2_), channel_id=1, source_target_pairs={{0,192},{4,196},{8,200},{12,204},{16,208},{20,212},{24,216},{28,22... | collective-permute-start | bytes 2359304 | tf_op jit(solution)/shard_map/keys_values/ppermute | solution.py:35
  60.3 21.0 %collective-permute-start.8 = (bf16[384,512]{1,0:T(8,128)(2,1)}, bf16[384,512]{1,0:T(8,128)(2,1)}, u32[]{:S(2)}, u32[]{:S(2)}) collective-permute-start(bf16[384,512]{1,0:T(8,128)(2,1)} %values.1.refs_1_), channel_id=1, source_target_pairs={{0,48},{4,52},{8,56},{12,60},{16,32},{20,36},{24,40},{28,44},{32,1... | collective-permute-start | bytes 1179656 | tf_op jit(solution)/shard_map/keys_values/ppermute | solution.py:35
  61.8 26.5 %collective-permute-start.7 = (bf16[384,512]{1,0:T(8,128)(2,1)}, bf16[384,512]{1,0:T(8,128)(2,1)}, u32[]{:S(2)}, u32[]{:S(2)}) collective-permute-start(bf16[384,512]{1,0:T(8,128)(2,1)} %values.1.refs_1_), channel_id=1, source_target_pairs={{0,192},{4,196},{8,200},{12,204},{16,208},{20,212},{24,216},{28,22... | collective-permute-start | bytes 1179656 | tf_op jit(solution)/shard_map/keys_values/ppermute | solution.py:35
  63.5 29.9 %collective-permute-start.2 = (bf16[384,512]{1,0:T(8,128)(2,1)}, bf16[384,512]{1,0:T(8,128)(2,1)S(1)}, u32[]{:S(2)}, u32[]{:S(2)}) collective-permute-start(bf16[384,512]{1,0:T(8,128)(2,1)} %values.1.refs_1_), channel_id=1, source_target_pairs={{0,240},{4,244},{8,248},{12,252},{16,224},{20,228},{24,232},{28,23... | collective-permute-start | bytes 1179656 | tf_op jit(solution)/shard_map/keys_values/ppermute | solution.py:35
  75.8 20.3 %collective-permute-start.5 = (bf16[256,768]{1,0:T(8,128)(2,1)}, bf16[256,768]{1,0:T(8,128)(2,1)}, u32[]{:S(2)}, u32[]{:S(2)}) collective-permute-start(bf16[256,768]{1,0:T(8,128)(2,1)} %get-tuple-element.51), channel_id=1, source_target_pairs={{0,192},{4,196},{8,200},{12,204},{16,208},{20,212},{24,216},{28,22... | collective-permute-start | bytes 1179656 | tf_op jit(solution)/shard_map/attention/ppermute | solution.py:35
  79.9 16.2 %collective-permute-start.6 = (bf16[256,768]{1,0:T(8,128)(2,1)}, bf16[256,768]{1,0:T(8,128)(2,1)}, u32[]{:S(2)}, u32[]{:S(2)}) collective-permute-start(bf16[256,768]{1,0:T(8,128)(2,1)} %get-tuple-element.52), channel_id=1, source_target_pairs={{0,48},{4,52},{8,56},{12,60},{16,32},{20,36},{24,40},{28,44},{32,1... | collective-permute-start | bytes 1179656 | tf_op jit(solution)/shard_map/attention/ppermute | solution.py:35
  93.4 2.7 %copy-start.3 = (bf16[384,512]{1,0:T(8,128)(2,1)}, bf16[384,512]{1,0:T(8,128)(2,1)S(1)}, u32[]{:S(2)}) copy-start(bf16[384,512]{1,0:T(8,128)(2,1)S(1)} %collective-permute-done.2.refs_1_) | copy-start | bytes 1179652

commit v8 on v7

--- a/solution.py
+++ b/solution.py
@@ -257,25 +257,24 @@
     for base in (0, PACK):
         outs, lses = merge([lambda a, b, k=k: p_ref[k, base + a : base + b, :] for k in range(4)])
         packed = pack_lse(lses, 128)
-        for k in range(4):
-            for h in range(HALF):
-                o_ref[k, base + h * VEC : base + (h + 1) * VEC, :] = outs[h].astype(BF16)
-            o_ref[k, base + ROWS : base + PACK, :] = packed
+        for h in range(HALF):
+            o_ref[base + h * VEC : base + (h + 1) * VEC, :] = outs[h].astype(BF16)
+        o_ref[base + ROWS : base + PACK, :] = packed
 
 
 def merge_second(parts):
     return pl.pallas_call(
         merge_second_kernel,
-        out_shape=jax.ShapeDtypeStruct((4, 2 * PACK, 128), BF16),
-        cost_estimate=cost(8 * PACK * 128 * 2, 16 * PACK * 128 * 2),
+        out_shape=jax.ShapeDtypeStruct((2 * PACK, 128), BF16),
+        cost_estimate=cost(8 * PACK * 128 * 2, 10 * PACK * 128 * 2),
         name="merge_second",
     )(parts)
 
 
-def merge_last_kernel(p_ref, o_ref):
-    outs = []
+def merge_last_kernel(*refs):
+    outs, o_ref = [], refs[4]
     for base in (0, PACK):
-        outs += merge([lambda a, b, k=k: p_ref[k, base + a : base + b, :] for k in range(4)])[0]
+        outs += merge([lambda a, b, r=r: r[base + a : base + b, :] for r in refs[:4]])[0]
     o_ref[...] = sum(outs[1:], outs[0])
 
 
@@ -285,7 +284,7 @@
         out_shape=jax.ShapeDtypeStruct((VEC, 128), F32),
         cost_estimate=cost(8 * PACK * 128 * 2, 10 * PACK * 128),
         name="merge_last",
-    )(parts)
+    )(*parts)
 
 
 def decode_kernel(refresh_ref, me_ref, level_ref, v_ref, base_ref, up_ref, down_ref, w_ref, b_ref, o_ref, all_ref):
@@ -424,7 +423,9 @@
         values_far, far_a, far_b, state = together((values_far, far_a, far_b, state))
         state = attend(queries, values_far, state, (far_a, far_b))
         part = merge_second(exchange(state, ("yl", "xl")))
-        parts = exchange(part, "z")
+        parts = [part]
+        for k in range(1, 4):
+            parts.append(lax.ppermute(part, "z", [(i, (i + k) % 4) for i in range(4)]))
 
     with jax.named_scope("velocity"):
         term = merge_last(parts)

time: 158 us -> 154 us (0.975)
  blocking collectives: 47.8 us -> 31.3 us
  starting transfers between devices: 39.1 us -> 45.6 us
  waiting for transfers between devices: 16.9 us -> 23 us
    all_to_all x3 -> x2, blocking collectives: 42.2 us -> 25.5 us  [exchange(): return lax.all_to_all(value, axis, 0, 0)]
    ppermute x0 -> x3, starting transfers between devices: none -> 6.55 us  [on_device(): parts.append(lax.ppermute(part, 'z', [(i, (i + k) % 4) for i in range(4)]))]
    ppermute x0 -> x3, waiting for transfers between devices: none -> 6.12 us  [on_device(): parts.append(lax.ppermute(part, 'z', [(i, (i + k) % 4) for i in range(4)]))]
  transfers between devices with their start and end apart: 11 -> 14, of which waited for: 6 -> 9; matrix products, arithmetic and copies ran while one was open for 9% -> 9% of each run, Pallas kernels for 14% -> 14%
where the time goes in v8:
time: 154 us; the launch traced here: 152 us
  starting transfers between devices  45.6 us (30%)
  Pallas kernels  34.6 us (22%)
  blocking collectives  31.3 us (20%)
  waiting for transfers between devices  23 us (15%)
  local copies, waits for them, and re-layouts  7.41 us (5%)
  matrix products  5.76 us (4%)
  other arithmetic  3.52 us (2%)
    all_to_all x2, blocking collectives, exchange(): return lax.all_to_all(value, axis, 0, 0)  25.5 us
    pallas_call x4, Pallas kernels, attend(): pl.pallas_call(functools.partial(attend_kernel, first, last), out_shape=o...  20 us
    all_to_all x2, starting transfers between devices, exchange(): return lax.all_to_all(value, axis, 0, 0)  18.2 us
    ppermute x7, starting transfers between devices, mirror(): return lax.ppermute(value, PATCH, pairs)  14.7 us
    all_to_all x2, waiting for transfers between devices, exchange(): return lax.all_to_all(value, axis, 0, 0)  10.8 us
    ppermute x3, starting transfers between devices, on_device(): parts.append(lax.ppermute(part, 'z', [(i, (i + k) % 4) for i in range(4)]))  6.55 us
    ppermute x3, waiting for transfers between devices, on_device(): parts.append(lax.ppermute(part, 'z', [(i, (i + k) % 4) for i in range(4)]))  6.12 us
    all_gather x1, blocking collectives, on_device(): term = jnp.sum(lax.all_gather(term, HEAD), axis=0).astype(BF16)  5.81 us
  transfers between devices with their start and end apart: 14, of which 9 were waited for; matrix products, arithmetic and copies ran while one was open for 9% of the time, Pallas kernels for 14%

profile of v8, /device:TPU:32, one launch (start us, length us, event | category | flops | bytes accessed | tf_op | source)
XLA Modules:
  0.0 152.0 jit_solution(9250008366437605260)
XLA Ops:
  0.0 2.3 %slice_bitcast_fusion = bf16[64,8,768]{2,1,0:T(8,128)(2,1)} fusion(bf16[512,3,768]{2,0,1:T(8,128)(2,1)} %param.13), kind=kLoop, calls=%fused_computation.13 | loop fusion | bytes 1572864 | tf_op jit(solution)/shard_map/queries/reshape;queries/squeeze | solution.py:381
  2.3 13.9 %all-to-all-start = ((bf16[64,8,768]{2,1,0:T(8,128)(2,1)}), bf16[64,8,768]{2,1,0:T(8,128)(2,1)}, u32[]{:S(2)}, u32[]{:S(2)}) async-start(bf16[64,8,768]{2,1,0:T(8,128)(2,1)} %slice_bitcast_fusion), calls=%async_computation | async-start | bytes 1572864 | tf_op jit(solution)/shard_map/queries/all_to_all | solution.py:43
  20.5 4.9 %collective-permute-start = (f32[16,1024]{1,0:T(8,128)}, f32[16,1024]{1,0:T(8,128)}, u32[]{:S(2)}, u32[]{:S(2)}) collective-permute-start(f32[16,1024]{1,0:T(8,128)} %get-tuple-element.42), channel_id=1, source_target_pairs={{0,4},{4,8},{8,12},{12,16},{16,20},{20,24},{24,28},{28,32},{32,36}... | collective-permute-start | bytes 196616 | tf_op jit(solution)/shard_map/latent_base/ppermute | solution.py:398
  27.4 4.4 %fusion.8 = (bf16[512,1,768]{2,1,0:T(2,128)(2,1)S(1)}, bf16[512,1,768]{2,1,0:T(2,128)(2,1)S(1)}) fusion(bf16[512,2,768]{2,1,0:T(2,128)(2,1)} %param.14), kind=kLoop, calls=%fused_computation.17 | loop fusion | bytes 3145728 | tf_op jit(solution)/shard_map/keys_values/slice | solution.py:388
  35.4 8.0 %all-to-all-done.got_ref = bf16[64,8,768]{2,1,0:T(8,128)(2,1)} async-done(((bf16[64,8,768]{2,1,0:T(8,128)(2,1)}), bf16[64,8,768]{2,1,0:T(8,128)(2,1)}, u32[]{:S(2)}, u32[]{:S(2)}) %all-to-all-start) | async-done | bytes 786464 | tf_op jit(solution)/shard_map/queries/all_to_all | solution.py:43
  45.5 4.3 %all-to-all-start.1 = ((bf16[16,32,768]{2,1,0:T(8,128)(2,1)}), bf16[16,32,768]{2,1,0:T(8,128)(2,1)}, u32[]{:S(2)}, u32[]{:S(2)}) async-start(bf16[16,32,768]{2,1,0:T(8,128)(2,1)} %select.1), calls=%async_computation.1 | async-start | bytes 1572864 | tf_op jit(solution)/shard_map/queries/all_to_all | solution.py:43
  50.8 2.3 %collective-permute-start.4 = (bf16[512,768]{1,0:T(8,128)(2,1)}, bf16[512,768]{1,0:T(8,128)(2,1)}, u32[]{:S(2)}, u32[]{:S(2)}) collective-permute-start(bf16[512,768]{1,0:T(8,128)(2,1)} %get-tuple-element.76.refs_2_), channel_id=1, source_target_pairs={{0,192},{4,196},{8,200},{12,204},{16,208},{20,212},{24,216},{28,22... | collective-permute-start | bytes 2359304 | tf_op jit(solution)/shard_map/keys_values/ppermute | solution.py:35
  53.3 4.0 %fusion.1 = f32[128,768]{1,0:T(8,128)S(1)} fusion(bf16[768,3072]{1,0:T(8,128)(2,1)} %param.17, bf16[64,3072]{1,0:T(8,128)(2,1)S(1)} %get-tuple-element.80, bf16[64,3072]{1,0:T(8,128)(2,1)S(1)} %get-tuple-element.79), kind=kOutput, calls=%fused_computation.4 | convolution fusion | flops 605552640 | bytes 5898240 | tf_op jit(solution)/shard_map/keys_values/dot_general | solution.py:410
  58.0 2.3 %values.1.refs_1_ = bf16[384,512]{1,0:T(8,128)(2,1)} custom-call(bf16[512,768]{1,0:T(8,128)(2,1)} %get-tuple-element.75.v_ref, f32[64,768]{1,0:T(8,128)} %slice_add_fusion.w_ref), custom_call_target="tpu_custom_call" | custom-call | flops 100663296 | bytes 1572864 | tf_op jit(solution)/shard_map/keys_values/values/pallas_call | solution.py:88
  63.5 2.7 %collective-permute-start.2 = (bf16[384,512]{1,0:T(8,128)(2,1)}, bf16[384,512]{1,0:T(8,128)(2,1)S(1)}, u32[]{:S(2)}, u32[]{:S(2)}) collective-permute-start(bf16[384,512]{1,0:T(8,128)(2,1)} %values.1.refs_1_), channel_id=1, source_target_pairs={{0,240},{4,244},{8,248},{12,252},{16,224},{20,228},{24,232},{28,23... | collective-permute-start | bytes 1179656 | tf_op jit(solution)/shard_map/keys_values/ppermute | solution.py:35
  66.2 2.8 %all-to-all-done.1 = bf16[16,32,768]{2,1,0:T(8,128)(2,1)} async-done(((bf16[16,32,768]{2,1,0:T(8,128)(2,1)}), bf16[16,32,768]{2,1,0:T(8,128)(2,1)}, u32[]{:S(2)}, u32[]{:S(2)}) %all-to-all-start.1) | async-done | bytes 786464 | tf_op jit(solution)/shard_map/queries/all_to_all | solution.py:43
  69.0 4.8 %attend.4 = (f32[384,512]{1,0:T(8,128)}, f32[8,512]{1,0:T(8,128)}, f32[8,512]{1,0:T(8,128)}) custom-call(bf16[512,768]{1,0:T(8,128)(2,1)} %bitcast.4.refs_0_, bf16[384,512]{1,0:T(8,128)(2,1)} %values.1.refs_1_, bf16[512,768]{1,0:T(8,128)(2,1)} %get-tuple-element.76.refs_2_), custom_call_target="tpu_custom_call" | custom-call | flops 805306368 | bytes 3145728 | tf_op jit(solution)/shard_map/attention/attend/pallas_call | solution.py:227
  75.8 4.1 %collective-permute-start.5 = (bf16[256,768]{1,0:T(8,128)(2,1)}, bf16[256,768]{1,0:T(8,128)(2,1)}, u32[]{:S(2)}, u32[]{:S(2)}) collective-permute-start(bf16[256,768]{1,0:T(8,128)(2,1)} %get-tuple-element.51), channel_id=1, source_target_pairs={{0,192},{4,196},{8,200},{12,204},{16,208},{20,212},{24,216},{28,22... | collective-permute-start | bytes 1179656 | tf_op jit(solution)/shard_map/attention/ppermute | solution.py:35
  81.2 5.1 %attend.5 = (f32[384,512]{1,0:T(8,128)}, f32[8,512]{1,0:T(8,128)}, f32[8,512]{1,0:T(8,128)}) custom-call(bf16[512,768]{1,0:T(8,128)(2,1)} %bitcast.4.refs_0_, bf16[384,512]{1,0:T(8,128)(2,1)} %collective-permute-done.8.refs_1_, f32[384,512]{1,0:T(8,128)} %get-tuple-element.53.refs_2_, f32[8,512]{1,0:T(8,128)} %get-tuple-element.54.refs_3_, ...), custom_call_target="tpu_custom_call" | custom-call | flops 805306368 | bytes 3145728 | tf_op jit(solution)/shard_map/attention/attend/pallas_call | solution.py:227
  88.3 5.2 %attend.6 = (f32[384,512]{1,0:T(8,128)}, f32[8,512]{1,0:T(8,128)}, f32[8,512]{1,0:T(8,128)}) custom-call(bf16[512,768]{1,0:T(8,128)(2,1)} %bitcast.4.refs_0_, bf16[384,512]{1,0:T(8,128)(2,1)} %collective-permute-done.7.refs_1_, f32[384,512]{1,0:T(8,128)} %get-tuple-element.60.refs_2_, f32[8,512]{1,0:T(8,128)} %get-tuple-element.61.refs_3_, ...), custom_call_target="tpu_custom_call" | custom-call | flops 805306368 | bytes 3145728 | tf_op jit(solution)/shard_map/attention/attend/pallas_call | solution.py:227
  93.5 2.6 %collective-permute-done.5.refs_5_ = bf16[256,768]{1,0:T(8,128)(2,1)} collective-permute-done((bf16[256,768]{1,0:T(8,128)(2,1)}, bf16[256,768]{1,0:T(8,128)(2,1)}, u32[]{:S(2)}, u32[]{:S(2)}) %collective-permute-start.5) | collective-permute-done | bytes 393248 | tf_op jit(solution)/shard_map/attention/ppermute | solution.py:35
  96.1 4.9 %attend.7 = bf16[4,416,128]{2,1,0:T(8,128)(2,1)} custom-call(bf16[512,768]{1,0:T(8,128)(2,1)} %bitcast.4.refs_0_, bf16[384,512]{1,0:T(8,128)(2,1)} %copy-done.3, f32[384,512]{1,0:T(8,128)} %get-tuple-element.67.refs_2_, f32[8,512]{1,0:T(8,128)} %get-tuple-element.68.refs_3_, f32[8,512]{1,0:T(8,128)} %get-tuple-element.69.refs_4_, ...), custom_call_target="tpu_custom_call" | custom-call | flops 805306368 | bytes 3145728 | tf_op jit(solution)/shard_map/attention/attend/pallas_call | solution.py:227
  101.0 12.2 %all_to_all.20.p_ref = bf16[4,416,128]{2,1,0:T(8,128)(2,1)} all-to-all(bf16[4,416,128]{2,1,0:T(8,128)(2,1)} %attend.7), channel_id=1, replica_groups=mesh['yh'=2,'yl'=2,'xh'=2,'xl'=2,'z'=4,'w'=2,'c'=2] {'yl','xl'}, dimensions={0} | all-to-all | bytes 851968 | tf_op jit(solution)/shard_map/attention/all_to_all | solution.py:43
  115.0 3.6 %collective-permute-start.10 = (bf16[416,128]{1,0:T(8,128)(2,1)}, bf16[416,128]{1,0:T(8,128)(2,1)S(1)}, u32[]{:S(2)}, u32[]{:S(2)}) collective-permute-start(bf16[416,128]{1,0:T(8,128)(2,1)} %merge_second.1.refs_0_), channel_id=1, source_target_pairs={{0,8},{4,12},{8,0},{12,4},{1,9},{5,13},{9,1},{13,5},{2,10},{6,14},... | collective-permute-start | bytes 319496 | tf_op jit(solution)/shard_map/attention/ppermute | solution.py:428
  119.3 2.3 %collective-permute-start.9 = (bf16[416,128]{1,0:T(8,128)(2,1)}, bf16[416,128]{1,0:T(8,128)(2,1)S(1)}, u32[]{:S(2)}, u32[]{:S(2)}) collective-permute-start(bf16[416,128]{1,0:T(8,128)(2,1)} %merge_second.1.refs_0_), channel_id=1, source_target_pairs={{0,4},{4,8},{8,12},{12,0},{1,5},{5,9},{9,13},{13,1},{2,6},{6,10},{... | collective-permute-start | bytes 319496 | tf_op jit(solution)/shard_map/attention/ppermute | solution.py:428
  121.6 4.4 %collective-permute-done.10.refs_2_ = bf16[416,128]{1,0:T(8,128)(2,1)S(1)} collective-permute-done((bf16[416,128]{1,0:T(8,128)(2,1)}, bf16[416,128]{1,0:T(8,128)(2,1)S(1)}, u32[]{:S(2)}, u32[]{:S(2)}) %collective-permute-start.10) | collective-permute-done | bytes 106528 | tf_op jit(solution)/shard_map/attention/ppermute | solution.py:428
  130.1 5.8 %all-gather = f32[256,128]{1,0:T(8,128)S(1)} all-gather(f32[64,128]{1,0:T(8,128)} %merge_last.1), channel_id=2, replica_groups=mesh['yh'=2,'yl'=2,'xh'=2,'xl'=2,'z'=4,'w'=2,'c'=2] {'w','c'}, dimensions={0}, use_global_device_ids=true | all-gather | bytes 163840 | tf_op jit(solution)/shard_map/velocity/all_gather | solution.py:432
  136.0 13.3 %all_to_all.21.v_ref = bf16[16,64,128]{2,1,0:T(8,128)(2,1)} all-to-all(bf16[16,64,128]{2,1,0:T(8,128)(2,1)S(1)} %broadcast_in_dim.2), channel_id=1, replica_groups=mesh['yh'=2,'yl'=2,'xh'=2,'xl'=2,'z'=4,'w'=2,'c'=2] {'yh','yl','xh','xl'}, dimensions={0} | all-to-all | bytes 524288 | tf_op jit(solution)/shard_map/velocity/all_to_all | solution.py:43
  149.3 2.7 %decode.1 = bf16[2,128,1024]{2,1,0:T(8,128)(2,1)} custom-call(s32[4]{0:T(128)} %refresh_ref.5, s32[1]{0:T(128)} %bitcast.me_ref, f32[1]{0:T(128)S(6)} %copy.24.level_ref, bf16[16,64,128]{2,1,0:T(8,128)(2,1)} %all_to_all.21.v_ref, f32[32,1024]{1,0:T(8,128)} %get-tuple-element.72.base_ref, f32[16,1024]{1,0:T(8,128)} %collective-permute-done.up_ref, ...), custom_call_target="tpu_custom_call" | custom-call | flops 83886080 | bytes 2097152 | tf_op jit(solution)/shard_map/decode/decode/pallas_call | solution.py:350
  (48 shorter events, 28.3 us)
Async XLA Ops:
  0.0 16.9 %copy-start = (bf16[512,3072]{1,0:T(8,128)(2,1)S(1)}, bf16[512,3072]{1,0:T(8,128)(2,1)}, u32[]{:S(2)}) copy-start(bf16[512,3072]{1,0:T(8,128)(2,1)} %param.15) | copy-start | bytes 9437188
  0.0 16.9 %copy-start.2 = (bf16[3072,64]{0,1:T(8,128)(2,1)S(1)}, bf16[3072,64]{0,1:T(8,128)(2,1)}, u32[]{:S(2)}) copy-start(bf16[3072,64]{0,1:T(8,128)(2,1)} %param.18) | copy-start | bytes 1179652
  0.0 16.9 %copy-start.9 = (f32[64]{0:T(128)S(1)}, f32[64]{0:T(128)}, u32[]{:S(2)}) copy-start(f32[64]{0:T(128)} %param.19) | copy-start | bytes 772
  2.3 41.1 %all-to-all-start = ((bf16[64,8,768]{2,1,0:T(8,128)(2,1)}), bf16[64,8,768]{2,1,0:T(8,128)(2,1)}, u32[]{:S(2)}, u32[]{:S(2)}) async-start(bf16[64,8,768]{2,1,0:T(8,128)(2,1)} %slice_bitcast_fusion), calls=%async_computation | async-start | bytes 1572864 | tf_op jit(solution)/shard_map/queries/all_to_all | solution.py:43
  16.2 10.6 %copy-start.8 = (s32[4]{0:T(128)S(1)}, s32[4]{0:T(128)}, u32[]{:S(2)}) copy-start(s32[4]{0:T(128)} %refresh_ref.5) | copy-start | bytes 52
  20.5 14.5 %collective-permute-start = (f32[16,1024]{1,0:T(8,128)}, f32[16,1024]{1,0:T(8,128)}, u32[]{:S(2)}, u32[]{:S(2)}) collective-permute-start(f32[16,1024]{1,0:T(8,128)} %get-tuple-element.42), channel_id=1, source_target_pairs={{0,4},{4,8},{8,12},{12,16},{16,20},{20,24},{24,28},{28,32},{32,36}... | collective-permute-start | bytes 196616 | tf_op jit(solution)/shard_map/latent_base/ppermute | solution.py:398
  25.5 10.0 %collective-permute-start.1 = (f32[16,1024]{1,0:T(8,128)}, f32[16,1024]{1,0:T(8,128)}, u32[]{:S(2)}, u32[]{:S(2)}) collective-permute-start(f32[16,1024]{1,0:T(8,128)} %get-tuple-element.43), channel_id=1, source_target_pairs={{4,0},{8,4},{12,8},{16,12},{20,16},{24,20},{28,24},{32,28},{36,32}... | collective-permute-start | bytes 196616 | tf_op jit(solution)/shard_map/latent_base/ppermute | solution.py:399
  27.4 4.4 %copy-start.1 = (bf16[512,3,768]{2,0,1:T(8,128)(2,1)S(1)}, bf16[512,3,768]{2,0,1:T(8,128)(2,1)}, u32[]{:S(2)}) copy-start(bf16[512,3,768]{2,0,1:T(8,128)(2,1)} %param.13) | copy-start | bytes 7077892
  33.9 19.3 %copy-start.7 = (f32[3072]{0:T(1024)S(1)}, f32[3072]{0:T(1024)}, u32[]{:S(2)}) copy-start(f32[3072]{0:T(1024)} %param.20) | copy-start | bytes 36868
  45.5 23.5 %all-to-all-start.1 = ((bf16[16,32,768]{2,1,0:T(8,128)(2,1)}), bf16[16,32,768]{2,1,0:T(8,128)(2,1)}, u32[]{:S(2)}, u32[]{:S(2)}) async-start(bf16[16,32,768]{2,1,0:T(8,128)(2,1)} %select.1), calls=%async_computation.1 | async-start | bytes 1572864 | tf_op jit(solution)/shard_map/queries/all_to_all | solution.py:43
  49.8 23.9 %collective-permute-start.3 = (bf16[512,768]{1,0:T(8,128)(2,1)}, bf16[512,768]{1,0:T(8,128)(2,1)}, u32[]{:S(2)}, u32[]{:S(2)}) collective-permute-start(bf16[512,768]{1,0:T(8,128)(2,1)} %get-tuple-element.76.refs_2_), channel_id=1, source_target_pairs={{0,48},{4,52},{8,56},{12,60},{16,32},{20,36},{24,40},{28,44},{32,1... | collective-permute-start | bytes 2359304 | tf_op jit(solution)/shard_map/keys_values/ppermute | solution.py:35
  50.8 22.9 %collective-permute-start.4 = (bf16[512,768]{1,0:T(8,128)(2,1)}, bf16[512,768]{1,0:T(8,128)(2,1)}, u32[]{:S(2)}, u32[]{:S(2)}) collective-permute-start(bf16[512,768]{1,0:T(8,128)(2,1)} %get-tuple-element.76.refs_2_), channel_id=1, source_target_pairs={{0,192},{4,196},{8,200},{12,204},{16,208},{20,212},{24,216},{28,22... | collective-permute-start | bytes 2359304 | tf_op jit(solution)/shard_map/keys_values/ppermute | solution.py:35
  60.3 21.0 %collective-permute-start.8 = (bf16[384,512]{1,0:T(8,128)(2,1)}, bf16[384,512]{1,0:T(8,128)(2,1)}, u32[]{:S(2)}, u32[]{:S(2)}) collective-permute-start(bf16[384,512]{1,0:T(8,128)(2,1)} %values.1.refs_1_), channel_id=1, source_target_pairs={{0,48},{4,52},{8,56},{12,60},{16,32},{20,36},{24,40},{28,44},{32,1... | collective-permute-start | bytes 1179656 | tf_op jit(solution)/shard_map/keys_values/ppermute | solution.py:35
  61.8 26.5 %collective-permute-start.7 = (bf16[384,512]{1,0:T(8,128)(2,1)}, bf16[384,512]{1,0:T(8,128)(2,1)}, u32[]{:S(2)}, u32[]{:S(2)}) collective-permute-start(bf16[384,512]{1,0:T(8,128)(2,1)} %values.1.refs_1_), channel_id=1, source_target_pairs={{0,192},{4,196},{8,200},{12,204},{16,208},{20,212},{24,216},{28,22... | collective-permute-start | bytes 1179656 | tf_op jit(solution)/shard_map/keys_values/ppermute | solution.py:35
  63.5 30.0 %collective-permute-start.2 = (bf16[384,512]{1,0:T(8,128)(2,1)}, bf16[384,512]{1,0:T(8,128)(2,1)S(1)}, u32[]{:S(2)}, u32[]{:S(2)}) collective-permute-start(bf16[384,512]{1,0:T(8,128)(2,1)} %values.1.refs_1_), channel_id=1, source_target_pairs={{0,240},{4,244},{8,248},{12,252},{16,224},{20,228},{24,232},{28,23... | collective-permute-start | bytes 1179656 | tf_op jit(solution)/shard_map/keys_values/ppermute | solution.py:35
  75.8 20.3 %collective-permute-start.5 = (bf16[256,768]{1,0:T(8,128)(2,1)}, bf16[256,768]{1,0:T(8,128)(2,1)}, u32[]{:S(2)}, u32[]{:S(2)}) collective-permute-start(bf16[256,768]{1,0:T(8,128)(2,1)} %get-tuple-element.51), channel_id=1, source_target_pairs={{0,192},{4,196},{8,200},{12,204},{16,208},{20,212},{24,216},{28,22... | collective-permute-start | bytes 1179656 | tf_op jit(solution)/shard_map/attention/ppermute | solution.py:35
  79.9 16.2 %collective-permute-start.6 = (bf16[256,768]{1,0:T(8,128)(2,1)}, bf16[256,768]{1,0:T(8,128)(2,1)}, u32[]{:S(2)}, u32[]{:S(2)}) collective-permute-start(bf16[256,768]{1,0:T(8,128)(2,1)} %get-tuple-element.52), channel_id=1, source_target_pairs={{0,48},{4,52},{8,56},{12,60},{16,32},{20,36},{24,40},{28,44},{32,1... | collective-permute-start | bytes 1179656 | tf_op jit(solution)/shard_map/attention/ppermute | solution.py:35
  93.5 2.7 %copy-start.3 = (bf16[384,512]{1,0:T(8,128)(2,1)}, bf16[384,512]{1,0:T(8,128)(2,1)S(1)}, u32[]{:S(2)}) copy-start(bf16[384,512]{1,0:T(8,128)(2,1)S(1)} %collective-permute-done.2.refs_1_) | copy-start | bytes 1179652
  115.0 11.0 %collective-permute-start.10 = (bf16[416,128]{1,0:T(8,128)(2,1)}, bf16[416,128]{1,0:T(8,128)(2,1)S(1)}, u32[]{:S(2)}, u32[]{:S(2)}) collective-permute-start(bf16[416,128]{1,0:T(8,128)(2,1)} %merge_second.1.refs_0_), channel_id=1, source_target_pairs={{0,8},{4,12},{8,0},{12,4},{1,9},{5,13},{9,1},{13,5},{2,10},{6,14},... | collective-permute-start | bytes 319496 | tf_op jit(solution)/shard_map/attention/ppermute | solution.py:428
  118.7 8.0 %collective-permute-start.11 = (bf16[416,128]{1,0:T(8,128)(2,1)}, bf16[416,128]{1,0:T(8,128)(2,1)S(1)}, u32[]{:S(2)}, u32[]{:S(2)}) collective-permute-start(bf16[416,128]{1,0:T(8,128)(2,1)} %merge_second.1.refs_0_), channel_id=1, source_target_pairs={{0,12},{4,0},{8,4},{12,8},{1,13},{5,1},{9,5},{13,9},{2,14},{6,2},{... | collective-permute-start | bytes 319496 | tf_op jit(solution)/shard_map/attention/ppermute | solution.py:428
  119.3 8.4 %collective-permute-start.9 = (bf16[416,128]{1,0:T(8,128)(2,1)}, bf16[416,128]{1,0:T(8,128)(2,1)S(1)}, u32[]{:S(2)}, u32[]{:S(2)}) collective-permute-start(bf16[416,128]{1,0:T(8,128)(2,1)} %merge_second.1.refs_0_), channel_id=1, source_target_pairs={{0,4},{4,8},{8,12},{12,0},{1,5},{5,9},{9,13},{13,1},{2,6},{6,10},{... | collective-permute-start | bytes 319496 | tf_op jit(solution)/shard_map/attention/ppermute | solution.py:428
  126.0 1.7 %copy-start.4 = (bf16[416,128]{1,0:T(8,128)(2,1)}, bf16[416,128]{1,0:T(8,128)(2,1)S(1)}, u32[]{:S(2)}) copy-start(bf16[416,128]{1,0:T(8,128)(2,1)S(1)} %collective-permute-done.10.refs_2_) | copy-start | bytes 319492
  126.6 1.1 copy-start.5
  127.7 0.6 copy-start.6
